TPU v7x, 32 devices: a whole 2x2x4 slice. The times are simulated.
32 devices in a mesh: samp: 4 (over x, core), pos: 8 (over z, y).
Axes of the slice: x: 2, y: 2, z: 4, core: 2. Of those that a mesh axis runs over, the one named last changes fastest.
Arguments:
- dosages: bfloat16 [16384, 8192], P('samp', 'pos'), may hold values from -64 to 64
- phenotypes: bfloat16 [16384, 3072], P('samp', 'pos'), may hold values from -64 to 64
- window_low: int32 [3072], P('pos'), may hold values from 0 to 8191, as said below
- window_high: int32 [3072], P('pos'), may hold values from 0 to 8191, as said below
Outputs:
- statistics: float32 [8, 2048, 384], P('pos', 'samp')
Inputs may be any that keep to these rules, and one draw needn't show every extreme that they name: For peak p in block b = p // 384: b * 1024 - 512 <= window_low[p] <= window_high[p] <= b * 1024 + 1535. In every block but the first, one window starts exactly 512 variants before the block; in every block but the last, one ends exactly 512 variants after it. Same bounds as window_low; window_high[p] >= window_low[p].
All inputs are finite; a program needn't handle non-finite values.
Results may differ from a plain program's by a relative error of at most 0.0003.
Values may be sent and summed in bfloat16 or wider, within the bound.
No kernel may reach another device: no remote copies, remote signals or barrier semaphores. Data moves between devices by JAX's collectives and lax.ppermute only.
A program may use at most 64 MiB of HBM per device.

v0:
```python
import math

import jax
import jax.numpy as jnp
from jax import lax
from jax.sharding import PartitionSpec as P

HALO = 512


EPS = 1e-06


def padded(cells, sides, width):
    for axis, dim in sides:
        count = lax.axis_size(axis)
        ends = count - 1
        head = lax.slice_in_dim(cells, 0, width, axis=dim)
        tail = lax.slice_in_dim(cells, cells.shape[dim] - width, cells.shape[dim], axis=dim)
        cells = jnp.concatenate(
            [
                lax.ppermute(tail, axis, [(i, (i + 1) % count) for i in range(ends)]),
                cells,
                lax.ppermute(head, axis, [((i + 1) % count, i) for i in range(ends)]),
            ],
            axis=dim,
        )
    return cells


def from_behind(array, axis, by):
    devices = lax.axis_size(axis)
    pairs = [(i, i + by) for i in range(devices) if 0 <= i + by < devices]
    return lax.ppermute(array, axis, pairs)


def sum_squares(values):
    return jnp.sum(jnp.square(values.astype(jnp.float32)), axis=0)


def cross_rows(variant_panel, phenotypes):
    return lax.dot_general(
        variant_panel, phenotypes, (((0,), (0,)), ((), ())), preferred_element_type=jnp.float32
    )


def shards(dosages, phenotypes, window_low, window_high):
    sample_rows, block_width = dosages.shape
    peak_width = phenotypes.shape[1]
    span_width = block_width + 2 * HALO
    samp_count = lax.axis_size("samp")
    samp_index = lax.axis_index("samp")
    pos_index = lax.axis_index("pos")
    share_rows = span_width // samp_count
    own_first = samp_index * share_rows
    peak_squares = sum_squares(phenotypes)
    near_peaks = padded(phenotypes, (("pos", 1),), peak_width)
    own_tile = cross_rows(dosages, phenotypes)
    lower_edge = cross_rows(dosages[:, :HALO], near_peaks[:, :peak_width])
    upper_edge = cross_rows(dosages[:, block_width - HALO :], near_peaks[:, 2 * peak_width :])
    from_below = from_behind(upper_edge, "pos", 1)
    from_above = from_behind(lower_edge, "pos", -1)
    assembled = jnp.concatenate([from_below, own_tile, from_above], axis=0)
    owned_squares, peak_total = lax.psum((sum_squares(dosages), peak_squares), "samp")
    variant_total = padded(owned_squares, (("pos", 0),), HALO)
    cross_total = lax.psum(assembled, "samp")
    cross_share = lax.dynamic_slice_in_dim(cross_total, own_first, share_rows, 0)
    variant_share = lax.dynamic_slice_in_dim(variant_total, own_first, share_rows, 0)
    variant_index = (
        pos_index * block_width
        - HALO
        + own_first
        + jnp.arange(share_rows, dtype=jnp.int32)[:, None]
    )
    inside = (variant_index >= window_low[None, :]) & (variant_index <= window_high[None, :])
    factor = math.sqrt(float(sample_rows * samp_count - 2))
    scale_terms = (variant_share[:, None] + EPS) * (peak_total[None, :] + EPS)
    statistic = factor * cross_share / jnp.sqrt(scale_terms)
    return jnp.where(inside, statistic, jnp.zeros_like(statistic))[None]


def solution(mesh):
    placed = (P("samp", "pos"), P("samp", "pos"), P("pos"), P("pos"))
    return jax.shard_map(
        shards, mesh=mesh, in_specs=placed, out_specs=P("pos", "samp", None), check_vma=False
    )
```

profile of v0, /device:TPU:0, one launch (start us, length us, event | category | flops | bytes accessed | tf_op | source)
XLA Modules:
  0.0 270.4 jit_solution(13024341628665601439)
XLA Ops:
  6.5 0.0 all-reduce.3.cloned.1.call-start
  6.5 0.0 copy-start
  6.5 5.4 %collective-permute-start.2 = (bf16[4096,384]{1,0:T(8,128)(2,1)}, bf16[4096,384]{1,0:T(8,128)(2,1)S(1)}, u32[]{:S(2)}, u32[]{:S(2)}) collective-permute-start(bf16[4096,384]{1,0:T(8,128)(2,1)} %param.5), channel_id=1, source_target_pairs={{0,1},{1,2},{2,3},{3,4},{4,5},{5,6},{6,7},{8,9},{9,10},{10,11},{11... | collective-permute-start | bytes 9437192 | tf_op jit(solution)/shard_map/ppermute | solution.py:22
  11.9 1.3 collective-permute-start
  13.2 133.6 %collective-permute-done.2 = bf16[4096,384]{1,0:T(8,128)(2,1)S(1)} collective-permute-done((bf16[4096,384]{1,0:T(8,128)(2,1)}, bf16[4096,384]{1,0:T(8,128)(2,1)S(1)}, u32[]{:S(2)}, u32[]{:S(2)}) %collective-permute-start.2) | collective-permute-done | bytes 3145760 | tf_op jit(solution)/shard_map/ppermute | solution.py:22
  146.8 4.5 %fusion = f32[512,384]{1,0:T(8,128)S(1)} fusion(bf16[4096,384]{1,0:T(8,128)(2,1)S(1)} %collective-permute-done.2, bf16[4096,1024]{1,0:T(8,128)(2,1)} %param.4), kind=kOutput, calls=%fused_computation.2 | convolution fusion | flops 1610612736 | bytes 8126464 | tf_op jit(solution)/shard_map/dot_general | solution.py:42
  151.3 0.0 copy-start.1
  151.3 1.6 collective-permute-start.3
  152.9 0.0 collective-permute-done
  152.9 0.0 copy-done
  152.9 2.4 fusion.2
  155.3 5.0 %collective-permute-start.1 = (f32[512,384]{1,0:T(8,128)S(1)}, f32[512,384]{1,0:T(8,128)S(1)}, u32[]{:S(2)}, u32[]{:S(2)}) collective-permute-start(f32[512,384]{1,0:T(8,128)S(1)} %fusion.2), channel_id=1, source_target_pairs={{0,1},{1,2},{2,3},{3,4},{4,5},{5,6},{6,7},{8,9},{9,10},{10,11},{11... | collective-permute-start | bytes 2359304 | tf_op jit(solution)/shard_map/ppermute | solution.py:34
  160.3 0.0 copy-done.1
  160.3 4.5 %fusion.8 = f32[1024,384]{1,0:T(8,128)S(1)} fusion(bf16[4096,1024]{1,0:T(8,128)(2,1)S(1)} %copy-done, bf16[4096,384]{1,0:T(8,128)(2,1)S(1)} %copy-done.1), kind=kOutput, calls=%fused_computation.17 | convolution fusion | flops 3221225472 | bytes 13107200 | tf_op jit(solution)/shard_map/dot_general | solution.py:42
  164.8 7.7 %collective-permute-done.3 = f32[512,384]{1,0:T(8,128)S(1)} collective-permute-done((f32[512,384]{1,0:T(8,128)S(1)}, f32[512,384]{1,0:T(8,128)S(1)}, u32[]{:S(2)}, u32[]{:S(2)}) %collective-permute-start.3) | collective-permute-done | bytes 786464 | tf_op jit(solution)/shard_map/ppermute | solution.py:34
  172.6 17.0 %collective-permute-done.1 = f32[512,384]{1,0:T(8,128)S(1)} collective-permute-done((f32[512,384]{1,0:T(8,128)S(1)}, f32[512,384]{1,0:T(8,128)S(1)}, u32[]{:S(2)}, u32[]{:S(2)}) %collective-permute-start.1) | collective-permute-done | bytes 786464 | tf_op jit(solution)/shard_map/ppermute | solution.py:34
  189.6 1.9 pad_maximum_fusion
  191.4 0.0 all-reduce.3.cloned.1.call-update
  191.4 0.8 multiply_reduce_fusion.1
  192.2 0.0 copy-start.2
  192.2 0.0 copy-start.3
  192.2 5.1 %multiply_reduce_fusion = f32[1024]{0:T(1024)S(1)} fusion(bf16[4096,1024]{1,0:T(8,128)(2,1)} %param.4), kind=kLoop, calls=%fused_computation | loop fusion | flops 12581888 | bytes 8392704 | tf_op jit(solution)/shard_map/reduce_sum | solution.py:38
  197.3 7.8 %all-reduce = (f32[384]{0:T(512)S(1)}, f32[1024]{0:T(1024)S(1)}) all-reduce(f32[384]{0:T(512)S(1)} %multiply_reduce_fusion.1, f32[1024]{0:T(1024)S(1)} %multiply_reduce_fusion), channel_id=1, replica_groups=mesh['samp'=4,'pos'=8] {'samp'}, use_global_device_ids=true, to_apply=%region_4.0 | all-reduce | flops 1408 | bytes 11264 | tf_op jit(solution)/shard_map/psum | solution.py:64
  205.1 4.4 %collective-permute-start.4 = (f32[512]{0:T(512)S(1)}, f32[512]{0:T(512)S(1)}, u32[]{:S(2)}, u32[]{:S(2)}) collective-permute-start(f32[512]{0:T(512)S(1)} %get-tuple-element.8), channel_id=1, source_target_pairs={{0,1},{1,2},{2,3},{3,4},{4,5},{5,6},{6,7},{8,9},{9,10},{10,11},{11... | collective-permute-start | bytes 6152 | tf_op jit(solution)/shard_map/ppermute | solution.py:22
  209.5 1.3 collective-permute-start.5
  210.9 0.0 collective-permute-done.4
  210.9 4.1 %collective-permute-done.5 = f32[512]{0:T(512)S(1)} collective-permute-done((f32[512]{0:T(512)S(1)}, f32[512]{0:T(512)S(1)}, u32[]{:S(2)}, u32[]{:S(2)}) %collective-permute-start.5) | collective-permute-done | bytes 2080 | tf_op jit(solution)/shard_map/ppermute | solution.py:24
  215.0 0.1 fusion.6
  215.1 46.1 %all-reduce.3.cloned.1.call-done = f32[2048,384]{1,0:T(8,128)} async-done(((f32[2048,384]{1,0:T(8,128)}), f32[2048,384]{1,0:T(8,128)}) %all-reduce.3.cloned.1.call-update) | async-done | bytes 3145744 | tf_op jit(solution)/shard_map/psum | solution.py:66
  261.2 0.0 copy-done.2
  261.2 0.0 copy-done.3
  261.2 2.3 select_bitcast_fusion
  (3 shorter events, 0.0 us)
Async XLA Ops:
  6.5 254.7 %all-reduce.3.cloned.1.call-start = ((), (), s32[]{:S(2)}) async-start(), calls=%async_computation | async-start | bytes 6291456 | tf_op jit(solution)/shard_map/psum | solution.py:66
  6.5 146.4 %copy-start = (bf16[4096,1024]{1,0:T(8,128)(2,1)S(1)}, bf16[4096,1024]{1,0:T(8,128)(2,1)}, u32[]{:S(2)}) copy-start(bf16[4096,1024]{1,0:T(8,128)(2,1)} %param.4) | copy-start | bytes 25165828
  6.5 140.2 %collective-permute-start.2 = (bf16[4096,384]{1,0:T(8,128)(2,1)}, bf16[4096,384]{1,0:T(8,128)(2,1)S(1)}, u32[]{:S(2)}, u32[]{:S(2)}) collective-permute-start(bf16[4096,384]{1,0:T(8,128)(2,1)} %param.5), channel_id=1, source_target_pairs={{0,1},{1,2},{2,3},{3,4},{4,5},{5,6},{6,7},{8,9},{9,10},{10,11},{11... | collective-permute-start | bytes 9437192 | tf_op jit(solution)/shard_map/ppermute | solution.py:22
  11.9 141.0 %collective-permute-start = (bf16[4096,384]{1,0:T(8,128)(2,1)}, bf16[4096,384]{1,0:T(8,128)(2,1)S(1)}, u32[]{:S(2)}, u32[]{:S(2)}) collective-permute-start(bf16[4096,384]{1,0:T(8,128)(2,1)} %param.5), channel_id=1, source_target_pairs={{1,0},{2,1},{3,2},{4,3},{5,4},{6,5},{7,6},{9,8},{10,9},{11,10},{12... | collective-permute-start | bytes 9437192 | tf_op jit(solution)/shard_map/ppermute | solution.py:24
  151.3 9.0 %copy-start.1 = (bf16[4096,384]{1,0:T(8,128)(2,1)S(1)}, bf16[4096,384]{1,0:T(8,128)(2,1)}, u32[]{:S(2)}) copy-start(bf16[4096,384]{1,0:T(8,128)(2,1)} %param.5) | copy-start | bytes 9437188
  151.3 21.2 %collective-permute-start.3 = (f32[512,384]{1,0:T(8,128)S(1)}, f32[512,384]{1,0:T(8,128)S(1)}, u32[]{:S(2)}, u32[]{:S(2)}) collective-permute-start(f32[512,384]{1,0:T(8,128)S(1)} %fusion), channel_id=1, source_target_pairs={{1,0},{2,1},{3,2},{4,3},{5,4},{6,5},{7,6},{9,8},{10,9},{11,10},{12... | collective-permute-start | bytes 2359304 | tf_op jit(solution)/shard_map/ppermute | solution.py:34
  155.3 34.2 %collective-permute-start.1 = (f32[512,384]{1,0:T(8,128)S(1)}, f32[512,384]{1,0:T(8,128)S(1)}, u32[]{:S(2)}, u32[]{:S(2)}) collective-permute-start(f32[512,384]{1,0:T(8,128)S(1)} %fusion.2), channel_id=1, source_target_pairs={{0,1},{1,2},{2,3},{3,4},{4,5},{5,6},{6,7},{8,9},{9,10},{10,11},{11... | collective-permute-start | bytes 2359304 | tf_op jit(solution)/shard_map/ppermute | solution.py:34
  192.2 69.0 %copy-start.2 = (s32[384]{0:T(512)S(1)}, s32[384]{0:T(512)}, u32[]{:S(2)}) copy-start(s32[384]{0:T(512)} %param.7) | copy-start | bytes 4612
  192.2 69.0 %copy-start.3 = (s32[384]{0:T(512)S(1)}, s32[384]{0:T(512)}, u32[]{:S(2)}) copy-start(s32[384]{0:T(512)} %param.6) | copy-start | bytes 4612
  205.1 5.7 %collective-permute-start.4 = (f32[512]{0:T(512)S(1)}, f32[512]{0:T(512)S(1)}, u32[]{:S(2)}, u32[]{:S(2)}) collective-permute-start(f32[512]{0:T(512)S(1)} %get-tuple-element.8), channel_id=1, source_target_pairs={{0,1},{1,2},{2,3},{3,4},{4,5},{5,6},{6,7},{8,9},{9,10},{10,11},{11... | collective-permute-start | bytes 6152 | tf_op jit(solution)/shard_map/ppermute | solution.py:22
  209.5 5.5 %collective-permute-start.5 = (f32[512]{0:T(512)S(1)}, f32[512]{0:T(512)S(1)}, u32[]{:S(2)}, u32[]{:S(2)}) collective-permute-start(f32[512]{0:T(512)S(1)} %get-tuple-element.7), channel_id=1, source_target_pairs={{1,0},{2,1},{3,2},{4,3},{5,4},{6,5},{7,6},{9,8},{10,9},{11,10},{12... | collective-permute-start | bytes 6152 | tf_op jit(solution)/shard_map/ppermute | solution.py:24
Sparse Core Ops, SparseCore 0:
  191.6 69.6 all-reduce.2
where the time goes:
time: 271 us; the launch traced here: 270 us
  waiting for transfers between devices  209 us (77%)
  starting transfers between devices  18.8 us (7%)
  between operations  13.5 us (5%)
  matrix products  11.5 us (4%)
  other arithmetic  10.1 us (4%)
  blocking collectives  7.8 us (3%)
    ppermute x2, waiting for transfers between devices, padded(): lax.ppermute(tail, axis, [(i, (i + 1) % count) for i in range(ends)])  134 us
    psum x1, waiting for transfers between devices, shards(): cross_total = lax.psum(assembled, 'samp')  46.1 us
    ppermute x2, waiting for transfers between devices, from_behind(): return lax.ppermute(array, axis, pairs)  24.7 us
    dot_general x3, matrix products, cross_rows(): lax.dot_general(variant_panel, phenotypes, (((0,), (0,)), ((), ())), pref...  11.5 us
    ppermute x2, starting transfers between devices, padded(): lax.ppermute(tail, axis, [(i, (i + 1) % count) for i in range(ends)])  9.74 us
    psum x1, blocking collectives, shards(): lax.psum((sum_squares(dosages), peak_squares), 'samp')  7.8 us
    ppermute x2, starting transfers between devices, from_behind(): return lax.ppermute(array, axis, pairs)  6.51 us
    reduce_sum x2, other arithmetic, sum_squares(): return jnp.sum(jnp.square(values.astype(jnp.float32)), axis=0)  5.86 us
  transfers between devices with their start and end apart: 7, of which 5 were waited for; matrix products, arithmetic and copies ran while one was open for 6% of the time, Pallas kernels for 0%

commit v1 on v0

v1 whole, which is shorter than its diff:
```python
import functools
import math

import jax
import jax.numpy as jnp
from jax import lax
from jax.experimental import pallas as pl
from jax.experimental.pallas import tpu as pltpu
from jax.sharding import PartitionSpec as P


HALO = 512
EPS = 1e-06
LANES = 128
TAIL = 8
EARLY_SHARE = 8
EARLY_PARTS = 4
END_SHARE = 4
OWN_STEPS = 4
OWN_CALLS = 2
OWN_VMEM = 20 * 1024 * 1024


def cross_rows(variant_panel, phenotypes):
    return lax.dot_general(
        variant_panel, phenotypes, (((0,), (0,)), ((), ())), preferred_element_type=jnp.float32
    )


def added(total, part):
    return part if total is None else lax.optimization_barrier(total) + part


def folded_squares(block):
    wide = block.astype(jnp.float32)
    return jnp.sum((wide * wide).reshape(-1, 8, wide.shape[1]), axis=0)


def own_kernel(has_base, dosages, phenotypes, *refs):
    cross, variant_sq, peak_sq = refs[-3:]

    @pl.when(pl.program_id(0) == 0)
    def _():
        for index, ref in enumerate(refs[-3:]):
            ref[...] = refs[index][...] if has_base else jnp.zeros_like(ref)

    cross[...] += cross_rows(dosages[...], phenotypes[...])
    variant_sq[...] += folded_squares(dosages[...])
    peak_sq[...] += folded_squares(phenotypes[...])


def own_block(dosages, phenotypes, rows, first, count, base):
    block_width = dosages.shape[1]
    peak_width = phenotypes.shape[1]
    shapes = [(block_width, peak_width), (8, block_width), (8, peak_width)]
    sums = [pl.BlockSpec(shape, lambda i: (0, 0)) for shape in shapes]
    return pl.pallas_call(
        functools.partial(own_kernel, base is not None),
        grid=(count,),
        in_specs=[
            pl.BlockSpec((rows, block_width), lambda i: (first + i, 0)),
            pl.BlockSpec((rows, peak_width), lambda i: (first + i, 0)),
            *(sums if base else []),
        ],
        out_specs=sums,
        out_shape=[jax.ShapeDtypeStruct(shape, jnp.float32) for shape in shapes],
        compiler_params=pltpu.CompilerParams(vmem_limit_bytes=OWN_VMEM),
        name="own_block",
    )(dosages, phenotypes, *(base or ()))


def statistics_share(dosages, phenotypes, window_low, window_high):
    sample_rows, block_width = dosages.shape
    peak_width = phenotypes.shape[1]
    span_width = block_width + 2 * HALO
    samp_count = lax.axis_size("samp")
    pos_count = lax.axis_size("pos")
    samp_index = lax.axis_index("samp")
    pos_index = lax.axis_index("pos")
    share_rows = span_width // samp_count
    halo_shares = HALO // share_rows
    half = samp_count // 2
    even = pos_index % 2 == 0
    all_samp = range(samp_count)
    all_pos = range(pos_count)
    split = peak_width - LANES
    early = sample_rows * EARLY_SHARE // 16
    end = sample_rows - sample_rows * END_SHARE // 16
    step = early // EARLY_PARTS

    def hop(array, pairs):
        flat = [(a * pos_count + b, c * pos_count + d) for a, b, c, d in pairs]
        return lax.ppermute(array, ("samp", "pos"), flat)

    def parity(x, y):
        return jnp.where(even, x, y)

    swap = [(b, b ^ 1) for b in all_pos]
    onward = [(b, b + 2) for b in range(0, pos_count - 2, 2)] + [(b, b - 2) for b in range(3, pos_count, 2)]
    back = [(d, s) for s, d in onward]

    near_start = jnp.where(even, block_width - HALO, 0)
    far_start = jnp.where(even, 0, block_width - HALO)

    def half_rows(start, low, high):
        return lax.dynamic_slice(dosages, (low, start), (high - low, HALO))

    windows = [(i * step, (i + 1) * step, 0, peak_width) for i in range(EARLY_PARTS)]
    windows += [(early, sample_rows, 0, split), (early, end, split, peak_width), (end, sample_rows, split, peak_width)]
    held, source = [], phenotypes
    for i, (a, b, c, d) in enumerate(windows):
        piece = lax.slice(source, (a, c), (b, d))
        held.append(lax.ppermute(piece, "pos", swap))
        if i == 0:
            source = lax.optimization_barrier(phenotypes)
    first, left, right, tip = held[:EARLY_PARTS], *held[EARLY_PARTS:]
    passed = [lax.ppermute(x, "pos", onward) for x in first]

    far_late = lax.optimization_barrier(half_rows(far_start, early, sample_rows))
    far_in = lax.ppermute(far_late, "pos", back)

    inner_shares = list(range(halo_shares, samp_count - halo_shares))
    outer_shares = [*range(halo_shares), *range(samp_count - halo_shares, samp_count)]
    outer = (samp_index < halo_shares) | (samp_index >= samp_count - halo_shares)
    bits = [1 << i for i in range(samp_count.bit_length() - 2)]

    def rows_of(vector, width):
        block = vector.reshape(-1, width)
        return jnp.pad(block, ((0, TAIL - block.shape[0]), (0, 0)))

    def pieces_of(first, second, owners, tail):
        out = []
        for k, t in enumerate(owners):
            rows, squares = first if k < halo_shares else second
            low = (k % halo_shares) * share_rows
            high = low + share_rows
            piece = rows[low:high]
            out.append((t, jnp.concatenate([piece, tail(squares[low:high])]) if tail else piece))
        return out

    def exchange(tagged, bit):
        mine = (samp_index // bit) % 2 == 1
        zeros = [x for x in tagged if (x[0] // bit) % 2 == 0]
        ones = [x for x in tagged if (x[0] // bit) % 2 == 1]
        kept = []
        for (tag, z), (_, o) in zip(zeros, ones):
            keep, send = jnp.where(mine, o, z), jnp.where(mine, z, o)
            kept.append((tag, keep + lax.ppermute(send, "samp", [(s, s ^ bit) for s in all_samp])))
        return kept

    own = None
    for i in range(OWN_CALLS):
        count = OWN_STEPS // OWN_CALLS
        own = own_block(dosages, phenotypes, sample_rows // OWN_STEPS, i * count, count, own)
    own, own_sq, peak_sq = own
    own_sq, peak_sq = jnp.sum(own_sq, axis=0), jnp.sum(peak_sq, axis=0)
    low_sq, high_sq = own_sq[:HALO], own_sq[block_width - HALO :]
    near_sq, far_sq = parity(high_sq, low_sq), parity(low_sq, high_sq)

    def own_tail(sums):
        return jnp.concatenate([rows_of(sums, split), rows_of(peak_sq, LANES)], axis=1)

    own = pieces_of((own[:HALO], low_sq), (own[block_width - HALO :], high_sq), inner_shares, own_tail)
    for bit in bits:
        own = exchange(own, bit)
    ((_, own),) = own
    own_total = own + lax.ppermute(own, "samp", [(t ^ half, t) for t in inner_shares])
    peak_total = own[share_rows:, split:]
    peak_total = peak_total + lax.ppermute(peak_total, "samp", [(s, s ^ half) for s in all_samp])
    peak_total = peak_total[: peak_width // LANES].reshape(peak_width)

    near_early = cross_rows(half_rows(near_start, 0, early), jnp.concatenate(first))
    far_early = cross_rows(half_rows(far_start, 0, early - step), jnp.concatenate(passed[:-1]))
    far_early = added(far_early, cross_rows(half_rows(far_start, early - step, early), passed[-1]))

    def acc_tail(sums):
        return jnp.pad(rows_of(sums, split), ((0, 0), (0, LANES)))

    acc = pieces_of(
        (parity(0.0, far_early), parity(0.0, far_sq)),
        (parity(far_early, 0.0), parity(far_sq, 0.0)),
        outer_shares,
        acc_tail,
    )
    acc = exchange(acc, 1)
    acc_pairs = [(s, b, s, d) for s in all_samp for b, d in back if halo_shares > 1 or (s + b) % 2 == 1]
    acc = [hop(x, acc_pairs) for _, x in acc]

    straight = [(t, b, t, b ^ 1) for t in outer_shares for b in all_pos]
    across = [(t ^ half, b, t, b ^ 1) for t in outer_shares for b in all_pos]

    def reduced(pieces, low, high):
        pieces = exchange(pieces, 1)
        pieces = [(t, x + y[: x.shape[0], low:high]) for (t, x), y in zip(pieces, acc)]
        for bit in bits[1:]:
            pieces = exchange(pieces, bit)
        ((_, only),) = pieces
        return only

    near_edge = near_early[:, :split] + cross_rows(half_rows(near_start, early, sample_rows), left)
    far_edge = cross_rows(far_in, left)
    up, down = parity(near_edge, far_edge), parity(far_edge, near_edge)
    none = jnp.zeros_like(near_sq)
    pieces = pieces_of(
        (up, parity(near_sq, none)),
        (down, parity(none, near_sq)),
        outer_shares,
        lambda sums: rows_of(sums, split),
    )
    edge = reduced(pieces, 0, split)
    left_total = hop(edge, straight) + hop(edge, across)

    near_edge = near_early[:, split:] + cross_rows(half_rows(near_start, early, end), right)
    far_edge = cross_rows(far_in[: end - early], right)
    near_edge = added(near_edge, cross_rows(half_rows(near_start, end, sample_rows), tip))
    far_edge = added(far_edge, cross_rows(far_in[end - early :], tip))
    up, down = parity(near_edge, far_edge), parity(far_edge, near_edge)
    pieces = pieces_of((up, near_sq), (down, near_sq), outer_shares, None)
    edge = reduced(pieces, split, peak_width)
    right_total = hop(edge, straight) + hop(edge, across)

    left_share = jnp.where(outer, left_total, own_total[:, :split])
    right_share = jnp.where(outer, right_total, own_total[:share_rows, split:])
    variant_share = left_share[share_rows : share_rows + share_rows // split].reshape(share_rows)
    cross_share = jnp.concatenate([left_share[:share_rows], right_share], axis=1)

    variant_index = (
        pos_index * block_width
        - HALO
        + samp_index * share_rows
        + jnp.arange(share_rows, dtype=jnp.int32)[:, None]
    )
    inside = (variant_index >= window_low[None, :]) & (variant_index <= window_high[None, :])
    factor = math.sqrt(float(sample_rows * samp_count - 2))
    scale_terms = (variant_share[:, None] + EPS) * (peak_total[None, :] + EPS)
    statistic = factor * cross_share / jnp.sqrt(scale_terms)
    return jnp.where(inside, statistic, jnp.zeros_like(statistic))[None]


def solution(mesh):
    placed = (P("samp", "pos"), P("samp", "pos"), P("pos"), P("pos"))
    return jax.shard_map(
        statistics_share, mesh=mesh, in_specs=placed, out_specs=P("pos", "samp", None), check_vma=False
    )
```

time: 271 us -> 144 us (0.53)
  waiting for transfers between devices: 209 us -> 64.3 us
  starting transfers between devices: 18.8 us -> 38.6 us
  local copies, waits for them, and re-layouts: 0.02 us -> 16.8 us
  between operations: 13.5 us -> 0.45 us
  blocking collectives: 7.8 us -> 0 us
  Pallas kernels: 0 us -> 5.89 us
  other arithmetic: 10.1 us -> 5.73 us
    ppermute x6 -> x23, waiting for transfers between devices: 162 us -> 64.3 us  [the longest x1 16.7 us: statistics_share(): far_in = lax.ppermute(far_late, 'pos', back)]
    psum x1 -> x0, waiting for transfers between devices: 46.1 us -> none  [shards(): cross_total = lax.psum(assembled, 'samp')]
    ppermute x6 -> x23, starting transfers between devices: 18.8 us -> 38.6 us  [the longest x4 13.9 us: statistics_share(): passed = [lax.ppermute(x, 'pos', onward) for x in first]]
    slice x1 -> x9, local copies, waits for them, and re-layouts: 0.01 us -> 8.89 us  [the longest x4 6.16 us: statistics_share(): piece = lax.slice(source, (a, c), (b, d))]
    psum x1 -> x0, blocking collectives: 7.8 us -> none  [shards(): lax.psum((sum_squares(dosages), peak_squares), 'samp')]
    pallas_call x0 -> x2, Pallas kernels: none -> 5.89 us  [own_block(): pl.pallas_call(functools.partial(own_kernel, base is not None), grid=(cou...]
    reduce_sum x2, other arithmetic: 5.86 us -> 0.03 us  [statistics_share(): own_sq, peak_sq = (jnp.sum(own_sq, axis=0), jnp.sum(peak_sq, axis=0))]
    unnamed x8 -> x23, local copies, waits for them, and re-layouts: 0.02 us -> 4.75 us
  transfers between devices with their start and end apart: 7 -> 23, of which waited for: 5 -> 8; matrix products, arithmetic and copies ran while one was open for 6% -> 18% of each run, Pallas kernels for 0% -> 4%
where the time goes in v1:
time: 144 us; the launch traced here: 143 us
  waiting for transfers between devices  64.3 us (45%)
  starting transfers between devices  38.6 us (27%)
  local copies, waits for them, and re-layouts  16.8 us (12%)
  matrix products  11.7 us (8%)
  Pallas kernels  5.89 us (4%)
  other arithmetic  5.73 us (4%)
    ppermute x1, waiting for transfers between devices, statistics_share(): far_in = lax.ppermute(far_late, 'pos', back)  16.7 us
    ppermute x7, waiting for transfers between devices, statistics_share(): held.append(lax.ppermute(piece, 'pos', swap))  16 us
    ppermute x4, waiting for transfers between devices, statistics_share(): passed = [lax.ppermute(x, 'pos', onward) for x in first]  15.5 us
    ppermute x4, starting transfers between devices, statistics_share(): passed = [lax.ppermute(x, 'pos', onward) for x in first]  13.9 us
    dot_general x9, matrix products, cross_rows(): lax.dot_general(variant_panel, phenotypes, (((0,), (0,)), ((), ())), pref...  11.7 us
    ppermute x5, waiting for transfers between devices, hop(): return lax.ppermute(array, ('samp', 'pos'), flat)  10.5 us
    ppermute x7, starting transfers between devices, statistics_share(): held.append(lax.ppermute(piece, 'pos', swap))  10 us
    ppermute x5, starting transfers between devices, hop(): return lax.ppermute(array, ('samp', 'pos'), flat)  9.13 us
  transfers between devices with their start and end apart: 23, of which 8 were waited for; matrix products, arithmetic and copies ran while one was open for 18% of the time, Pallas kernels for 4%

profile of v1, /device:TPU:0, one launch (start us, length us, event | category | flops | bytes accessed | tf_op | source)
XLA Modules:
  0.0 143.4 jit_solution(16002603737560749478)
XLA Ops:
  0.0 2.4 %fusion.49 = (bf16[512,384]{1,0:T(8,128)(2,1)}, bf16[512,384]{1,0:T(8,128)(2,1)}, bf16[512,384]{1,0:T(8,128)(2,1)}) fusion(bf16[4096,384]{1,0:T(8,128)(2,1)} %phenotypes.3), kind=kLoop, calls=%fused_computation.86 | loop fusion | bytes 2359296 | tf_op jit(solution)/shard_map/slice | solution.py:112
  2.4 3.0 %collective-permute-start.4 = (bf16[512,384]{1,0:T(8,128)(2,1)}, bf16[512,384]{1,0:T(8,128)(2,1)}, u32[]{:S(2)}, u32[]{:S(2)}) collective-permute-start(bf16[512,384]{1,0:T(8,128)(2,1)} %get-tuple-element.23), channel_id=1, source_target_pairs={{0,1},{1,0},{2,3},{3,2},{4,5},{5,4},{6,7},{7,6},{8,9},{9,8},{10,11... | collective-permute-start | bytes 1179656 | tf_op jit(solution)/shard_map/ppermute | solution.py:113
  5.5 1.8 %slice.106 = bf16[512,384]{1,0:T(8,128)(2,1)} slice(bf16[4096,384]{1,0:T(8,128)(2,1)} %phenotypes.3), slice={[0:512], [0:384]} | slice | bytes 786432 | tf_op jit(solution)/shard_map/slice | solution.py:112
  7.3 2.0 %collective-permute-start.2 = (bf16[512,384]{1,0:T(8,128)(2,1)}, bf16[512,384]{1,0:T(8,128)(2,1)}, u32[]{:S(2)}, u32[]{:S(2)}) collective-permute-start(bf16[512,384]{1,0:T(8,128)(2,1)} %slice.106), channel_id=1, source_target_pairs={{0,1},{1,0},{2,3},{3,2},{4,5},{5,4},{6,7},{7,6},{8,9},{9,8},{10,11... | collective-permute-start | bytes 1179656 | tf_op jit(solution)/shard_map/ppermute | solution.py:113
  9.3 3.4 %copy-done = bf16[4096,1024]{1,0:T(8,128)(2,1)S(1)} copy-done((bf16[4096,1024]{1,0:T(8,128)(2,1)S(1)}, bf16[4096,1024]{1,0:T(8,128)(2,1)}, u32[]{:S(2)}) %copy-start) | copy-done | bytes 8388632
  12.6 2.9 %own_block.2 = (f32[1024,384]{1,0:T(8,128)S(1)}, f32[8,1024]{1,0:T(8,128)S(1)}, f32[8,384]{1,0:T(8,128)S(1)}) custom-call(bf16[4096,1024]{1,0:T(8,128)(2,1)S(1)} %copy-done, bf16[4096,384]{1,0:T(8,128)(2,1)S(1)} %copy-done.1), custom_call_target="tpu_custom_call" | custom-call | tf_op jit(solution)/shard_map/own_block/pallas_call | solution.py:57
  15.5 3.0 %own_block.3 = (f32[1024,384]{1,0:T(8,128)S(1)}, f32[8,1024]{1,0:T(8,128)S(1)}, f32[8,384]{1,0:T(8,128)S(1)}) custom-call(bf16[4096,1024]{1,0:T(8,128)(2,1)S(1)} %copy-done, bf16[4096,384]{1,0:T(8,128)(2,1)S(1)} %copy-done.1, f32[1024,384]{1,0:T(8,128)S(1)} %get-tuple-element.11.refs_0_, f32[8,1024]{1,0:T(8,128)S(1)} %get-tuple-element.12.refs_1_, ...), custom_call_target="tpu_custom_call" | custom-call | tf_op jit(solution)/shard_map/own_block/pallas_call | solution.py:57
  19.8 2.7 %fusion.50 = (f32[512,384]{1,0:T(8,128)}, f32[512,384]{1,0:T(8,128)}) fusion(f32[1024,384]{1,0:T(8,128)} %copy-done.2), kind=kLoop, calls=%fused_computation.87 | loop fusion | bytes 3145728 | tf_op jit(solution)/shard_map/slice | solution.py:163
  22.5 2.3 %broadcast_select_fusion = f32[520,384]{1,0:T(8,128)} fusion(pred[]{:T(512)S(6)} %eq.15, f32[3,128]{1,0:T(4,128)S(1)} %bitcast.20, f32[2,256]{1,0:T(2,128)S(1)} %slice.114, f32[512,384]{1,0:T(8,128)} %get-tuple-element.30, f32[2,256]{1,0:T(2,128)S(1)} %slice.112, f32[512,384]{1,0:T(8,128)} %get-tuple-element.29), kind=kLoop, calls=%fused_computation.52 | loop fusion | flops 3194880 | bytes 2377217 | tf_op jit(solution)/shard_map/jit(_where)/select_n | solution.py:147
  24.9 3.1 %constant_dynamic-slice_fusion = bf16[2048,512]{1,0:T(8,128)(2,1)} fusion(bf16[4096,1024]{1,0:T(8,128)(2,1)} %dosages.3, s32[]{:T(128)S(6)} %select_n.184), kind=kLoop, calls=%fused_computation.77 | loop fusion | bytes 4194308 | tf_op jit(solution)/shard_map/dynamic_slice | solution.py:106
  28.0 4.8 %collective-permute-start.9 = (bf16[512,384]{1,0:T(8,128)(2,1)}, bf16[512,384]{1,0:T(8,128)(2,1)}, u32[]{:S(2)}, u32[]{:S(2)}) collective-permute-start(bf16[512,384]{1,0:T(8,128)(2,1)} %collective-permute-done.4), channel_id=1, source_target_pairs={{0,2},{2,4},{4,6},{3,1},{5,3},{7,5},{8,10},{10,12},{12,14},{11,9},... | collective-permute-start | bytes 1179656 | tf_op jit(solution)/shard_map/ppermute | solution.py:117
  32.7 3.5 %collective-permute-start.8 = (bf16[512,384]{1,0:T(8,128)(2,1)}, bf16[512,384]{1,0:T(8,128)(2,1)}, u32[]{:S(2)}, u32[]{:S(2)}) collective-permute-start(bf16[512,384]{1,0:T(8,128)(2,1)} %collective-permute-done.3), channel_id=1, source_target_pairs={{0,2},{2,4},{4,6},{3,1},{5,3},{7,5},{8,10},{10,12},{12,14},{11,9},... | collective-permute-start | bytes 1179656 | tf_op jit(solution)/shard_map/ppermute | solution.py:117
  36.2 3.5 %collective-permute-start.7 = (bf16[512,384]{1,0:T(8,128)(2,1)}, bf16[512,384]{1,0:T(8,128)(2,1)}, u32[]{:S(2)}, u32[]{:S(2)}) collective-permute-start(bf16[512,384]{1,0:T(8,128)(2,1)} %collective-permute-done.2), channel_id=1, source_target_pairs={{0,2},{2,4},{4,6},{3,1},{5,3},{7,5},{8,10},{10,12},{12,14},{11,9},... | collective-permute-start | bytes 1179656 | tf_op jit(solution)/shard_map/ppermute | solution.py:117
  41.6 2.2 %collective-permute-start.10 = (bf16[512,384]{1,0:T(8,128)(2,1)}, bf16[512,384]{1,0:T(8,128)(2,1)S(1)}, u32[]{:S(2)}, u32[]{:S(2)}) collective-permute-start(bf16[512,384]{1,0:T(8,128)(2,1)} %collective-permute-done.5), channel_id=1, source_target_pairs={{0,2},{2,4},{4,6},{3,1},{5,3},{7,5},{8,10},{10,12},{12,14},{11,9},... | collective-permute-start | bytes 1179656 | tf_op jit(solution)/shard_map/ppermute | solution.py:117
  44.2 6.0 %collective-permute-done.8 = bf16[512,384]{1,0:T(8,128)(2,1)} collective-permute-done((bf16[512,384]{1,0:T(8,128)(2,1)}, bf16[512,384]{1,0:T(8,128)(2,1)}, u32[]{:S(2)}, u32[]{:S(2)}) %collective-permute-start.8) | collective-permute-done | bytes 393248 | tf_op jit(solution)/shard_map/ppermute | solution.py:117
  50.2 2.4 %collective-permute-start.18 = (bf16[1024,128]{1,0:T(8,128)(2,1)}, bf16[1024,128]{1,0:T(8,128)(2,1)S(1)}, u32[]{:S(2)}, u32[]{:S(2)}) collective-permute-start(bf16[1024,128]{1,0:T(8,128)(2,1)} %get-tuple-element.20), channel_id=1, source_target_pairs={{0,1},{1,0},{2,3},{3,2},{4,5},{5,4},{6,7},{7,6},{8,9},{9,8},{10,11... | collective-permute-start | bytes 786440 | tf_op jit(solution)/shard_map/ppermute | solution.py:113
  52.6 6.0 %collective-permute-done.7 = bf16[512,384]{1,0:T(8,128)(2,1)} collective-permute-done((bf16[512,384]{1,0:T(8,128)(2,1)}, bf16[512,384]{1,0:T(8,128)(2,1)}, u32[]{:S(2)}, u32[]{:S(2)}) %collective-permute-start.7) | collective-permute-done | bytes 393248 | tf_op jit(solution)/shard_map/ppermute | solution.py:117
  59.9 2.9 %fusion.11 = f32[512,384]{1,0:T(8,128)S(1)} fusion(bf16[4096,1024]{1,0:T(8,128)(2,1)} %dosages.3, s32[]{:T(128)S(6)} %select_n.184, bf16[512,384]{1,0:T(8,128)(2,1)} %collective-permute-done.9, bf16[512,384]{1,0:T(8,128)(2,1)} %collective-permute-done.8, bf16[512,384]{1,0:T(8,128)(2,1)} %collective-permute-done.7), kind=kOutput, calls=%fused_computation.11 | convolution fusion | flops 607518720 | bytes 3538948 | tf_op jit(solution)/shard_map/dot_general | solution.py:25
  62.8 3.5 %collective-permute-done.10 = bf16[512,384]{1,0:T(8,128)(2,1)S(1)} collective-permute-done((bf16[512,384]{1,0:T(8,128)(2,1)}, bf16[512,384]{1,0:T(8,128)(2,1)S(1)}, u32[]{:S(2)}, u32[]{:S(2)}) %collective-permute-start.10) | collective-permute-done | bytes 393248 | tf_op jit(solution)/shard_map/ppermute | solution.py:117
  66.3 2.3 %collective-permute-start.1 = (bf16[2048,256]{1,0:T(8,128)(2,1)S(1)}, bf16[2048,256]{1,0:T(8,128)(2,1)S(1)}, u32[]{:S(2)}, u32[]{:S(2)}) collective-permute-start(bf16[2048,256]{1,0:T(8,128)(2,1)S(1)} %copy-done.5), channel_id=1, source_target_pairs={{0,1},{1,0},{2,3},{3,2},{4,5},{5,4},{6,7},{7,6},{8,9},{9,8},{10,11... | collective-permute-start | bytes 3145736 | tf_op jit(solution)/shard_map/ppermute | solution.py:113
  68.6 1.5 %fusion.33 = f32[512,384]{1,0:T(8,128)S(1)} fusion(bf16[512,384]{1,0:T(8,128)(2,1)S(1)} %collective-permute-done.10, bf16[4096,1024]{1,0:T(8,128)(2,1)} %dosages.3, s32[]{:T(128)S(6)} %select_n.184), kind=kOutput, calls=%fused_computation.50 | convolution fusion | flops 201326592 | bytes 1703940 | tf_op jit(solution)/shard_map/dot_general | solution.py:25
  70.4 1.7 %fusion.22 = f32[512,128]{1,0:T(8,128)S(1)} fusion(bf16[1024,128]{1,0:T(8,128)(2,1)S(1)} %collective-permute-done.18, bf16[4096,1024]{1,0:T(8,128)(2,1)} %dosages.3, s32[]{:T(128)S(6)} %select_n.185), kind=kOutput, calls=%fused_computation.22 | convolution fusion | flops 134217728 | bytes 1572868 | tf_op jit(solution)/shard_map/dot_general | solution.py:25
  72.1 2.6 %fusion.2 = f32[512,384]{1,0:T(8,128)S(1)} fusion(bf16[4096,1024]{1,0:T(8,128)(2,1)S(1)} %bitcast.19, s32[]{:T(128)S(6)} %select_n.185, bf16[512,384]{1,0:T(8,128)(2,1)} %collective-permute-done.5, bf16[512,384]{1,0:T(8,128)(2,1)} %collective-permute-done.4, bf16[512,384]{1,0:T(8,128)(2,1)} %collective-permute-done.3, ...), kind=kOutput, calls=%fused_computation.2 | convolution fusion | flops 811597824 | bytes 4456452 | tf_op jit(solution)/shard_map/dot_general | solution.py:25
  75.3 16.0 %collective-permute-done.1 = bf16[2048,256]{1,0:T(8,128)(2,1)S(1)} collective-permute-done((bf16[2048,256]{1,0:T(8,128)(2,1)S(1)}, bf16[2048,256]{1,0:T(8,128)(2,1)S(1)}, u32[]{:S(2)}, u32[]{:S(2)}) %collective-permute-start.1) | collective-permute-done | bytes 1048608 | tf_op jit(solution)/shard_map/ppermute | solution.py:113
  92.9 16.7 %collective-permute-done = bf16[2048,512]{1,0:T(8,128)(2,1)S(1)} collective-permute-done((bf16[2048,512]{1,0:T(8,128)(2,1)}, bf16[2048,512]{1,0:T(8,128)(2,1)S(1)}, u32[]{:S(2)}, u32[]{:S(2)}) %collective-permute-start) | collective-permute-done | bytes 2097184 | tf_op jit(solution)/shard_map/ppermute | solution.py:120
  113.6 3.4 %collective-permute-start.16 = (f32[520,384]{1,0:T(8,128)S(1)}, f32[520,384]{1,0:T(8,128)S(1)}, u32[]{:S(2)}, u32[]{:S(2)}) collective-permute-start(f32[520,384]{1,0:T(8,128)S(1)} %select_add_fusion), channel_id=1, source_target_pairs={{24,8},{0,16},{25,9},{1,17},{26,10},{2,18},{27,11},{3,19},{28,12},... | collective-permute-start | bytes 2396168 | tf_op jit(solution)/shard_map/ppermute | solution.py:167
  117.2 1.9 %collective-permute-start.20 = (f32[512,128]{1,0:T(8,128)S(1)}, f32[512,128]{1,0:T(8,128)S(1)}, u32[]{:S(2)}, u32[]{:S(2)}) collective-permute-start(f32[512,128]{1,0:T(8,128)S(1)} %slice_add_fusion.2), channel_id=1, source_target_pairs={{0,1},{1,0},{2,3},{3,2},{4,5},{5,4},{6,7},{7,6},{24,25},{25,24},{2... | collective-permute-start | bytes 786440 | tf_op jit(solution)/shard_map/ppermute | solution.py:93
  119.2 1.3 collective-permute-start.21
  120.6 3.9 %collective-permute-start.13 = (f32[520,256]{1,0:T(8,128)S(1)}, f32[520,256]{1,0:T(8,128)S(1)}, u32[]{:S(2)}, u32[]{:S(2)}) collective-permute-start(f32[520,256]{1,0:T(8,128)S(1)} %slice_add_fusion), channel_id=1, source_target_pairs={{0,1},{1,0},{2,3},{3,2},{4,5},{5,4},{6,7},{7,6},{24,25},{25,24},{2... | collective-permute-start | bytes 1597448 | tf_op jit(solution)/shard_map/ppermute | solution.py:93
  124.5 5.4 %collective-permute-done.22 = f32[8,128]{1,0:T(8,128)S(1)} collective-permute-done((f32[8,128]{1,0:T(8,128)S(1)}, f32[8,128]{1,0:T(8,128)S(1)}, u32[]{:S(2)}, u32[]{:S(2)}) %collective-permute-start.22) | collective-permute-done | bytes 4128 | tf_op jit(solution)/shard_map/ppermute | solution.py:169
  131.5 2.5 %collective-permute-done.13 = f32[520,256]{1,0:T(8,128)S(1)} collective-permute-done((f32[520,256]{1,0:T(8,128)S(1)}, f32[520,256]{1,0:T(8,128)S(1)}, u32[]{:S(2)}, u32[]{:S(2)}) %collective-permute-start.13) | collective-permute-done | bytes 532512 | tf_op jit(solution)/shard_map/ppermute | solution.py:93
  134.0 8.0 %collective-permute-done.14 = f32[520,256]{1,0:T(8,128)S(1)} collective-permute-done((f32[520,256]{1,0:T(8,128)S(1)}, f32[520,256]{1,0:T(8,128)S(1)}, u32[]{:S(2)}, u32[]{:S(2)}) %collective-permute-start.14) | collective-permute-done | bytes 532512 | tf_op jit(solution)/shard_map/ppermute | solution.py:93
  (80 shorter events, 14.1 us)
Async XLA Ops:
  0.0 9.3 %copy-start.1 = (bf16[4096,384]{1,0:T(8,128)(2,1)S(1)}, bf16[4096,384]{1,0:T(8,128)(2,1)}, u32[]{:S(2)}) copy-start(bf16[4096,384]{1,0:T(8,128)(2,1)} %phenotypes.3) | copy-start | bytes 9437188
  2.4 25.5 %collective-permute-start.4 = (bf16[512,384]{1,0:T(8,128)(2,1)}, bf16[512,384]{1,0:T(8,128)(2,1)}, u32[]{:S(2)}, u32[]{:S(2)}) collective-permute-start(bf16[512,384]{1,0:T(8,128)(2,1)} %get-tuple-element.23), channel_id=1, source_target_pairs={{0,1},{1,0},{2,3},{3,2},{4,5},{5,4},{6,7},{7,6},{8,9},{9,8},{10,11... | collective-permute-start | bytes 1179656 | tf_op jit(solution)/shard_map/ppermute | solution.py:113
  5.4 27.3 %collective-permute-start.3 = (bf16[512,384]{1,0:T(8,128)(2,1)}, bf16[512,384]{1,0:T(8,128)(2,1)}, u32[]{:S(2)}, u32[]{:S(2)}) collective-permute-start(bf16[512,384]{1,0:T(8,128)(2,1)} %get-tuple-element.24), channel_id=1, source_target_pairs={{0,1},{1,0},{2,3},{3,2},{4,5},{5,4},{6,7},{7,6},{8,9},{9,8},{10,11... | collective-permute-start | bytes 1179656 | tf_op jit(solution)/shard_map/ppermute | solution.py:113
  7.3 29.0 %collective-permute-start.2 = (bf16[512,384]{1,0:T(8,128)(2,1)}, bf16[512,384]{1,0:T(8,128)(2,1)}, u32[]{:S(2)}, u32[]{:S(2)}) collective-permute-start(bf16[512,384]{1,0:T(8,128)(2,1)} %slice.106), channel_id=1, source_target_pairs={{0,1},{1,0},{2,3},{3,2},{4,5},{5,4},{6,7},{7,6},{8,9},{9,8},{10,11... | collective-permute-start | bytes 1179656 | tf_op jit(solution)/shard_map/ppermute | solution.py:113
  9.3 3.4 %copy-start = (bf16[4096,1024]{1,0:T(8,128)(2,1)S(1)}, bf16[4096,1024]{1,0:T(8,128)(2,1)}, u32[]{:S(2)}) copy-start(bf16[4096,1024]{1,0:T(8,128)(2,1)} %dosages.3) | copy-start | bytes 25165828
  19.8 5.1 %copy-start.6 = (bf16[512,384]{1,0:T(8,128)(2,1)S(1)}, bf16[512,384]{1,0:T(8,128)(2,1)}, u32[]{:S(2)}) copy-start(bf16[512,384]{1,0:T(8,128)(2,1)} %get-tuple-element.22) | copy-start | bytes 1179652
  24.9 87.3 %collective-permute-start.15 = (f32[520,384]{1,0:T(8,128)}, f32[520,384]{1,0:T(8,128)}, u32[]{:S(2)}, u32[]{:S(2)}) collective-permute-start(f32[520,384]{1,0:T(8,128)} %broadcast_select_fusion), channel_id=1, source_target_pairs={{0,8},{8,0},{16,24},{24,16},{1,9},{9,1},{17,25},{25,17},{2,10},{10... | collective-permute-start | bytes 2396168 | tf_op jit(solution)/shard_map/ppermute | solution.py:148
  24.9 16.8 %collective-permute-start.5 = (bf16[512,384]{1,0:T(8,128)(2,1)S(1)}, bf16[512,384]{1,0:T(8,128)(2,1)}, u32[]{:S(2)}, u32[]{:S(2)}) collective-permute-start(bf16[512,384]{1,0:T(8,128)(2,1)S(1)} %copy-done.6), channel_id=1, source_target_pairs={{0,1},{1,0},{2,3},{3,2},{4,5},{5,4},{6,7},{7,6},{8,9},{9,8},{10,11... | collective-permute-start | bytes 1179656 | tf_op jit(solution)/shard_map/ppermute | solution.py:113
  28.0 15.9 %collective-permute-start.9 = (bf16[512,384]{1,0:T(8,128)(2,1)}, bf16[512,384]{1,0:T(8,128)(2,1)}, u32[]{:S(2)}, u32[]{:S(2)}) collective-permute-start(bf16[512,384]{1,0:T(8,128)(2,1)} %collective-permute-done.4), channel_id=1, source_target_pairs={{0,2},{2,4},{4,6},{3,1},{5,3},{7,5},{8,10},{10,12},{12,14},{11,9},... | collective-permute-start | bytes 1179656 | tf_op jit(solution)/shard_map/ppermute | solution.py:117
  32.7 17.4 %collective-permute-start.8 = (bf16[512,384]{1,0:T(8,128)(2,1)}, bf16[512,384]{1,0:T(8,128)(2,1)}, u32[]{:S(2)}, u32[]{:S(2)}) collective-permute-start(bf16[512,384]{1,0:T(8,128)(2,1)} %collective-permute-done.3), channel_id=1, source_target_pairs={{0,2},{2,4},{4,6},{3,1},{5,3},{7,5},{8,10},{10,12},{12,14},{11,9},... | collective-permute-start | bytes 1179656 | tf_op jit(solution)/shard_map/ppermute | solution.py:117
  36.2 22.4 %collective-permute-start.7 = (bf16[512,384]{1,0:T(8,128)(2,1)}, bf16[512,384]{1,0:T(8,128)(2,1)}, u32[]{:S(2)}, u32[]{:S(2)}) collective-permute-start(bf16[512,384]{1,0:T(8,128)(2,1)} %collective-permute-done.2), channel_id=1, source_target_pairs={{0,2},{2,4},{4,6},{3,1},{5,3},{7,5},{8,10},{10,12},{12,14},{11,9},... | collective-permute-start | bytes 1179656 | tf_op jit(solution)/shard_map/ppermute | solution.py:117
  41.6 24.6 %collective-permute-start.10 = (bf16[512,384]{1,0:T(8,128)(2,1)}, bf16[512,384]{1,0:T(8,128)(2,1)S(1)}, u32[]{:S(2)}, u32[]{:S(2)}) collective-permute-start(bf16[512,384]{1,0:T(8,128)(2,1)} %collective-permute-done.5), channel_id=1, source_target_pairs={{0,2},{2,4},{4,6},{3,1},{5,3},{7,5},{8,10},{10,12},{12,14},{11,9},... | collective-permute-start | bytes 1179656 | tf_op jit(solution)/shard_map/ppermute | solution.py:117
  43.9 30.9 %collective-permute-start.17 = (bf16[1024,128]{1,0:T(8,128)(2,1)}, bf16[1024,128]{1,0:T(8,128)(2,1)S(1)}, u32[]{:S(2)}, u32[]{:S(2)}) collective-permute-start(bf16[1024,128]{1,0:T(8,128)(2,1)} %get-tuple-element.21), channel_id=1, source_target_pairs={{0,1},{1,0},{2,3},{3,2},{4,5},{5,4},{6,7},{7,6},{8,9},{9,8},{10,11... | collective-permute-start | bytes 786440 | tf_op jit(solution)/shard_map/ppermute | solution.py:113
  50.2 16.1 %copy-start.5 = (bf16[2048,256]{1,0:T(8,128)(2,1)S(1)}, bf16[2048,256]{1,0:T(8,128)(2,1)}, u32[]{:S(2)}) copy-start(bf16[2048,256]{1,0:T(8,128)(2,1)} %slice.130) | copy-start | bytes 3145732
  50.2 20.1 %collective-permute-start.18 = (bf16[1024,128]{1,0:T(8,128)(2,1)}, bf16[1024,128]{1,0:T(8,128)(2,1)S(1)}, u32[]{:S(2)}, u32[]{:S(2)}) collective-permute-start(bf16[1024,128]{1,0:T(8,128)(2,1)} %get-tuple-element.20), channel_id=1, source_target_pairs={{0,1},{1,0},{2,3},{3,2},{4,5},{5,4},{6,7},{7,6},{8,9},{9,8},{10,11... | collective-permute-start | bytes 786440 | tf_op jit(solution)/shard_map/ppermute | solution.py:113
  58.6 51.1 %collective-permute-start = (bf16[2048,512]{1,0:T(8,128)(2,1)}, bf16[2048,512]{1,0:T(8,128)(2,1)S(1)}, u32[]{:S(2)}, u32[]{:S(2)}) collective-permute-start(bf16[2048,512]{1,0:T(8,128)(2,1)} %constant_dynamic-slice_fusion), channel_id=1, source_target_pairs={{2,0},{4,2},{6,4},{1,3},{3,5},{5,7},{10,8},{12,10},{14,12},{9,11},... | collective-permute-start | bytes 6291464 | tf_op jit(solution)/shard_map/ppermute | solution.py:120
  59.9 12.2 %slice-start = ((s8[8388608]{0:T(1024)(128)(4,1)}), s8[4194304]{0:T(1024)(128)(4,1)S(1)}, s32[]{:S(2)}) async-start(s8[8388608]{0:T(1024)(128)(4,1)} %bitcast.18), calls=%async_computation | async-start | bytes 8388608
  62.8 9.4 %slice-start.1 = ((s8[8388608]{0:T(1024)(128)(4,1)}), s8[4194304]{0:T(1024)(128)(4,1)S(1)}, s32[]{:S(2)}) async-start(s8[8388608]{0:T(1024)(128)(4,1)} %bitcast.18), calls=%async_computation.1 | async-start | bytes 8388608
  66.3 25.0 %collective-permute-start.1 = (bf16[2048,256]{1,0:T(8,128)(2,1)S(1)}, bf16[2048,256]{1,0:T(8,128)(2,1)S(1)}, u32[]{:S(2)}, u32[]{:S(2)}) collective-permute-start(bf16[2048,256]{1,0:T(8,128)(2,1)S(1)} %copy-done.5), channel_id=1, source_target_pairs={{0,1},{1,0},{2,3},{3,2},{4,5},{5,4},{6,7},{7,6},{8,9},{9,8},{10,11... | collective-permute-start | bytes 3145736 | tf_op jit(solution)/shard_map/ppermute | solution.py:113
  70.3 21.7 %collective-permute-start.11 = (f32[520,384]{1,0:T(8,128)S(1)}, f32[520,384]{1,0:T(8,128)S(1)}, u32[]{:S(2)}, u32[]{:S(2)}) collective-permute-start(f32[520,384]{1,0:T(8,128)S(1)} %fusion.32), channel_id=1, source_target_pairs={{0,8},{8,0},{16,24},{24,16},{1,9},{9,1},{17,25},{25,17},{2,10},{10... | collective-permute-start | bytes 2396168 | tf_op jit(solution)/shard_map/ppermute | solution.py:148
  92.2 25.0 %collective-permute-start.12 = (f32[520,384]{1,0:T(8,128)S(1)}, f32[520,384]{1,0:T(8,128)S(1)}, u32[]{:S(2)}, u32[]{:S(2)}) collective-permute-start(f32[520,384]{1,0:T(8,128)S(1)} %select_add_fusion.1), channel_id=1, source_target_pairs={{1,3},{3,5},{5,7},{10,8},{12,10},{14,12},{17,19},{19,21},{21,23},{... | collective-permute-start | bytes 2396168 | tf_op jit(solution)/shard_map/ppermute | solution.py:93
  111.0 1.4 copy-start.4
  111.0 9.5 %collective-permute-start.6 = (f32[520,256]{1,0:T(8,128)S(1)}, f32[520,256]{1,0:T(8,128)S(1)}, u32[]{:S(2)}, u32[]{:S(2)}) collective-permute-start(f32[520,256]{1,0:T(8,128)S(1)} %fusion.35), channel_id=1, source_target_pairs={{0,8},{8,0},{16,24},{24,16},{1,9},{9,1},{17,25},{25,17},{2,10},{10... | collective-permute-start | bytes 1597448 | tf_op jit(solution)/shard_map/ppermute | solution.py:148
  111.6 5.5 %collective-permute-start.19 = (f32[512,128]{1,0:T(8,128)S(1)}, f32[512,128]{1,0:T(8,128)S(1)}, u32[]{:S(2)}, u32[]{:S(2)}) collective-permute-start(f32[512,128]{1,0:T(8,128)S(1)} %get-tuple-element.17), channel_id=1, source_target_pairs={{0,8},{8,0},{16,24},{24,16},{1,9},{9,1},{17,25},{25,17},{2,10},{10... | collective-permute-start | bytes 786440 | tf_op jit(solution)/shard_map/ppermute | solution.py:148
  113.6 17.7 %collective-permute-start.16 = (f32[520,384]{1,0:T(8,128)S(1)}, f32[520,384]{1,0:T(8,128)S(1)}, u32[]{:S(2)}, u32[]{:S(2)}) collective-permute-start(f32[520,384]{1,0:T(8,128)S(1)} %select_add_fusion), channel_id=1, source_target_pairs={{24,8},{0,16},{25,9},{1,17},{26,10},{2,18},{27,11},{3,19},{28,12},... | collective-permute-start | bytes 2396168 | tf_op jit(solution)/shard_map/ppermute | solution.py:167
  117.1 12.9 %collective-permute-start.22 = (f32[8,128]{1,0:T(8,128)S(1)}, f32[8,128]{1,0:T(8,128)S(1)}, u32[]{:S(2)}, u32[]{:S(2)}) collective-permute-start(f32[8,128]{1,0:T(8,128)S(1)} %slice.146), channel_id=1, source_target_pairs={{0,16},{8,24},{16,0},{24,8},{1,17},{9,25},{17,1},{25,9},{2,18},{10... | collective-permute-start | bytes 12296 | tf_op jit(solution)/shard_map/ppermute | solution.py:169
  117.2 14.2 %collective-permute-start.20 = (f32[512,128]{1,0:T(8,128)S(1)}, f32[512,128]{1,0:T(8,128)S(1)}, u32[]{:S(2)}, u32[]{:S(2)}) collective-permute-start(f32[512,128]{1,0:T(8,128)S(1)} %slice_add_fusion.2), channel_id=1, source_target_pairs={{0,1},{1,0},{2,3},{3,2},{4,5},{5,4},{6,7},{7,6},{24,25},{25,24},{2... | collective-permute-start | bytes 786440 | tf_op jit(solution)/shard_map/ppermute | solution.py:93
  119.2 12.3 %collective-permute-start.21 = (f32[512,128]{1,0:T(8,128)S(1)}, f32[512,128]{1,0:T(8,128)S(1)}, u32[]{:S(2)}, u32[]{:S(2)}) collective-permute-start(f32[512,128]{1,0:T(8,128)S(1)} %slice_add_fusion.2), channel_id=1, source_target_pairs={{16,1},{17,0},{18,3},{19,2},{20,5},{21,4},{22,7},{23,6},{8,25},{9,... | collective-permute-start | bytes 786440 | tf_op jit(solution)/shard_map/ppermute | solution.py:93
  120.6 13.4 %collective-permute-start.13 = (f32[520,256]{1,0:T(8,128)S(1)}, f32[520,256]{1,0:T(8,128)S(1)}, u32[]{:S(2)}, u32[]{:S(2)}) collective-permute-start(f32[520,256]{1,0:T(8,128)S(1)} %slice_add_fusion), channel_id=1, source_target_pairs={{0,1},{1,0},{2,3},{3,2},{4,5},{5,4},{6,7},{7,6},{24,25},{25,24},{2... | collective-permute-start | bytes 1597448 | tf_op jit(solution)/shard_map/ppermute | solution.py:93
  130.0 12.0 %collective-permute-start.14 = (f32[520,256]{1,0:T(8,128)S(1)}, f32[520,256]{1,0:T(8,128)S(1)}, u32[]{:S(2)}, u32[]{:S(2)}) collective-permute-start(f32[520,256]{1,0:T(8,128)S(1)} %slice_add_fusion), channel_id=1, source_target_pairs={{16,1},{17,0},{18,3},{19,2},{20,5},{21,4},{22,7},{23,6},{8,25},{9,... | collective-permute-start | bytes 1597448 | tf_op jit(solution)/shard_map/ppermute | solution.py:93
  131.4 10.8 %copy-start.7 = (s32[384]{0:T(512)S(1)}, s32[384]{0:T(512)}, u32[]{:S(2)}) copy-start(s32[384]{0:T(512)} %param.7) | copy-start | bytes 4612
  131.4 10.8 %copy-start.8 = (s32[384]{0:T(512)S(1)}, s32[384]{0:T(512)}, u32[]{:S(2)}) copy-start(s32[384]{0:T(512)} %param.6) | copy-start | bytes 4612
  (2 other events, 2.4 us)

commit v2 on v1

v2 whole, which is shorter than its diff:
```python
import functools
import math

import jax
import jax.numpy as jnp
from jax import lax
from jax.experimental import pallas as pl
from jax.experimental.pallas import tpu as pltpu
from jax.sharding import PartitionSpec as P


HALO = 512
EPS = 1e-06
LANES = 128
TAIL = 8
EARLY_SHARE = 8
EARLY_PARTS = 4
END_SHARE = 2
GROUP_TILES = (2,)
X_STAGE = False
OWN_CALLS = 2
OWN_STEPS = 4
OWN_VMEM = 20 * 1024 * 1024


def cross_rows(variant_panel, phenotypes):
    return lax.dot_general(
        variant_panel, phenotypes, (((0,), (0,)), ((), ())), preferred_element_type=jnp.float32
    )


def added(total, part):
    return part if total is None else lax.optimization_barrier(total) + part


def folded_squares(block):
    wide = block.astype(jnp.float32)
    return jnp.sum((wide * wide).reshape(-1, 8, wide.shape[1]), axis=0)


def own_kernel(share_rows, dosages, phenotypes, *refs):
    (*pieces, tails), (cross, variant_sq, peak_sq) = refs[:-3], refs[-3:]
    split = tails.shape[1]
    last = phenotypes.shape[1] - LANES

    @pl.when(pl.program_id(0) == 0)
    def _():
        for ref in (cross, variant_sq, peak_sq):
            ref[...] = jnp.zeros_like(ref)

    cross[...] += cross_rows(dosages[...], phenotypes[...])
    variant_sq[...] += folded_squares(dosages[...])
    peak_sq[...] += folded_squares(phenotypes[...])

    @pl.when(pl.program_id(0) == pl.num_programs(0) - 1)
    def _():
        variant_sums = jnp.sum(variant_sq[...], axis=0, keepdims=True)
        peak_sums = jnp.sum(peak_sq[...], axis=0, keepdims=True)
        tails[...] = jnp.zeros_like(tails)
        for k, piece in enumerate(pieces):
            first = k * share_rows
            piece[:share_rows] = cross[first : first + share_rows]
            piece[share_rows:] = jnp.zeros((TAIL, piece.shape[1]), jnp.float32)
            for row in range(share_rows // split):
                sums = variant_sums[:, first + row * split : first + (row + 1) * split]
                piece[share_rows + row : share_rows + row + 1, :split] = sums
                tails[k * TAIL + row : k * TAIL + row + 1] = sums
            for row in range(peak_sums.shape[1] // LANES):
                sums = peak_sums[:, row * LANES : (row + 1) * LANES]
                piece[share_rows + row : share_rows + row + 1, last:] = sums


def own_block(dosages, phenotypes, share_rows, split, part):
    sample_rows, block_width = dosages.shape
    peak_width = phenotypes.shape[1]
    rows = sample_rows // OWN_STEPS
    shares = block_width // share_rows
    steps = OWN_STEPS // OWN_CALLS
    shapes = [(share_rows + TAIL, peak_width)] * shares + [(shares * TAIL, split)]
    return pl.pallas_call(
        functools.partial(own_kernel, share_rows),
        grid=(steps,),
        in_specs=[
            pl.BlockSpec((rows, block_width), lambda i: (part * steps + i, 0)),
            pl.BlockSpec((rows, peak_width), lambda i: (part * steps + i, 0)),
        ],
        out_specs=[pl.BlockSpec(shape, lambda i: (0, 0)) for shape in shapes],
        out_shape=[jax.ShapeDtypeStruct(shape, jnp.float32) for shape in shapes],
        scratch_shapes=[
            pltpu.VMEM((block_width, peak_width), jnp.float32),
            pltpu.VMEM((8, block_width), jnp.float32),
            pltpu.VMEM((8, peak_width), jnp.float32),
        ],
        compiler_params=pltpu.CompilerParams(vmem_limit_bytes=OWN_VMEM),
        name="own_block",
    )(dosages, phenotypes)


def statistics_share(dosages, phenotypes, window_low, window_high):
    sample_rows, block_width = dosages.shape
    peak_width = phenotypes.shape[1]
    span_width = block_width + 2 * HALO
    samp_count = lax.axis_size("samp")
    pos_count = lax.axis_size("pos")
    samp_index = lax.axis_index("samp")
    pos_index = lax.axis_index("pos")
    share_rows = span_width // samp_count
    halo_shares = HALO // share_rows
    half = samp_count // 2
    all_samp = range(samp_count)
    all_pos = range(pos_count)
    ends = [0]
    for tiles in GROUP_TILES:
        ends.append(ends[-1] + tiles * LANES)
    groups = list(zip(ends, [*ends[1:], peak_width]))
    early = sample_rows * EARLY_SHARE // 16
    end = sample_rows - sample_rows * END_SHARE // 16
    step = early // EARLY_PARTS

    even = (pos_index & 1) == 0
    near_start = jnp.where(even, block_width - HALO, 0)
    far_start = jnp.where(even, 0, block_width - HALO)
    outer = (samp_index < halo_shares) | (samp_index >= samp_count - halo_shares)
    odd_at = [(samp_index & (1 << i)) != 0 for i in range(samp_count.bit_length() - 2)]
    first_variant = pos_index * block_width - HALO + samp_index * share_rows
    dosages, phenotypes, even, near_start, far_start, outer, odd_at, first_variant = lax.optimization_barrier(
        (dosages, phenotypes, even, near_start, far_start, outer, odd_at, first_variant)
    )

    def hop(array, pairs):
        flat = [(a * pos_count + b, c * pos_count + d) for a, b, c, d in pairs]
        return lax.ppermute(array, ("samp", "pos"), flat)

    def parity(x, y):
        return jnp.where(even, x, y)

    swap = [(b, b ^ 1) for b in all_pos]
    onward = [(b, b + 2) for b in range(0, pos_count - 2, 2)] + [(b, b - 2) for b in range(3, pos_count, 2)]
    back = [(d, s) for s, d in onward]

    def half_rows(start, low, high):
        return lax.dynamic_slice(dosages, (low, start), (high - low, HALO), allow_negative_indices=False)

    windows = [(i * step, (i + 1) * step, 0, peak_width) for i in range(EARLY_PARTS)]
    windows += [(early, sample_rows, low, high) for low, high in groups[:-1]]
    windows += [(early, end, ends[-1], peak_width), (end, sample_rows, ends[-1], peak_width)]
    held, source = [], phenotypes
    for i, (a, b, c, d) in enumerate(windows):
        piece = lax.slice(source, (a, c), (b, d))
        held.append(lax.ppermute(piece, "pos", swap))
        if i == 0:
            source = lax.optimization_barrier(phenotypes)
    first, late, right, tip = held[:EARLY_PARTS], held[EARLY_PARTS:-2], held[-2], held[-1]
    passed = [lax.ppermute(x, "pos", onward) for x in first]

    far_late = lax.optimization_barrier(half_rows(far_start, early, sample_rows))
    far_in = lax.ppermute(far_late, "pos", back)

    inner_shares = list(range(halo_shares, samp_count - halo_shares))
    outer_shares = [*range(halo_shares), *range(samp_count - halo_shares, samp_count)]
    bits = [1 << i for i in range(samp_count.bit_length() - 2)]

    def pieces_of(first, second, owners):
        out = []
        for k, t in enumerate(owners):
            rows, tails = first if k < halo_shares else second
            low = (k % halo_shares) * share_rows
            piece = rows[low : low + share_rows]
            out.append((t, jnp.concatenate([piece, tails[k % halo_shares]]) if tails else piece))
        return out

    def exchange(tagged, bit):
        mine = odd_at[bit.bit_length() - 1]
        zeros = [x for x in tagged if (x[0] // bit) % 2 == 0]
        ones = [x for x in tagged if (x[0] // bit) % 2 == 1]
        kept = []
        for (tag, z), (_, o) in zip(zeros, ones):
            keep, send = jnp.where(mine, o, z), jnp.where(mine, z, o)
            kept.append((tag, keep + lax.ppermute(send, "samp", [(s, s ^ bit) for s in all_samp])))
        return kept

    parts = []
    for part in range(OWN_CALLS):
        parts.append(own_block(dosages, phenotypes, share_rows, groups[0][1], part))
    *own, tails = [sum(x[1:], x[0]) for x in zip(*parts)]
    tails = [tails[k * TAIL : (k + 1) * TAIL] for k in range(len(own))]
    own = list(zip(inner_shares, own))
    low_tails, high_tails = tails[:halo_shares], tails[-halo_shares:]
    near_tails = [parity(h, l) for h, l in zip(high_tails, low_tails)]
    far_tails = [parity(l, h) for h, l in zip(high_tails, low_tails)]
    for bit in bits:
        own = exchange(own, bit)
    ((_, own),) = own
    own_total = own + lax.ppermute(own, "samp", [(t ^ half, t) for t in inner_shares])
    peak_total = jnp.maximum(own[share_rows:, peak_width - LANES :], 0.0)
    peak_total = peak_total + lax.ppermute(peak_total, "samp", [(s, s ^ half) for s in all_samp])
    peak_total = peak_total[: peak_width // LANES].reshape(peak_width)

    near_early = cross_rows(half_rows(near_start, 0, early), jnp.concatenate(first))
    far_early = cross_rows(half_rows(far_start, 0, early - step), jnp.concatenate(passed[:-1]))
    far_early = added(far_early, cross_rows(half_rows(far_start, early - step, early), passed[-1]))

    wide = [jnp.pad(x, ((0, 0), (0, peak_width - x.shape[1]))) for x in far_tails]
    acc = pieces_of(
        (parity(0.0, far_early), [parity(0.0, x) for x in wide]),
        (parity(far_early, 0.0), [parity(x, 0.0) for x in wide]),
        outer_shares,
    )
    acc = exchange(acc, 1)
    acc_pairs = [(s, b, s, d) for s in all_samp for b, d in back if halo_shares > 1 or (s + b) % 2 == 1]
    acc = [hop(x, acc_pairs) for _, x in acc]

    straight = [(t, b, t, b ^ 1) for t in outer_shares for b in all_pos]
    across = [(t ^ half, b, t, b ^ 1) for t in outer_shares for b in all_pos]

    def reduced(pieces, low, high):
        pieces = exchange(pieces, 1)
        pieces = [(t, x + y[: x.shape[0], low:high]) for (t, x), y in zip(pieces, acc)]
        for bit in bits[1:]:
            pieces = exchange(pieces, bit)
        ((_, only),) = pieces
        return only

    totals = []
    for g, ((low, high), peaks) in enumerate(zip(groups, late)):
        near_edge = near_early[:, low:high] + cross_rows(half_rows(near_start, early, sample_rows), peaks)
        far_edge = cross_rows(far_in, peaks)
        up, down = parity(near_edge, far_edge), parity(far_edge, near_edge)
        up_tails = [parity(x, 0.0) for x in near_tails] if g == 0 else None
        down_tails = [parity(0.0, x) for x in near_tails] if g == 0 else None
        edge = reduced(pieces_of((up, up_tails), (down, down_tails), outer_shares), low, high)
        if X_STAGE:
            edge = edge + lax.ppermute(edge, "samp", [(t ^ half, t) for t in outer_shares])
            totals.append(hop(edge, straight))
        else:
            totals.append(hop(edge, straight) + hop(edge, across))

    low, high = groups[-1]
    near_edge = near_early[:, low:high] + cross_rows(half_rows(near_start, early, end), right)
    far_edge = cross_rows(far_in[: end - early], right)
    near_edge = added(near_edge, cross_rows(half_rows(near_start, end, sample_rows), tip))
    far_edge = added(far_edge, cross_rows(far_in[end - early :], tip))
    up, down = parity(near_edge, far_edge), parity(far_edge, near_edge)
    edge = reduced(pieces_of((up, None), (down, None), outer_shares), low, high)
    totals.append(hop(edge, straight) + hop(edge, across))

    shares = [
        jnp.where(outer, total, own_total[: total.shape[0], low:high]) for total, (low, high) in zip(totals, groups)
    ]
    split = groups[0][1]
    variant_share = shares[0][share_rows : share_rows + share_rows // split].reshape(share_rows)
    cross_share = jnp.concatenate([x[:share_rows] for x in shares], axis=1)

    variant_index = first_variant + jnp.arange(share_rows, dtype=jnp.int32)[:, None]
    inside = (variant_index >= window_low[None, :]) & (variant_index <= window_high[None, :])
    factor = math.sqrt(float(sample_rows * samp_count - 2))
    scale_terms = (variant_share[:, None] + EPS) * (peak_total[None, :] + EPS)
    statistic = factor * cross_share / jnp.sqrt(scale_terms)
    return jnp.where(inside, statistic, jnp.zeros_like(statistic))[None]


def solution(mesh):
    placed = (P("samp", "pos"), P("samp", "pos"), P("pos"), P("pos"))
    return jax.shard_map(
        statistics_share, mesh=mesh, in_specs=placed, out_specs=P("pos", "samp", None), check_vma=False
    )
```

time: 144 us -> 133 us (0.924)
  local copies, waits for them, and re-layouts: 16.8 us -> 7.2 us
  other arithmetic: 5.73 us -> 2.62 us
  matrix products: 11.7 us -> 9.04 us
  waiting for transfers between devices: 64.3 us -> 66.5 us
  starting transfers between devices: 38.6 us -> 40.3 us
    ppermute x7, waiting for transfers between devices: 16 us -> 26.1 us  [statistics_share(): held.append(lax.ppermute(piece, 'pos', swap))]
    ppermute x4, waiting for transfers between devices: 15.5 us -> 8.85 us  [statistics_share(): passed = [lax.ppermute(x, 'pos', onward) for x in first]]
    slice x4 -> x5, local copies, waits for them, and re-layouts: 6.16 us -> 2.64 us  [statistics_share(): piece = lax.slice(source, (a, c), (b, d))]
    slice x5 -> x0, local copies, waits for them, and re-layouts: 2.73 us -> none  [the longest x1 2.69 us: statistics_share(): own[block_width - HALO:]]
    dot_general x9, matrix products: 11.7 us -> 9.04 us  [cross_rows(): lax.dot_general(variant_panel, phenotypes, (((0,), (0,)), ((), ())), pref...]
    select_n x4, other arithmetic: 2.58 us -> 0.46 us  [exchange(): keep, send = (jnp.where(mine, o, z), jnp.where(mine, z, o))]
    dynamic_slice x1, local copies, waits for them, and re-layouts: 3.08 us -> 1.11 us  [half_rows(): lax.dynamic_slice(dosages, (low, start), (high - low, HALO), allow_negati...]
    ppermute x4, starting transfers between devices: 13.9 us -> 15.6 us  [statistics_share(): passed = [lax.ppermute(x, 'pos', onward) for x in first]]
  transfers between devices with their start and end apart: 23 -> 23, of which waited for: 8 -> 10; matrix products, arithmetic and copies ran while one was open for 18% -> 10% of each run, Pallas kernels for 4% -> 5%
where the time goes in v2:
time: 133 us; the launch traced here: 132 us
  waiting for transfers between devices  66.5 us (50%)
  starting transfers between devices  40.3 us (30%)
  matrix products  9.04 us (7%)
  local copies, waits for them, and re-layouts  7.2 us (5%)
  Pallas kernels  5.96 us (4%)
  other arithmetic  2.62 us (2%)
    ppermute x7, waiting for transfers between devices, statistics_share(): held.append(lax.ppermute(piece, 'pos', swap))  26.1 us
    ppermute x1, waiting for transfers between devices, statistics_share(): far_in = lax.ppermute(far_late, 'pos', back)  15.9 us
    ppermute x4, starting transfers between devices, statistics_share(): passed = [lax.ppermute(x, 'pos', onward) for x in first]  15.6 us
    ppermute x5, waiting for transfers between devices, hop(): return lax.ppermute(array, ('samp', 'pos'), flat)  10.5 us
    ppermute x7, starting transfers between devices, statistics_share(): held.append(lax.ppermute(piece, 'pos', swap))  9.75 us
    ppermute x5, starting transfers between devices, hop(): return lax.ppermute(array, ('samp', 'pos'), flat)  9.13 us
    dot_general x9, matrix products, cross_rows(): lax.dot_general(variant_panel, phenotypes, (((0,), (0,)), ((), ())), pref...  9.04 us
    ppermute x4, waiting for transfers between devices, statistics_share(): passed = [lax.ppermute(x, 'pos', onward) for x in first]  8.85 us
  transfers between devices with their start and end apart: 23, of which 10 were waited for; matrix products, arithmetic and copies ran while one was open for 10% of the time, Pallas kernels for 5%

profile of v2, /device:TPU:0, one launch (start us, length us, event | category | flops | bytes accessed | tf_op | source)
XLA Modules:
  0.0 132.1 jit_solution(3185340959282643346)
XLA Ops:
  0.0 1.5 %fusion.45 = (bf16[512,384]{1,0:T(8,128)(2,1)S(1)}, bf16[512,384]{1,0:T(8,128)(2,1)S(1)}, bf16[512,384]{1,0:T(8,128)(2,1)S(1)}) fusion(bf16[4096,384]{1,0:T(8,128)(2,1)} %phenotypes.1), kind=kLoop, calls=%fused_computation.76 | loop fusion | bytes 2359296 | tf_op jit(solution)/shard_map/slice | solution.py:149
  1.5 3.1 %collective-permute-start.4 = (bf16[512,384]{1,0:T(8,128)(2,1)S(1)}, bf16[512,384]{1,0:T(8,128)(2,1)S(1)}, u32[]{:S(2)}, u32[]{:S(2)}) collective-permute-start(bf16[512,384]{1,0:T(8,128)(2,1)S(1)} %get-tuple-element.37), channel_id=1, source_target_pairs={{0,1},{1,0},{2,3},{3,2},{4,5},{5,4},{6,7},{7,6},{8,9},{9,8},{10,11... | collective-permute-start | bytes 1179656 | tf_op jit(solution)/shard_map/ppermute | solution.py:150
  5.7 2.0 %collective-permute-start.2 = (bf16[512,384]{1,0:T(8,128)(2,1)S(1)}, bf16[512,384]{1,0:T(8,128)(2,1)S(1)}, u32[]{:S(2)}, u32[]{:S(2)}) collective-permute-start(bf16[512,384]{1,0:T(8,128)(2,1)S(1)} %slice.64), channel_id=1, source_target_pairs={{0,1},{1,0},{2,3},{3,2},{4,5},{5,4},{6,7},{7,6},{8,9},{9,8},{10,11... | collective-permute-start | bytes 1179656 | tf_op jit(solution)/shard_map/ppermute | solution.py:150
  7.7 3.4 %copy-done = bf16[4096,1024]{1,0:T(8,128)(2,1)S(1)} copy-done((bf16[4096,1024]{1,0:T(8,128)(2,1)S(1)}, bf16[4096,1024]{1,0:T(8,128)(2,1)}, u32[]{:S(2)}) %copy-start) | copy-done | bytes 8388632
  11.1 3.0 %own_block.2 = (f32[520,384]{1,0:T(8,128)S(1)}, f32[520,384]{1,0:T(8,128)S(1)}, f32[16,256]{1,0:T(8,128)S(1)}) custom-call(bf16[4096,1024]{1,0:T(8,128)(2,1)S(1)} %copy-done, bf16[4096,384]{1,0:T(8,128)(2,1)S(1)} %copy-done.1), custom_call_target="tpu_custom_call" | custom-call | tf_op jit(solution)/shard_map/own_block/pallas_call | solution.py:80
  14.1 3.0 %own_block.3 = (f32[520,384]{1,0:T(8,128)S(1)}, f32[520,384]{1,0:T(8,128)S(1)}, f32[16,256]{1,0:T(8,128)S(1)}) custom-call(bf16[4096,1024]{1,0:T(8,128)(2,1)S(1)} %copy-done, bf16[4096,384]{1,0:T(8,128)(2,1)S(1)} %copy-done.1), custom_call_target="tpu_custom_call" | custom-call | tf_op jit(solution)/shard_map/own_block/pallas_call | solution.py:80
  18.8 3.9 %collective-permute-start.9 = (bf16[512,384]{1,0:T(8,128)(2,1)S(1)}, bf16[512,384]{1,0:T(8,128)(2,1)S(1)}, u32[]{:S(2)}, u32[]{:S(2)}) collective-permute-start(bf16[512,384]{1,0:T(8,128)(2,1)S(1)} %collective-permute-done.4), channel_id=1, source_target_pairs={{0,2},{2,4},{4,6},{3,1},{5,3},{7,5},{8,10},{10,12},{12,14},{11,9},... | collective-permute-start | bytes 1179656 | tf_op jit(solution)/shard_map/ppermute | solution.py:154
  23.0 4.0 %collective-permute-start.8 = (bf16[512,384]{1,0:T(8,128)(2,1)S(1)}, bf16[512,384]{1,0:T(8,128)(2,1)S(1)}, u32[]{:S(2)}, u32[]{:S(2)}) collective-permute-start(bf16[512,384]{1,0:T(8,128)(2,1)S(1)} %collective-permute-done.3), channel_id=1, source_target_pairs={{0,2},{2,4},{4,6},{3,1},{5,3},{7,5},{8,10},{10,12},{12,14},{11,9},... | collective-permute-start | bytes 1179656 | tf_op jit(solution)/shard_map/ppermute | solution.py:154
  27.0 4.4 %collective-permute-done.2 = bf16[512,384]{1,0:T(8,128)(2,1)S(1)} collective-permute-done((bf16[512,384]{1,0:T(8,128)(2,1)S(1)}, bf16[512,384]{1,0:T(8,128)(2,1)S(1)}, u32[]{:S(2)}, u32[]{:S(2)}) %collective-permute-start.2) | collective-permute-done | bytes 393248 | tf_op jit(solution)/shard_map/ppermute | solution.py:150
  31.4 4.0 %collective-permute-start.7 = (bf16[512,384]{1,0:T(8,128)(2,1)S(1)}, bf16[512,384]{1,0:T(8,128)(2,1)S(1)}, u32[]{:S(2)}, u32[]{:S(2)}) collective-permute-start(bf16[512,384]{1,0:T(8,128)(2,1)S(1)} %collective-permute-done.2), channel_id=1, source_target_pairs={{0,2},{2,4},{4,6},{3,1},{5,3},{7,5},{8,10},{10,12},{12,14},{11,9},... | collective-permute-start | bytes 1179656 | tf_op jit(solution)/shard_map/ppermute | solution.py:154
  35.4 3.6 %collective-permute-done.5 = bf16[512,384]{1,0:T(8,128)(2,1)S(1)} collective-permute-done((bf16[512,384]{1,0:T(8,128)(2,1)S(1)}, bf16[512,384]{1,0:T(8,128)(2,1)S(1)}, u32[]{:S(2)}, u32[]{:S(2)}) %collective-permute-start.5) | collective-permute-done | bytes 393248 | tf_op jit(solution)/shard_map/ppermute | solution.py:150
  39.0 3.7 %collective-permute-start.10 = (bf16[512,384]{1,0:T(8,128)(2,1)S(1)}, bf16[512,384]{1,0:T(8,128)(2,1)S(1)}, u32[]{:S(2)}, u32[]{:S(2)}) collective-permute-start(bf16[512,384]{1,0:T(8,128)(2,1)S(1)} %collective-permute-done.5), channel_id=1, source_target_pairs={{0,2},{2,4},{4,6},{3,1},{5,3},{7,5},{8,10},{10,12},{12,14},{11,9},... | collective-permute-start | bytes 1179656 | tf_op jit(solution)/shard_map/ppermute | solution.py:154
  42.8 2.0 %collective-permute-start.18 = (bf16[512,128]{1,0:T(8,128)(2,1)S(1)}, bf16[512,128]{1,0:T(8,128)(2,1)S(1)}, u32[]{:S(2)}, u32[]{:S(2)}) collective-permute-start(bf16[512,128]{1,0:T(8,128)(2,1)S(1)} %slice.97), channel_id=1, source_target_pairs={{0,1},{1,0},{2,3},{3,2},{4,5},{5,4},{6,7},{7,6},{8,9},{9,8},{10,11... | collective-permute-start | bytes 393224 | tf_op jit(solution)/shard_map/ppermute | solution.py:150
  44.8 4.2 %collective-permute-done.7 = bf16[512,384]{1,0:T(8,128)(2,1)S(1)} collective-permute-done((bf16[512,384]{1,0:T(8,128)(2,1)S(1)}, bf16[512,384]{1,0:T(8,128)(2,1)S(1)}, u32[]{:S(2)}, u32[]{:S(2)}) %collective-permute-start.7) | collective-permute-done | bytes 393248 | tf_op jit(solution)/shard_map/ppermute | solution.py:154
  49.1 1.5 %collective-permute-start = (bf16[2048,512]{1,0:T(8,128)(2,1)S(1)}, bf16[2048,512]{1,0:T(8,128)(2,1)S(1)}, u32[]{:S(2)}, u32[]{:S(2)}) collective-permute-start(bf16[2048,512]{1,0:T(8,128)(2,1)S(1)} %constant_dynamic-slice_fusion), channel_id=1, source_target_pairs={{2,0},{4,2},{6,4},{1,3},{3,5},{5,7},{10,8},{12,10},{14,12},{9,11},... | collective-permute-start | bytes 6291464 | tf_op jit(solution)/shard_map/ppermute | solution.py:157
  50.5 1.5 %fusion.15 = f32[512,384]{1,0:T(8,128)S(1)} fusion(bf16[4096,1024]{1,0:T(8,128)(2,1)S(1)} %bitcast.18, s32[]{:T(128)S(6)} %select_n.149, bf16[512,384]{1,0:T(8,128)(2,1)S(1)} %collective-permute-done.9, bf16[512,384]{1,0:T(8,128)(2,1)S(1)} %collective-permute-done.8, bf16[512,384]{1,0:T(8,128)(2,1)S(1)} %collective-permute-done.7), kind=kOutput, calls=%fused_computation.15 | convolution fusion | flops 607518720 | bytes 3538948 | tf_op jit(solution)/shard_map/dot_general | solution.py:27
  52.1 4.6 %collective-permute-done.10 = bf16[512,384]{1,0:T(8,128)(2,1)S(1)} collective-permute-done((bf16[512,384]{1,0:T(8,128)(2,1)S(1)}, bf16[512,384]{1,0:T(8,128)(2,1)S(1)}, u32[]{:S(2)}, u32[]{:S(2)}) %collective-permute-start.10) | collective-permute-done | bytes 393248 | tf_op jit(solution)/shard_map/ppermute | solution.py:154
  56.7 2.4 %collective-permute-start.1 = (bf16[2048,256]{1,0:T(8,128)(2,1)S(1)}, bf16[2048,256]{1,0:T(8,128)(2,1)S(1)}, u32[]{:S(2)}, u32[]{:S(2)}) collective-permute-start(bf16[2048,256]{1,0:T(8,128)(2,1)S(1)} %slice.84), channel_id=1, source_target_pairs={{0,1},{1,0},{2,3},{3,2},{4,5},{5,4},{6,7},{7,6},{8,9},{9,8},{10,11... | collective-permute-start | bytes 3145736 | tf_op jit(solution)/shard_map/ppermute | solution.py:150
  60.7 1.9 %fusion.2 = f32[512,384]{1,0:T(8,128)S(1)} fusion(bf16[4096,1024]{1,0:T(8,128)(2,1)S(1)} %bitcast.18, s32[]{:T(128)S(6)} %select_n.148, bf16[512,384]{1,0:T(8,128)(2,1)S(1)} %collective-permute-done.5, bf16[512,384]{1,0:T(8,128)(2,1)S(1)} %collective-permute-done.4, bf16[512,384]{1,0:T(8,128)(2,1)S(1)} %collective-permute-done.3, ...), kind=kOutput, calls=%fused_computation.2 | convolution fusion | flops 811597824 | bytes 4456452 | tf_op jit(solution)/shard_map/dot_general | solution.py:27
  62.7 1.1 slice_add_fusion.3
  63.8 17.9 %collective-permute-done.1 = bf16[2048,256]{1,0:T(8,128)(2,1)S(1)} collective-permute-done((bf16[2048,256]{1,0:T(8,128)(2,1)S(1)}, bf16[2048,256]{1,0:T(8,128)(2,1)S(1)}, u32[]{:S(2)}, u32[]{:S(2)}) %collective-permute-start.1) | collective-permute-done | bytes 1048608 | tf_op jit(solution)/shard_map/ppermute | solution.py:150
  81.7 1.4 %fusion = f32[512,256]{1,0:T(8,128)S(1)} fusion(bf16[2048,256]{1,0:T(8,128)(2,1)S(1)} %collective-permute-done.1, bf16[4096,1024]{1,0:T(8,128)(2,1)S(1)} %bitcast.18, s32[]{:T(128)S(6)} %select_n.148), kind=kOutput, calls=%fused_computation | convolution fusion | flops 536870912 | bytes 3670020 | tf_op jit(solution)/shard_map/dot_general | solution.py:27
  84.0 15.9 %collective-permute-done = bf16[2048,512]{1,0:T(8,128)(2,1)S(1)} collective-permute-done((bf16[2048,512]{1,0:T(8,128)(2,1)S(1)}, bf16[2048,512]{1,0:T(8,128)(2,1)S(1)}, u32[]{:S(2)}, u32[]{:S(2)}) %collective-permute-start) | collective-permute-done | bytes 2097184 | tf_op jit(solution)/shard_map/ppermute | solution.py:157
  102.7 3.5 %collective-permute-start.16 = (f32[520,384]{1,0:T(8,128)S(1)}, f32[520,384]{1,0:T(8,128)S(1)}, u32[]{:S(2)}, u32[]{:S(2)}) collective-permute-start(f32[520,384]{1,0:T(8,128)S(1)} %select_add_fusion), channel_id=1, source_target_pairs={{24,8},{0,16},{25,9},{1,17},{26,10},{2,18},{27,11},{3,19},{28,12},... | collective-permute-start | bytes 2396168 | tf_op jit(solution)/shard_map/ppermute | solution.py:194
  106.3 2.7 %collective-permute-start.20 = (f32[512,128]{1,0:T(8,128)S(1)}, f32[512,128]{1,0:T(8,128)S(1)}, u32[]{:S(2)}, u32[]{:S(2)}) collective-permute-start(f32[512,128]{1,0:T(8,128)S(1)} %slice_add_fusion.2), channel_id=1, source_target_pairs={{0,1},{1,0},{2,3},{3,2},{4,5},{5,4},{6,7},{7,6},{24,25},{25,24},{2... | collective-permute-start | bytes 786440 | tf_op jit(solution)/shard_map/ppermute | solution.py:132
  109.0 1.3 collective-permute-start.21
  110.4 3.2 %collective-permute-start.13 = (f32[520,256]{1,0:T(8,128)S(1)}, f32[520,256]{1,0:T(8,128)S(1)}, u32[]{:S(2)}, u32[]{:S(2)}) collective-permute-start(f32[520,256]{1,0:T(8,128)S(1)} %slice_add_fusion), channel_id=1, source_target_pairs={{0,1},{1,0},{2,3},{3,2},{4,5},{5,4},{6,7},{7,6},{24,25},{25,24},{2... | collective-permute-start | bytes 1597448 | tf_op jit(solution)/shard_map/ppermute | solution.py:132
  113.6 5.1 %collective-permute-done.22 = f32[8,128]{1,0:T(8,128)S(1)} collective-permute-done((f32[8,128]{1,0:T(8,128)S(1)}, f32[8,128]{1,0:T(8,128)S(1)}, u32[]{:S(2)}, u32[]{:S(2)}) %collective-permute-start.22) | collective-permute-done | bytes 4128 | tf_op jit(solution)/shard_map/ppermute | solution.py:196
  118.7 1.3 collective-permute-start.14
  120.2 3.6 %collective-permute-done.13 = f32[520,256]{1,0:T(8,128)S(1)} collective-permute-done((f32[520,256]{1,0:T(8,128)S(1)}, f32[520,256]{1,0:T(8,128)S(1)}, u32[]{:S(2)}, u32[]{:S(2)}) %collective-permute-start.13) | collective-permute-done | bytes 532512 | tf_op jit(solution)/shard_map/ppermute | solution.py:132
  123.9 6.9 %collective-permute-done.14 = f32[520,256]{1,0:T(8,128)S(1)} collective-permute-done((f32[520,256]{1,0:T(8,128)S(1)}, f32[520,256]{1,0:T(8,128)S(1)}, u32[]{:S(2)}, u32[]{:S(2)}) %collective-permute-start.14) | collective-permute-done | bytes 532512 | tf_op jit(solution)/shard_map/ppermute | solution.py:132
  131.0 1.2 fusion.23
  (67 shorter events, 8.9 us)
Async XLA Ops:
  0.0 7.7 %copy-start.1 = (bf16[4096,384]{1,0:T(8,128)(2,1)S(1)}, bf16[4096,384]{1,0:T(8,128)(2,1)}, u32[]{:S(2)}) copy-start(bf16[4096,384]{1,0:T(8,128)(2,1)} %phenotypes.1) | copy-start | bytes 9437188
  1.5 17.3 %collective-permute-start.4 = (bf16[512,384]{1,0:T(8,128)(2,1)S(1)}, bf16[512,384]{1,0:T(8,128)(2,1)S(1)}, u32[]{:S(2)}, u32[]{:S(2)}) collective-permute-start(bf16[512,384]{1,0:T(8,128)(2,1)S(1)} %get-tuple-element.37), channel_id=1, source_target_pairs={{0,1},{1,0},{2,3},{3,2},{4,5},{5,4},{6,7},{7,6},{8,9},{9,8},{10,11... | collective-permute-start | bytes 1179656 | tf_op jit(solution)/shard_map/ppermute | solution.py:150
  4.6 18.4 %collective-permute-start.3 = (bf16[512,384]{1,0:T(8,128)(2,1)S(1)}, bf16[512,384]{1,0:T(8,128)(2,1)S(1)}, u32[]{:S(2)}, u32[]{:S(2)}) collective-permute-start(bf16[512,384]{1,0:T(8,128)(2,1)S(1)} %get-tuple-element.38), channel_id=1, source_target_pairs={{0,1},{1,0},{2,3},{3,2},{4,5},{5,4},{6,7},{7,6},{8,9},{9,8},{10,11... | collective-permute-start | bytes 1179656 | tf_op jit(solution)/shard_map/ppermute | solution.py:150
  5.7 25.7 %collective-permute-start.2 = (bf16[512,384]{1,0:T(8,128)(2,1)S(1)}, bf16[512,384]{1,0:T(8,128)(2,1)S(1)}, u32[]{:S(2)}, u32[]{:S(2)}) collective-permute-start(bf16[512,384]{1,0:T(8,128)(2,1)S(1)} %slice.64), channel_id=1, source_target_pairs={{0,1},{1,0},{2,3},{3,2},{4,5},{5,4},{6,7},{7,6},{8,9},{9,8},{10,11... | collective-permute-start | bytes 1179656 | tf_op jit(solution)/shard_map/ppermute | solution.py:150
  7.7 3.4 %copy-start = (bf16[4096,1024]{1,0:T(8,128)(2,1)S(1)}, bf16[4096,1024]{1,0:T(8,128)(2,1)}, u32[]{:S(2)}) copy-start(bf16[4096,1024]{1,0:T(8,128)(2,1)} %dosages.1) | copy-start | bytes 25165828
  11.1 6.5 %slice-start = ((s8[8388608]{0:T(1024)(128)(4,1)}), s8[4194304]{0:T(1024)(128)(4,1)S(1)}, s32[]{:S(2)}) async-start(s8[8388608]{0:T(1024)(128)(4,1)} %bitcast.17), calls=%async_computation | async-start | bytes 8388608
  14.1 3.6 %slice-start.1 = ((s8[8388608]{0:T(1024)(128)(4,1)}), s8[4194304]{0:T(1024)(128)(4,1)S(1)}, s32[]{:S(2)}) async-start(s8[8388608]{0:T(1024)(128)(4,1)} %bitcast.17), calls=%async_computation.1 | async-start | bytes 8388608
  17.3 85.1 %collective-permute-start.15 = (f32[520,384]{1,0:T(8,128)S(1)}, f32[520,384]{1,0:T(8,128)S(1)}, u32[]{:S(2)}, u32[]{:S(2)}) collective-permute-start(f32[520,384]{1,0:T(8,128)S(1)} %broadcast_select_fusion), channel_id=1, source_target_pairs={{0,8},{8,0},{16,24},{24,16},{1,9},{9,1},{17,25},{25,17},{2,10},{10... | collective-permute-start | bytes 2396168 | tf_op jit(solution)/shard_map/ppermute | solution.py:179
  17.4 21.6 %collective-permute-start.5 = (bf16[512,384]{1,0:T(8,128)(2,1)S(1)}, bf16[512,384]{1,0:T(8,128)(2,1)S(1)}, u32[]{:S(2)}, u32[]{:S(2)}) collective-permute-start(bf16[512,384]{1,0:T(8,128)(2,1)S(1)} %get-tuple-element.36), channel_id=1, source_target_pairs={{0,1},{1,0},{2,3},{3,2},{4,5},{5,4},{6,7},{7,6},{8,9},{9,8},{10,11... | collective-permute-start | bytes 1179656 | tf_op jit(solution)/shard_map/ppermute | solution.py:150
  18.8 23.9 %collective-permute-start.9 = (bf16[512,384]{1,0:T(8,128)(2,1)S(1)}, bf16[512,384]{1,0:T(8,128)(2,1)S(1)}, u32[]{:S(2)}, u32[]{:S(2)}) collective-permute-start(bf16[512,384]{1,0:T(8,128)(2,1)S(1)} %collective-permute-done.4), channel_id=1, source_target_pairs={{0,2},{2,4},{4,6},{3,1},{5,3},{7,5},{8,10},{10,12},{12,14},{11,9},... | collective-permute-start | bytes 1179656 | tf_op jit(solution)/shard_map/ppermute | solution.py:154
  23.0 19.8 %collective-permute-start.8 = (bf16[512,384]{1,0:T(8,128)(2,1)S(1)}, bf16[512,384]{1,0:T(8,128)(2,1)S(1)}, u32[]{:S(2)}, u32[]{:S(2)}) collective-permute-start(bf16[512,384]{1,0:T(8,128)(2,1)S(1)} %collective-permute-done.3), channel_id=1, source_target_pairs={{0,2},{2,4},{4,6},{3,1},{5,3},{7,5},{8,10},{10,12},{12,14},{11,9},... | collective-permute-start | bytes 1179656 | tf_op jit(solution)/shard_map/ppermute | solution.py:154
  31.4 17.7 %collective-permute-start.7 = (bf16[512,384]{1,0:T(8,128)(2,1)S(1)}, bf16[512,384]{1,0:T(8,128)(2,1)S(1)}, u32[]{:S(2)}, u32[]{:S(2)}) collective-permute-start(bf16[512,384]{1,0:T(8,128)(2,1)S(1)} %collective-permute-done.2), channel_id=1, source_target_pairs={{0,2},{2,4},{4,6},{3,1},{5,3},{7,5},{8,10},{10,12},{12,14},{11,9},... | collective-permute-start | bytes 1179656 | tf_op jit(solution)/shard_map/ppermute | solution.py:154
  39.0 17.7 %collective-permute-start.10 = (bf16[512,384]{1,0:T(8,128)(2,1)S(1)}, bf16[512,384]{1,0:T(8,128)(2,1)S(1)}, u32[]{:S(2)}, u32[]{:S(2)}) collective-permute-start(bf16[512,384]{1,0:T(8,128)(2,1)S(1)} %collective-permute-done.5), channel_id=1, source_target_pairs={{0,2},{2,4},{4,6},{3,1},{5,3},{7,5},{8,10},{10,12},{12,14},{11,9},... | collective-permute-start | bytes 1179656 | tf_op jit(solution)/shard_map/ppermute | solution.py:154
  42.7 19.9 %collective-permute-start.17 = (bf16[1536,128]{1,0:T(8,128)(2,1)S(1)}, bf16[1536,128]{1,0:T(8,128)(2,1)S(1)}, u32[]{:S(2)}, u32[]{:S(2)}) collective-permute-start(bf16[1536,128]{1,0:T(8,128)(2,1)S(1)} %slice.95), channel_id=1, source_target_pairs={{0,1},{1,0},{2,3},{3,2},{4,5},{5,4},{6,7},{7,6},{8,9},{9,8},{10,11... | collective-permute-start | bytes 1179656 | tf_op jit(solution)/shard_map/ppermute | solution.py:150
  42.8 17.2 %collective-permute-start.18 = (bf16[512,128]{1,0:T(8,128)(2,1)S(1)}, bf16[512,128]{1,0:T(8,128)(2,1)S(1)}, u32[]{:S(2)}, u32[]{:S(2)}) collective-permute-start(bf16[512,128]{1,0:T(8,128)(2,1)S(1)} %slice.97), channel_id=1, source_target_pairs={{0,1},{1,0},{2,3},{3,2},{4,5},{5,4},{6,7},{7,6},{8,9},{9,8},{10,11... | collective-permute-start | bytes 393224 | tf_op jit(solution)/shard_map/ppermute | solution.py:150
  49.1 50.9 %collective-permute-start = (bf16[2048,512]{1,0:T(8,128)(2,1)S(1)}, bf16[2048,512]{1,0:T(8,128)(2,1)S(1)}, u32[]{:S(2)}, u32[]{:S(2)}) collective-permute-start(bf16[2048,512]{1,0:T(8,128)(2,1)S(1)} %constant_dynamic-slice_fusion), channel_id=1, source_target_pairs={{2,0},{4,2},{6,4},{1,3},{3,5},{5,7},{10,8},{12,10},{14,12},{9,11},... | collective-permute-start | bytes 6291464 | tf_op jit(solution)/shard_map/ppermute | solution.py:157
  56.7 25.0 %collective-permute-start.1 = (bf16[2048,256]{1,0:T(8,128)(2,1)S(1)}, bf16[2048,256]{1,0:T(8,128)(2,1)S(1)}, u32[]{:S(2)}, u32[]{:S(2)}) collective-permute-start(bf16[2048,256]{1,0:T(8,128)(2,1)S(1)} %slice.84), channel_id=1, source_target_pairs={{0,1},{1,0},{2,3},{3,2},{4,5},{5,4},{6,7},{7,6},{8,9},{9,8},{10,11... | collective-permute-start | bytes 3145736 | tf_op jit(solution)/shard_map/ppermute | solution.py:150
  60.0 23.1 %collective-permute-start.11 = (f32[520,384]{1,0:T(8,128)S(1)}, f32[520,384]{1,0:T(8,128)S(1)}, u32[]{:S(2)}, u32[]{:S(2)}) collective-permute-start(f32[520,384]{1,0:T(8,128)S(1)} %fusion.24), channel_id=1, source_target_pairs={{0,8},{8,0},{16,24},{24,16},{1,9},{9,1},{17,25},{25,17},{2,10},{10... | collective-permute-start | bytes 2396168 | tf_op jit(solution)/shard_map/ppermute | solution.py:179
  83.3 22.9 %collective-permute-start.12 = (f32[520,384]{1,0:T(8,128)S(1)}, f32[520,384]{1,0:T(8,128)S(1)}, u32[]{:S(2)}, u32[]{:S(2)}) collective-permute-start(f32[520,384]{1,0:T(8,128)S(1)} %select_add_fusion.1), channel_id=1, source_target_pairs={{1,3},{3,5},{5,7},{10,8},{12,10},{14,12},{17,19},{19,21},{21,23},{... | collective-permute-start | bytes 2396168 | tf_op jit(solution)/shard_map/ppermute | solution.py:132
  100.9 5.3 %collective-permute-start.19 = (f32[512,128]{1,0:T(8,128)S(1)}, f32[512,128]{1,0:T(8,128)S(1)}, u32[]{:S(2)}, u32[]{:S(2)}) collective-permute-start(f32[512,128]{1,0:T(8,128)S(1)} %get-tuple-element.33), channel_id=1, source_target_pairs={{0,8},{8,0},{16,24},{24,16},{1,9},{9,1},{17,25},{25,17},{2,10},{10... | collective-permute-start | bytes 786440 | tf_op jit(solution)/shard_map/ppermute | solution.py:179
  101.9 8.4 %collective-permute-start.6 = (f32[520,256]{1,0:T(8,128)S(1)}, f32[520,256]{1,0:T(8,128)S(1)}, u32[]{:S(2)}, u32[]{:S(2)}) collective-permute-start(f32[520,256]{1,0:T(8,128)S(1)} %fusion.31), channel_id=1, source_target_pairs={{0,8},{8,0},{16,24},{24,16},{1,9},{9,1},{17,25},{25,17},{2,10},{10... | collective-permute-start | bytes 1597448 | tf_op jit(solution)/shard_map/ppermute | solution.py:179
  102.7 17.4 %collective-permute-start.16 = (f32[520,384]{1,0:T(8,128)S(1)}, f32[520,384]{1,0:T(8,128)S(1)}, u32[]{:S(2)}, u32[]{:S(2)}) collective-permute-start(f32[520,384]{1,0:T(8,128)S(1)} %select_add_fusion), channel_id=1, source_target_pairs={{24,8},{0,16},{25,9},{1,17},{26,10},{2,18},{27,11},{3,19},{28,12},... | collective-permute-start | bytes 2396168 | tf_op jit(solution)/shard_map/ppermute | solution.py:194
  106.1 12.6 %collective-permute-start.22 = (f32[8,128]{1,0:T(8,128)S(1)}, f32[8,128]{1,0:T(8,128)S(1)}, u32[]{:S(2)}, u32[]{:S(2)}) collective-permute-start(f32[8,128]{1,0:T(8,128)S(1)} %slice_maximum_fusion), channel_id=1, source_target_pairs={{0,16},{8,24},{16,0},{24,8},{1,17},{9,25},{17,1},{25,9},{2,18},{10... | collective-permute-start | bytes 12296 | tf_op jit(solution)/shard_map/ppermute | solution.py:196
  106.3 13.9 %collective-permute-start.20 = (f32[512,128]{1,0:T(8,128)S(1)}, f32[512,128]{1,0:T(8,128)S(1)}, u32[]{:S(2)}, u32[]{:S(2)}) collective-permute-start(f32[512,128]{1,0:T(8,128)S(1)} %slice_add_fusion.2), channel_id=1, source_target_pairs={{0,1},{1,0},{2,3},{3,2},{4,5},{5,4},{6,7},{7,6},{24,25},{25,24},{2... | collective-permute-start | bytes 786440 | tf_op jit(solution)/shard_map/ppermute | solution.py:132
  109.0 11.2 %collective-permute-start.21 = (f32[512,128]{1,0:T(8,128)S(1)}, f32[512,128]{1,0:T(8,128)S(1)}, u32[]{:S(2)}, u32[]{:S(2)}) collective-permute-start(f32[512,128]{1,0:T(8,128)S(1)} %slice_add_fusion.2), channel_id=1, source_target_pairs={{16,1},{17,0},{18,3},{19,2},{20,5},{21,4},{22,7},{23,6},{8,25},{9,... | collective-permute-start | bytes 786440 | tf_op jit(solution)/shard_map/ppermute | solution.py:132
  110.4 13.4 %collective-permute-start.13 = (f32[520,256]{1,0:T(8,128)S(1)}, f32[520,256]{1,0:T(8,128)S(1)}, u32[]{:S(2)}, u32[]{:S(2)}) collective-permute-start(f32[520,256]{1,0:T(8,128)S(1)} %slice_add_fusion), channel_id=1, source_target_pairs={{0,1},{1,0},{2,3},{3,2},{4,5},{5,4},{6,7},{7,6},{24,25},{25,24},{2... | collective-permute-start | bytes 1597448 | tf_op jit(solution)/shard_map/ppermute | solution.py:132
  118.7 12.0 %collective-permute-start.14 = (f32[520,256]{1,0:T(8,128)S(1)}, f32[520,256]{1,0:T(8,128)S(1)}, u32[]{:S(2)}, u32[]{:S(2)}) collective-permute-start(f32[520,256]{1,0:T(8,128)S(1)} %slice_add_fusion), channel_id=1, source_target_pairs={{16,1},{17,0},{18,3},{19,2},{20,5},{21,4},{22,7},{23,6},{8,25},{9,... | collective-permute-start | bytes 1597448 | tf_op jit(solution)/shard_map/ppermute | solution.py:132
  120.1 10.8 %copy-start.2 = (s32[384]{0:T(512)S(1)}, s32[384]{0:T(512)}, u32[]{:S(2)}) copy-start(s32[384]{0:T(512)} %param.7) | copy-start | bytes 4612
  120.1 10.8 %copy-start.3 = (s32[384]{0:T(512)S(1)}, s32[384]{0:T(512)}, u32[]{:S(2)}) copy-start(s32[384]{0:T(512)} %param.6) | copy-start | bytes 4612

commit v3 on v2

--- a/solution.py
+++ b/solution.py
@@ -19,6 +19,9 @@
 GROUP_TILES = (2,)
 X_STAGE = False
 OWN_CALLS = 2
+DIRECT_CUTS = 2
+COPY_STEPS = 4
+COPY_VMEM = 8 * 1024 * 1024
 OWN_STEPS = 4
 OWN_VMEM = 20 * 1024 * 1024
 
@@ -36,6 +39,23 @@
 def folded_squares(block):
     wide = block.astype(jnp.float32)
     return jnp.sum((wide * wide).reshape(-1, 8, wide.shape[1]), axis=0)
+
+
+def copy_kernel(source, copy):
+    copy[...] = source[...]
+
+
+def near_copy(array):
+    rows = array.shape[0] // COPY_STEPS
+    block = pl.BlockSpec((rows, array.shape[1]), lambda i: (i, 0))
+    return pl.pallas_call(
+        copy_kernel,
+        grid=(COPY_STEPS,),
+        in_specs=[block],
+        out_specs=block,
+        out_shape=jax.ShapeDtypeStruct(array.shape, array.dtype),
+        compiler_params=pltpu.CompilerParams(vmem_limit_bytes=COPY_VMEM),
+    )(array)
 
 
 def own_kernel(share_rows, dosages, phenotypes, *refs):
@@ -145,11 +165,12 @@
     windows += [(early, sample_rows, low, high) for low, high in groups[:-1]]
     windows += [(early, end, ends[-1], peak_width), (end, sample_rows, ends[-1], peak_width)]
     held, source = [], phenotypes
+    phenotypes = near_copy(phenotypes)
     for i, (a, b, c, d) in enumerate(windows):
         piece = lax.slice(source, (a, c), (b, d))
         held.append(lax.ppermute(piece, "pos", swap))
-        if i == 0:
-            source = lax.optimization_barrier(phenotypes)
+        if i == DIRECT_CUTS - 1:
+            source = phenotypes
     first, late, right, tip = held[:EARLY_PARTS], held[EARLY_PARTS:-2], held[-2], held[-1]
     passed = [lax.ppermute(x, "pos", onward) for x in first]
 
@@ -249,14 +270,20 @@
     ]
     split = groups[0][1]
     variant_share = shares[0][share_rows : share_rows + share_rows // split].reshape(share_rows)
-    cross_share = jnp.concatenate([x[:share_rows] for x in shares], axis=1)
-
     variant_index = first_variant + jnp.arange(share_rows, dtype=jnp.int32)[:, None]
-    inside = (variant_index >= window_low[None, :]) & (variant_index <= window_high[None, :])
     factor = math.sqrt(float(sample_rows * samp_count - 2))
-    scale_terms = (variant_share[:, None] + EPS) * (peak_total[None, :] + EPS)
-    statistic = factor * cross_share / jnp.sqrt(scale_terms)
-    return jnp.where(inside, statistic, jnp.zeros_like(statistic))[None]
+
+    def statistic_of(cross_share, low, high):
+        lows, highs = window_low[None, low:high], window_high[None, low:high]
+        inside = (variant_index >= lows) & (variant_index <= highs)
+        scale_terms = (variant_share[:, None] + EPS) * (peak_total[None, low:high] + EPS)
+        statistic = factor * cross_share / jnp.sqrt(scale_terms)
+        return jnp.where(inside, statistic, jnp.zeros_like(statistic))
+
+    head = [statistic_of(x[:share_rows], *group) for x, group in zip(shares[:-1], groups)]
+    head = jnp.pad(jnp.concatenate(head, axis=1), ((0, 0), (0, peak_width - ends[-1])))
+    head = lax.optimization_barrier(head)
+    return lax.dynamic_update_slice(head, statistic_of(shares[-1][:share_rows], *groups[-1]), (0, ends[-1]))[None]
 
 
 def solution(mesh):

time: 133 us -> 126 us (0.947)
  waiting for transfers between devices: 66.5 us -> 50.7 us
  starting transfers between devices: 40.3 us -> 50 us
    ppermute x1, waiting for transfers between devices: 15.9 us -> 0.01 us  [statistics_share(): far_in = lax.ppermute(far_late, 'pos', back)]
    ppermute x5, starting transfers between devices: 9.13 us -> 18.7 us  [hop(): return lax.ppermute(array, ('samp', 'pos'), flat)]
    ppermute x4, waiting for transfers between devices: 8.85 us -> 14.5 us  [statistics_share(): passed = [lax.ppermute(x, 'pos', onward) for x in first]]
    ppermute x1, waiting for transfers between devices: 5.11 us -> 0.01 us  [statistics_share(): lax.ppermute(peak_total, 'samp', [(s, s ^ half) for s in all_samp])]
    ppermute x7, waiting for transfers between devices: 26.1 us -> 23 us  [statistics_share(): held.append(lax.ppermute(piece, 'pos', swap))]
    ppermute x4, starting transfers between devices: 15.6 us -> 12.9 us  [statistics_share(): passed = [lax.ppermute(x, 'pos', onward) for x in first]]
    ppermute x5, waiting for transfers between devices: 10.5 us -> 12.9 us  [hop(): return lax.ppermute(array, ('samp', 'pos'), flat)]
    ppermute x7, starting transfers between devices: 9.75 us -> 12.1 us  [statistics_share(): held.append(lax.ppermute(piece, 'pos', swap))]
where the time goes in v3:
time: 126 us; the launch traced here: 125 us
  waiting for transfers between devices  50.7 us (40%)
  starting transfers between devices  50 us (40%)
  matrix products  9.06 us (7%)
  Pallas kernels  6.62 us (5%)
  local copies, waits for them, and re-layouts  5.92 us (5%)
  other arithmetic  2.55 us (2%)
    ppermute x7, waiting for transfers between devices, statistics_share(): held.append(lax.ppermute(piece, 'pos', swap))  23 us
    ppermute x5, starting transfers between devices, hop(): return lax.ppermute(array, ('samp', 'pos'), flat)  18.7 us
    ppermute x4, waiting for transfers between devices, statistics_share(): passed = [lax.ppermute(x, 'pos', onward) for x in first]  14.5 us
    ppermute x5, waiting for transfers between devices, hop(): return lax.ppermute(array, ('samp', 'pos'), flat)  12.9 us
    ppermute x4, starting transfers between devices, statistics_share(): passed = [lax.ppermute(x, 'pos', onward) for x in first]  12.9 us
    ppermute x7, starting transfers between devices, statistics_share(): held.append(lax.ppermute(piece, 'pos', swap))  12.1 us
    dot_general x9, matrix products, cross_rows(): lax.dot_general(variant_panel, phenotypes, (((0,), (0,)), ((), ())), pref...  9.06 us
    pallas_call x2, Pallas kernels, own_block(): pl.pallas_call(functools.partial(own_kernel, share_rows), grid=(steps,),...  6.3 us
  transfers between devices with their start and end apart: 23, of which 10 were waited for; matrix products, arithmetic and copies ran while one was open for 10% of the time, Pallas kernels for 5%

profile of v3, /device:TPU:0, one launch (start us, length us, event | category | flops | bytes accessed | tf_op | source)
XLA Modules:
  0.0 125.2 jit_solution(2374297571739812785)
XLA Ops:
  0.0 1.3 %fusion.50 = (bf16[512,384]{1,0:T(8,128)(2,1)S(1)}, bf16[512,384]{1,0:T(8,128)(2,1)S(1)}) fusion(bf16[4096,384]{1,0:T(8,128)(2,1)} %source), kind=kLoop, calls=%fused_computation.81 | loop fusion | bytes 1572864 | tf_op jit(solution)/shard_map/slice | solution.py:170
  1.3 3.1 %collective-permute-start.2 = (bf16[512,384]{1,0:T(8,128)(2,1)S(1)}, bf16[512,384]{1,0:T(8,128)(2,1)S(1)}, u32[]{:S(2)}, u32[]{:S(2)}) collective-permute-start(bf16[512,384]{1,0:T(8,128)(2,1)S(1)} %get-tuple-element.38), channel_id=1, source_target_pairs={{0,1},{1,0},{2,3},{3,2},{4,5},{5,4},{6,7},{7,6},{8,9},{9,8},{10,11... | collective-permute-start | bytes 1179656 | tf_op jit(solution)/shard_map/ppermute | solution.py:171
  4.5 1.9 %copy-done.1 = bf16[4096,384]{1,0:T(8,128)(2,1)S(1)} copy-done((bf16[4096,384]{1,0:T(8,128)(2,1)S(1)}, bf16[4096,384]{1,0:T(8,128)(2,1)}, u32[]{:S(2)}) %copy-start.1) | copy-done | bytes 3145752
  6.7 2.0 %collective-permute-start.19 = (bf16[512,128]{1,0:T(8,128)(2,1)S(1)}, bf16[512,128]{1,0:T(8,128)(2,1)S(1)}, u32[]{:S(2)}, u32[]{:S(2)}) collective-permute-start(bf16[512,128]{1,0:T(8,128)(2,1)S(1)} %slice.123), channel_id=1, source_target_pairs={{0,1},{1,0},{2,3},{3,2},{4,5},{5,4},{6,7},{7,6},{8,9},{9,8},{10,11... | collective-permute-start | bytes 393224 | tf_op jit(solution)/shard_map/ppermute | solution.py:171
  9.0 1.9 %collective-permute-start.4 = (bf16[512,384]{1,0:T(8,128)(2,1)S(1)}, bf16[512,384]{1,0:T(8,128)(2,1)S(1)}, u32[]{:S(2)}, u32[]{:S(2)}) collective-permute-start(bf16[512,384]{1,0:T(8,128)(2,1)S(1)} %get-tuple-element.37), channel_id=1, source_target_pairs={{0,1},{1,0},{2,3},{3,2},{4,5},{5,4},{6,7},{7,6},{8,9},{9,8},{10,11... | collective-permute-start | bytes 1179656 | tf_op jit(solution)/shard_map/ppermute | solution.py:171
  10.9 3.1 %own_block.3 = (f32[520,384]{1,0:T(8,128)S(1)}, f32[520,384]{1,0:T(8,128)S(1)}, f32[16,256]{1,0:T(8,128)S(1)}) custom-call(bf16[4096,1024]{1,0:T(8,128)(2,1)S(1)} %copy-done, bf16[4096,384]{1,0:T(8,128)(2,1)S(1)} %shard_map.46.phenotypes), custom_call_target="tpu_custom_call" | custom-call | tf_op jit(solution)/shard_map/own_block/pallas_call | solution.py:100
  14.1 3.2 %own_block.2 = (f32[520,384]{1,0:T(8,128)S(1)}, f32[520,384]{1,0:T(8,128)S(1)}, f32[16,256]{1,0:T(8,128)S(1)}) custom-call(bf16[4096,1024]{1,0:T(8,128)(2,1)S(1)} %copy-done, bf16[4096,384]{1,0:T(8,128)(2,1)S(1)} %shard_map.46.phenotypes), custom_call_target="tpu_custom_call" | custom-call | tf_op jit(solution)/shard_map/own_block/pallas_call | solution.py:100
  19.2 6.4 %collective-permute-done.19 = bf16[512,128]{1,0:T(8,128)(2,1)S(1)} collective-permute-done((bf16[512,128]{1,0:T(8,128)(2,1)S(1)}, bf16[512,128]{1,0:T(8,128)(2,1)S(1)}, u32[]{:S(2)}, u32[]{:S(2)}) %collective-permute-start.19) | collective-permute-done | bytes 131104 | tf_op jit(solution)/shard_map/ppermute | solution.py:171
  25.6 1.3 %collective-permute-start = (bf16[2048,512]{1,0:T(8,128)(2,1)S(1)}, bf16[2048,512]{1,0:T(8,128)(2,1)S(1)}, u32[]{:S(2)}, u32[]{:S(2)}) collective-permute-start(bf16[2048,512]{1,0:T(8,128)(2,1)S(1)} %constant_dynamic-slice_fusion), channel_id=1, source_target_pairs={{2,0},{4,2},{6,4},{1,3},{3,5},{5,7},{10,8},{12,10},{14,12},{9,11},... | collective-permute-start | bytes 6291464 | tf_op jit(solution)/shard_map/ppermute | solution.py:178
  26.9 7.1 %collective-permute-done.5 = bf16[512,384]{1,0:T(8,128)(2,1)S(1)} collective-permute-done((bf16[512,384]{1,0:T(8,128)(2,1)S(1)}, bf16[512,384]{1,0:T(8,128)(2,1)S(1)}, u32[]{:S(2)}, u32[]{:S(2)}) %collective-permute-start.5) | collective-permute-done | bytes 393248 | tf_op jit(solution)/shard_map/ppermute | solution.py:171
  34.0 4.0 %collective-permute-start.10 = (bf16[512,384]{1,0:T(8,128)(2,1)S(1)}, bf16[512,384]{1,0:T(8,128)(2,1)S(1)}, u32[]{:S(2)}, u32[]{:S(2)}) collective-permute-start(bf16[512,384]{1,0:T(8,128)(2,1)S(1)} %collective-permute-done.5), channel_id=1, source_target_pairs={{0,2},{2,4},{4,6},{3,1},{5,3},{7,5},{8,10},{10,12},{12,14},{11,9},... | collective-permute-start | bytes 1179656 | tf_op jit(solution)/shard_map/ppermute | solution.py:175
  38.7 3.5 %collective-permute-start.7 = (bf16[512,384]{1,0:T(8,128)(2,1)S(1)}, bf16[512,384]{1,0:T(8,128)(2,1)S(1)}, u32[]{:S(2)}, u32[]{:S(2)}) collective-permute-start(bf16[512,384]{1,0:T(8,128)(2,1)S(1)} %collective-permute-done.2), channel_id=1, source_target_pairs={{0,2},{2,4},{4,6},{3,1},{5,3},{7,5},{8,10},{10,12},{12,14},{11,9},... | collective-permute-start | bytes 1179656 | tf_op jit(solution)/shard_map/ppermute | solution.py:175
  42.2 3.5 %collective-permute-start.8 = (bf16[512,384]{1,0:T(8,128)(2,1)S(1)}, bf16[512,384]{1,0:T(8,128)(2,1)S(1)}, u32[]{:S(2)}, u32[]{:S(2)}) collective-permute-start(bf16[512,384]{1,0:T(8,128)(2,1)S(1)} %collective-permute-done.3), channel_id=1, source_target_pairs={{0,2},{2,4},{4,6},{3,1},{5,3},{7,5},{8,10},{10,12},{12,14},{11,9},... | collective-permute-start | bytes 1179656 | tf_op jit(solution)/shard_map/ppermute | solution.py:175
  45.7 1.9 %collective-permute-start.9 = (bf16[512,384]{1,0:T(8,128)(2,1)S(1)}, bf16[512,384]{1,0:T(8,128)(2,1)S(1)}, u32[]{:S(2)}, u32[]{:S(2)}) collective-permute-start(bf16[512,384]{1,0:T(8,128)(2,1)S(1)} %collective-permute-done.4), channel_id=1, source_target_pairs={{0,2},{2,4},{4,6},{3,1},{5,3},{7,5},{8,10},{10,12},{12,14},{11,9},... | collective-permute-start | bytes 1179656 | tf_op jit(solution)/shard_map/ppermute | solution.py:175
  47.6 1.9 %fusion.2 = f32[512,384]{1,0:T(8,128)S(1)} fusion(bf16[4096,1024]{1,0:T(8,128)(2,1)S(1)} %copy-done, s32[]{:T(128)S(6)} %select_n.145, bf16[512,384]{1,0:T(8,128)(2,1)S(1)} %collective-permute-done.5, bf16[512,384]{1,0:T(8,128)(2,1)S(1)} %collective-permute-done.4, bf16[512,384]{1,0:T(8,128)(2,1)S(1)} %collective-permute-done.3, ...), kind=kOutput, calls=%fused_computation.2 | convolution fusion | flops 811597824 | bytes 4456452 | tf_op jit(solution)/shard_map/dot_general | solution.py:30
  50.4 5.6 %collective-permute-done.7 = bf16[512,384]{1,0:T(8,128)(2,1)S(1)} collective-permute-done((bf16[512,384]{1,0:T(8,128)(2,1)S(1)}, bf16[512,384]{1,0:T(8,128)(2,1)S(1)}, u32[]{:S(2)}, u32[]{:S(2)}) %collective-permute-start.7) | collective-permute-done | bytes 393248 | tf_op jit(solution)/shard_map/ppermute | solution.py:175
  55.9 2.4 %collective-permute-start.18 = (bf16[1536,128]{1,0:T(8,128)(2,1)S(1)}, bf16[1536,128]{1,0:T(8,128)(2,1)S(1)}, u32[]{:S(2)}, u32[]{:S(2)}) collective-permute-start(bf16[1536,128]{1,0:T(8,128)(2,1)S(1)} %slice.121), channel_id=1, source_target_pairs={{0,1},{1,0},{2,3},{3,2},{4,5},{5,4},{6,7},{7,6},{8,9},{9,8},{10,11... | collective-permute-start | bytes 1179656 | tf_op jit(solution)/shard_map/ppermute | solution.py:171
  58.4 6.0 %collective-permute-done.8 = bf16[512,384]{1,0:T(8,128)(2,1)S(1)} collective-permute-done((bf16[512,384]{1,0:T(8,128)(2,1)S(1)}, bf16[512,384]{1,0:T(8,128)(2,1)S(1)}, u32[]{:S(2)}, u32[]{:S(2)}) %collective-permute-start.8) | collective-permute-done | bytes 393248 | tf_op jit(solution)/shard_map/ppermute | solution.py:175
  64.4 2.4 %collective-permute-start.1 = (bf16[2048,256]{1,0:T(8,128)(2,1)S(1)}, bf16[2048,256]{1,0:T(8,128)(2,1)S(1)}, u32[]{:S(2)}, u32[]{:S(2)}) collective-permute-start(bf16[2048,256]{1,0:T(8,128)(2,1)S(1)} %slice.109), channel_id=1, source_target_pairs={{0,1},{1,0},{2,3},{3,2},{4,5},{5,4},{6,7},{7,6},{8,9},{9,8},{10,11... | collective-permute-start | bytes 3145736 | tf_op jit(solution)/shard_map/ppermute | solution.py:171
  66.8 2.9 %collective-permute-done.9 = bf16[512,384]{1,0:T(8,128)(2,1)S(1)} collective-permute-done((bf16[512,384]{1,0:T(8,128)(2,1)S(1)}, bf16[512,384]{1,0:T(8,128)(2,1)S(1)}, u32[]{:S(2)}, u32[]{:S(2)}) %collective-permute-start.9) | collective-permute-done | bytes 393248 | tf_op jit(solution)/shard_map/ppermute | solution.py:175
  69.7 1.5 %fusion.15 = f32[512,384]{1,0:T(8,128)S(1)} fusion(bf16[4096,1024]{1,0:T(8,128)(2,1)S(1)} %copy-done, s32[]{:T(128)S(6)} %select_n.146, bf16[512,384]{1,0:T(8,128)(2,1)S(1)} %collective-permute-done.9, bf16[512,384]{1,0:T(8,128)(2,1)S(1)} %collective-permute-done.8, bf16[512,384]{1,0:T(8,128)(2,1)S(1)} %collective-permute-done.7), kind=kOutput, calls=%fused_computation.15 | convolution fusion | flops 607518720 | bytes 3538948 | tf_op jit(solution)/shard_map/dot_general | solution.py:30
  71.8 1.6 %collective-permute-start.17 = (f32[8,128]{1,0:T(8,128)S(1)}, f32[8,128]{1,0:T(8,128)S(1)}, u32[]{:S(2)}, u32[]{:S(2)}) collective-permute-start(f32[8,128]{1,0:T(8,128)S(1)} %slice_maximum_fusion), channel_id=1, source_target_pairs={{0,16},{8,24},{16,0},{24,8},{1,17},{9,25},{17,1},{25,9},{2,18},{10... | collective-permute-start | bytes 12296 | tf_op jit(solution)/shard_map/ppermute | solution.py:217
  74.5 2.7 %collective-permute-start.16 = (f32[520,384]{1,0:T(8,128)S(1)}, f32[520,384]{1,0:T(8,128)S(1)}, u32[]{:S(2)}, u32[]{:S(2)}) collective-permute-start(f32[520,384]{1,0:T(8,128)S(1)} %select_add_fusion), channel_id=1, source_target_pairs={{24,8},{0,16},{25,9},{1,17},{26,10},{2,18},{27,11},{3,19},{28,12},... | collective-permute-start | bytes 2396168 | tf_op jit(solution)/shard_map/ppermute | solution.py:215
  77.2 9.4 %collective-permute-done.1 = bf16[2048,256]{1,0:T(8,128)(2,1)S(1)} collective-permute-done((bf16[2048,256]{1,0:T(8,128)(2,1)S(1)}, bf16[2048,256]{1,0:T(8,128)(2,1)S(1)}, u32[]{:S(2)}, u32[]{:S(2)}) %collective-permute-start.1) | collective-permute-done | bytes 1048608 | tf_op jit(solution)/shard_map/ppermute | solution.py:171
  86.6 1.4 %fusion = f32[512,256]{1,0:T(8,128)S(1)} fusion(bf16[2048,256]{1,0:T(8,128)(2,1)S(1)} %collective-permute-done.1, bf16[4096,1024]{1,0:T(8,128)(2,1)S(1)} %copy-done, s32[]{:T(128)S(6)} %select_n.145), kind=kOutput, calls=%fused_computation | convolution fusion | flops 536870912 | bytes 3670020 | tf_op jit(solution)/shard_map/dot_general | solution.py:30
  91.8 1.3 %collective-permute-start.14 = (f32[520,256]{1,0:T(8,128)S(1)}, f32[520,256]{1,0:T(8,128)S(1)}, u32[]{:S(2)}, u32[]{:S(2)}) collective-permute-start(f32[520,256]{1,0:T(8,128)S(1)} %slice_add_fusion), channel_id=1, source_target_pairs={{16,1},{17,0},{18,3},{19,2},{20,5},{21,4},{22,7},{23,6},{8,25},{9,... | collective-permute-start | bytes 1597448 | tf_op jit(solution)/shard_map/ppermute | solution.py:152
  93.1 13.5 %collective-permute-start.13 = (f32[520,256]{1,0:T(8,128)S(1)}, f32[520,256]{1,0:T(8,128)S(1)}, u32[]{:S(2)}, u32[]{:S(2)}) collective-permute-start(f32[520,256]{1,0:T(8,128)S(1)} %slice_add_fusion), channel_id=1, source_target_pairs={{0,1},{1,0},{2,3},{3,2},{4,5},{5,4},{6,7},{7,6},{24,25},{25,24},{2... | collective-permute-start | bytes 1597448 | tf_op jit(solution)/shard_map/ppermute | solution.py:152
  106.9 1.3 %collective-permute-start.22 = (f32[512,128]{1,0:T(8,128)S(1)}, f32[512,128]{1,0:T(8,128)S(1)}, u32[]{:S(2)}, u32[]{:S(2)}) collective-permute-start(f32[512,128]{1,0:T(8,128)S(1)} %slice_add_fusion.2), channel_id=1, source_target_pairs={{16,1},{17,0},{18,3},{19,2},{20,5},{21,4},{22,7},{23,6},{8,25},{9,... | collective-permute-start | bytes 786440 | tf_op jit(solution)/shard_map/ppermute | solution.py:152
  108.2 1.9 %collective-permute-start.21 = (f32[512,128]{1,0:T(8,128)S(1)}, f32[512,128]{1,0:T(8,128)S(1)}, u32[]{:S(2)}, u32[]{:S(2)}) collective-permute-start(f32[512,128]{1,0:T(8,128)S(1)} %slice_add_fusion.2), channel_id=1, source_target_pairs={{0,1},{1,0},{2,3},{3,2},{4,5},{5,4},{6,7},{7,6},{24,25},{25,24},{2... | collective-permute-start | bytes 786440 | tf_op jit(solution)/shard_map/ppermute | solution.py:152
  110.1 2.9 %collective-permute-done.14 = f32[520,256]{1,0:T(8,128)S(1)} collective-permute-done((f32[520,256]{1,0:T(8,128)S(1)}, f32[520,256]{1,0:T(8,128)S(1)}, u32[]{:S(2)}, u32[]{:S(2)}) %collective-permute-start.14) | collective-permute-done | bytes 532512 | tf_op jit(solution)/shard_map/ppermute | solution.py:152
  113.0 8.5 %collective-permute-done.13 = f32[520,256]{1,0:T(8,128)S(1)} collective-permute-done((f32[520,256]{1,0:T(8,128)S(1)}, f32[520,256]{1,0:T(8,128)S(1)}, u32[]{:S(2)}, u32[]{:S(2)}) %collective-permute-start.13) | collective-permute-done | bytes 532512 | tf_op jit(solution)/shard_map/ppermute | solution.py:152
  122.8 1.5 %collective-permute-done.21 = f32[512,128]{1,0:T(8,128)S(1)} collective-permute-done((f32[512,128]{1,0:T(8,128)S(1)}, f32[512,128]{1,0:T(8,128)S(1)}, u32[]{:S(2)}, u32[]{:S(2)}) %collective-permute-start.21) | collective-permute-done | bytes 262176 | tf_op jit(solution)/shard_map/ppermute | solution.py:152
  (70 shorter events, 11.8 us)
Async XLA Ops:
  0.0 10.9 %copy-start = (bf16[4096,1024]{1,0:T(8,128)(2,1)S(1)}, bf16[4096,1024]{1,0:T(8,128)(2,1)}, u32[]{:S(2)}) copy-start(bf16[4096,1024]{1,0:T(8,128)(2,1)} %dosages.1) | copy-start | bytes 25165828
  1.3 37.3 %collective-permute-start.2 = (bf16[512,384]{1,0:T(8,128)(2,1)S(1)}, bf16[512,384]{1,0:T(8,128)(2,1)S(1)}, u32[]{:S(2)}, u32[]{:S(2)}) collective-permute-start(bf16[512,384]{1,0:T(8,128)(2,1)S(1)} %get-tuple-element.38), channel_id=1, source_target_pairs={{0,1},{1,0},{2,3},{3,2},{4,5},{5,4},{6,7},{7,6},{8,9},{9,8},{10,11... | collective-permute-start | bytes 1179656 | tf_op jit(solution)/shard_map/ppermute | solution.py:171
  4.4 37.8 %collective-permute-start.3 = (bf16[512,384]{1,0:T(8,128)(2,1)S(1)}, bf16[512,384]{1,0:T(8,128)(2,1)S(1)}, u32[]{:S(2)}, u32[]{:S(2)}) collective-permute-start(bf16[512,384]{1,0:T(8,128)(2,1)S(1)} %get-tuple-element.39), channel_id=1, source_target_pairs={{0,1},{1,0},{2,3},{3,2},{4,5},{5,4},{6,7},{7,6},{8,9},{9,8},{10,11... | collective-permute-start | bytes 1179656 | tf_op jit(solution)/shard_map/ppermute | solution.py:171
  4.5 1.9 %copy-start.1 = (bf16[4096,384]{1,0:T(8,128)(2,1)S(1)}, bf16[4096,384]{1,0:T(8,128)(2,1)}, u32[]{:S(2)}) copy-start(bf16[4096,384]{1,0:T(8,128)(2,1)} %source) | copy-start | bytes 9437188
  6.7 18.9 %collective-permute-start.19 = (bf16[512,128]{1,0:T(8,128)(2,1)S(1)}, bf16[512,128]{1,0:T(8,128)(2,1)S(1)}, u32[]{:S(2)}, u32[]{:S(2)}) collective-permute-start(bf16[512,128]{1,0:T(8,128)(2,1)S(1)} %slice.123), channel_id=1, source_target_pairs={{0,1},{1,0},{2,3},{3,2},{4,5},{5,4},{6,7},{7,6},{8,9},{9,8},{10,11... | collective-permute-start | bytes 393224 | tf_op jit(solution)/shard_map/ppermute | solution.py:171
  8.8 25.2 %collective-permute-start.5 = (bf16[512,384]{1,0:T(8,128)(2,1)S(1)}, bf16[512,384]{1,0:T(8,128)(2,1)S(1)}, u32[]{:S(2)}, u32[]{:S(2)}) collective-permute-start(bf16[512,384]{1,0:T(8,128)(2,1)S(1)} %get-tuple-element.36), channel_id=1, source_target_pairs={{0,1},{1,0},{2,3},{3,2},{4,5},{5,4},{6,7},{7,6},{8,9},{9,8},{10,11... | collective-permute-start | bytes 1179656 | tf_op jit(solution)/shard_map/ppermute | solution.py:171
  9.0 36.7 %collective-permute-start.4 = (bf16[512,384]{1,0:T(8,128)(2,1)S(1)}, bf16[512,384]{1,0:T(8,128)(2,1)S(1)}, u32[]{:S(2)}, u32[]{:S(2)}) collective-permute-start(bf16[512,384]{1,0:T(8,128)(2,1)S(1)} %get-tuple-element.37), channel_id=1, source_target_pairs={{0,1},{1,0},{2,3},{3,2},{4,5},{5,4},{6,7},{7,6},{8,9},{9,8},{10,11... | collective-permute-start | bytes 1179656 | tf_op jit(solution)/shard_map/ppermute | solution.py:171
  18.3 0.7 copy-start.2
  18.4 0.7 copy-start.3
  25.6 63.3 %collective-permute-start = (bf16[2048,512]{1,0:T(8,128)(2,1)S(1)}, bf16[2048,512]{1,0:T(8,128)(2,1)S(1)}, u32[]{:S(2)}, u32[]{:S(2)}) collective-permute-start(bf16[2048,512]{1,0:T(8,128)(2,1)S(1)} %constant_dynamic-slice_fusion), channel_id=1, source_target_pairs={{2,0},{4,2},{6,4},{1,3},{3,5},{5,7},{10,8},{12,10},{14,12},{9,11},... | collective-permute-start | bytes 6291464 | tf_op jit(solution)/shard_map/ppermute | solution.py:178
  34.0 15.5 %collective-permute-start.10 = (bf16[512,384]{1,0:T(8,128)(2,1)S(1)}, bf16[512,384]{1,0:T(8,128)(2,1)S(1)}, u32[]{:S(2)}, u32[]{:S(2)}) collective-permute-start(bf16[512,384]{1,0:T(8,128)(2,1)S(1)} %collective-permute-done.5), channel_id=1, source_target_pairs={{0,2},{2,4},{4,6},{3,1},{5,3},{7,5},{8,10},{10,12},{12,14},{11,9},... | collective-permute-start | bytes 1179656 | tf_op jit(solution)/shard_map/ppermute | solution.py:175
  38.7 17.3 %collective-permute-start.7 = (bf16[512,384]{1,0:T(8,128)(2,1)S(1)}, bf16[512,384]{1,0:T(8,128)(2,1)S(1)}, u32[]{:S(2)}, u32[]{:S(2)}) collective-permute-start(bf16[512,384]{1,0:T(8,128)(2,1)S(1)} %collective-permute-done.2), channel_id=1, source_target_pairs={{0,2},{2,4},{4,6},{3,1},{5,3},{7,5},{8,10},{10,12},{12,14},{11,9},... | collective-permute-start | bytes 1179656 | tf_op jit(solution)/shard_map/ppermute | solution.py:175
  42.2 22.2 %collective-permute-start.8 = (bf16[512,384]{1,0:T(8,128)(2,1)S(1)}, bf16[512,384]{1,0:T(8,128)(2,1)S(1)}, u32[]{:S(2)}, u32[]{:S(2)}) collective-permute-start(bf16[512,384]{1,0:T(8,128)(2,1)S(1)} %collective-permute-done.3), channel_id=1, source_target_pairs={{0,2},{2,4},{4,6},{3,1},{5,3},{7,5},{8,10},{10,12},{12,14},{11,9},... | collective-permute-start | bytes 1179656 | tf_op jit(solution)/shard_map/ppermute | solution.py:175
  45.7 24.0 %collective-permute-start.9 = (bf16[512,384]{1,0:T(8,128)(2,1)S(1)}, bf16[512,384]{1,0:T(8,128)(2,1)S(1)}, u32[]{:S(2)}, u32[]{:S(2)}) collective-permute-start(bf16[512,384]{1,0:T(8,128)(2,1)S(1)} %collective-permute-done.4), channel_id=1, source_target_pairs={{0,2},{2,4},{4,6},{3,1},{5,3},{7,5},{8,10},{10,12},{12,14},{11,9},... | collective-permute-start | bytes 1179656 | tf_op jit(solution)/shard_map/ppermute | solution.py:175
  49.5 21.9 %collective-permute-start.15 = (f32[520,384]{1,0:T(8,128)S(1)}, f32[520,384]{1,0:T(8,128)S(1)}, u32[]{:S(2)}, u32[]{:S(2)}) collective-permute-start(f32[520,384]{1,0:T(8,128)S(1)} %broadcast_select_fusion), channel_id=1, source_target_pairs={{0,8},{8,0},{16,24},{24,16},{1,9},{9,1},{17,25},{25,17},{2,10},{10... | collective-permute-start | bytes 2396168 | tf_op jit(solution)/shard_map/ppermute | solution.py:200
  55.9 17.4 %collective-permute-start.18 = (bf16[1536,128]{1,0:T(8,128)(2,1)S(1)}, bf16[1536,128]{1,0:T(8,128)(2,1)S(1)}, u32[]{:S(2)}, u32[]{:S(2)}) collective-permute-start(bf16[1536,128]{1,0:T(8,128)(2,1)S(1)} %slice.121), channel_id=1, source_target_pairs={{0,1},{1,0},{2,3},{3,2},{4,5},{5,4},{6,7},{7,6},{8,9},{9,8},{10,11... | collective-permute-start | bytes 1179656 | tf_op jit(solution)/shard_map/ppermute | solution.py:171
  64.4 22.2 %collective-permute-start.1 = (bf16[2048,256]{1,0:T(8,128)(2,1)S(1)}, bf16[2048,256]{1,0:T(8,128)(2,1)S(1)}, u32[]{:S(2)}, u32[]{:S(2)}) collective-permute-start(bf16[2048,256]{1,0:T(8,128)(2,1)S(1)} %slice.109), channel_id=1, source_target_pairs={{0,1},{1,0},{2,3},{3,2},{4,5},{5,4},{6,7},{7,6},{8,9},{9,8},{10,11... | collective-permute-start | bytes 3145736 | tf_op jit(solution)/shard_map/ppermute | solution.py:171
  71.4 16.6 %collective-permute-start.11 = (f32[520,384]{1,0:T(8,128)S(1)}, f32[520,384]{1,0:T(8,128)S(1)}, u32[]{:S(2)}, u32[]{:S(2)}) collective-permute-start(f32[520,384]{1,0:T(8,128)S(1)} %fusion.22), channel_id=1, source_target_pairs={{0,8},{8,0},{16,24},{24,16},{1,9},{9,1},{17,25},{25,17},{2,10},{10... | collective-permute-start | bytes 2396168 | tf_op jit(solution)/shard_map/ppermute | solution.py:200
  71.8 5.4 %collective-permute-start.17 = (f32[8,128]{1,0:T(8,128)S(1)}, f32[8,128]{1,0:T(8,128)S(1)}, u32[]{:S(2)}, u32[]{:S(2)}) collective-permute-start(f32[8,128]{1,0:T(8,128)S(1)} %slice_maximum_fusion), channel_id=1, source_target_pairs={{0,16},{8,24},{16,0},{24,8},{1,17},{9,25},{17,1},{25,9},{2,18},{10... | collective-permute-start | bytes 12296 | tf_op jit(solution)/shard_map/ppermute | solution.py:217
  74.5 32.2 %collective-permute-start.16 = (f32[520,384]{1,0:T(8,128)S(1)}, f32[520,384]{1,0:T(8,128)S(1)}, u32[]{:S(2)}, u32[]{:S(2)}) collective-permute-start(f32[520,384]{1,0:T(8,128)S(1)} %select_add_fusion), channel_id=1, source_target_pairs={{24,8},{0,16},{25,9},{1,17},{26,10},{2,18},{27,11},{3,19},{28,12},... | collective-permute-start | bytes 2396168 | tf_op jit(solution)/shard_map/ppermute | solution.py:215
  88.1 3.3 %collective-permute-start.12 = (f32[520,384]{1,0:T(8,128)S(1)}, f32[520,384]{1,0:T(8,128)S(1)}, u32[]{:S(2)}, u32[]{:S(2)}) collective-permute-start(f32[520,384]{1,0:T(8,128)S(1)} %select_add_fusion.1), channel_id=1, source_target_pairs={{1,3},{3,5},{5,7},{10,8},{12,10},{14,12},{17,19},{19,21},{21,23},{... | collective-permute-start | bytes 2396168 | tf_op jit(solution)/shard_map/ppermute | solution.py:152
  89.7 2.0 %collective-permute-start.6 = (f32[520,256]{1,0:T(8,128)S(1)}, f32[520,256]{1,0:T(8,128)S(1)}, u32[]{:S(2)}, u32[]{:S(2)}) collective-permute-start(f32[520,256]{1,0:T(8,128)S(1)} %fusion.31), channel_id=1, source_target_pairs={{0,8},{8,0},{16,24},{24,16},{1,9},{9,1},{17,25},{25,17},{2,10},{10... | collective-permute-start | bytes 1597448 | tf_op jit(solution)/shard_map/ppermute | solution.py:200
  90.8 16.0 %collective-permute-start.20 = (f32[512,128]{1,0:T(8,128)S(1)}, f32[512,128]{1,0:T(8,128)S(1)}, u32[]{:S(2)}, u32[]{:S(2)}) collective-permute-start(f32[512,128]{1,0:T(8,128)S(1)} %get-tuple-element.33), channel_id=1, source_target_pairs={{0,8},{8,0},{16,24},{24,16},{1,9},{9,1},{17,25},{25,17},{2,10},{10... | collective-permute-start | bytes 786440 | tf_op jit(solution)/shard_map/ppermute | solution.py:200
  91.8 21.1 %collective-permute-start.14 = (f32[520,256]{1,0:T(8,128)S(1)}, f32[520,256]{1,0:T(8,128)S(1)}, u32[]{:S(2)}, u32[]{:S(2)}) collective-permute-start(f32[520,256]{1,0:T(8,128)S(1)} %slice_add_fusion), channel_id=1, source_target_pairs={{16,1},{17,0},{18,3},{19,2},{20,5},{21,4},{22,7},{23,6},{8,25},{9,... | collective-permute-start | bytes 1597448 | tf_op jit(solution)/shard_map/ppermute | solution.py:152
  93.1 28.4 %collective-permute-start.13 = (f32[520,256]{1,0:T(8,128)S(1)}, f32[520,256]{1,0:T(8,128)S(1)}, u32[]{:S(2)}, u32[]{:S(2)}) collective-permute-start(f32[520,256]{1,0:T(8,128)S(1)} %slice_add_fusion), channel_id=1, source_target_pairs={{0,1},{1,0},{2,3},{3,2},{4,5},{5,4},{6,7},{7,6},{24,25},{25,24},{2... | collective-permute-start | bytes 1597448 | tf_op jit(solution)/shard_map/ppermute | solution.py:152
  106.8 14.9 %slice-start = ((s32[384]{0:T(512)}), s32[256]{0:T(256)S(1)}, s32[]{:S(2)}) async-start(s32[384]{0:T(512)} %param.6), calls=%async_computation | async-start | bytes 2048 | tf_op jit(solution)/shard_map/slice | solution.py:277
  106.8 14.9 %slice-start.1 = ((s32[384]{0:T(512)}), s32[256]{0:T(256)S(1)}, s32[]{:S(2)}) async-start(s32[384]{0:T(512)} %param.7), calls=%async_computation.1 | async-start | bytes 2048 | tf_op jit(solution)/shard_map/slice | solution.py:277
  106.9 15.9 %collective-permute-start.22 = (f32[512,128]{1,0:T(8,128)S(1)}, f32[512,128]{1,0:T(8,128)S(1)}, u32[]{:S(2)}, u32[]{:S(2)}) collective-permute-start(f32[512,128]{1,0:T(8,128)S(1)} %slice_add_fusion.2), channel_id=1, source_target_pairs={{16,1},{17,0},{18,3},{19,2},{20,5},{21,4},{22,7},{23,6},{8,25},{9,... | collective-permute-start | bytes 786440 | tf_op jit(solution)/shard_map/ppermute | solution.py:152
  108.2 16.1 %collective-permute-start.21 = (f32[512,128]{1,0:T(8,128)S(1)}, f32[512,128]{1,0:T(8,128)S(1)}, u32[]{:S(2)}, u32[]{:S(2)}) collective-permute-start(f32[512,128]{1,0:T(8,128)S(1)} %slice_add_fusion.2), channel_id=1, source_target_pairs={{0,1},{1,0},{2,3},{3,2},{4,5},{5,4},{6,7},{7,6},{24,25},{25,24},{2... | collective-permute-start | bytes 786440 | tf_op jit(solution)/shard_map/ppermute | solution.py:152

commit v4 on v3

--- a/solution.py
+++ b/solution.py
@@ -17,7 +17,6 @@
 EARLY_PARTS = 4
 END_SHARE = 2
 GROUP_TILES = (2,)
-X_STAGE = False
 OWN_CALLS = 2
 DIRECT_CUTS = 2
 COPY_STEPS = 4
@@ -250,11 +249,7 @@
         up_tails = [parity(x, 0.0) for x in near_tails] if g == 0 else None
         down_tails = [parity(0.0, x) for x in near_tails] if g == 0 else None
         edge = reduced(pieces_of((up, up_tails), (down, down_tails), outer_shares), low, high)
-        if X_STAGE:
-            edge = edge + lax.ppermute(edge, "samp", [(t ^ half, t) for t in outer_shares])
-            totals.append(hop(edge, straight))
-        else:
-            totals.append(hop(edge, straight) + hop(edge, across))
+        totals.append(hop(edge, straight) + hop(edge, across))
 
     low, high = groups[-1]
     near_edge = near_early[:, low:high] + cross_rows(half_rows(near_start, early, end), right)
@@ -273,17 +268,19 @@
     variant_index = first_variant + jnp.arange(share_rows, dtype=jnp.int32)[:, None]
     factor = math.sqrt(float(sample_rows * samp_count - 2))
 
-    def statistic_of(cross_share, low, high):
+    def scale_of(low, high):
+        return jnp.sqrt((variant_share[:, None] + EPS) * (peak_total[None, low:high] + EPS))
+
+    def statistic_of(cross_share, scale, low, high):
         lows, highs = window_low[None, low:high], window_high[None, low:high]
         inside = (variant_index >= lows) & (variant_index <= highs)
-        scale_terms = (variant_share[:, None] + EPS) * (peak_total[None, low:high] + EPS)
-        statistic = factor * cross_share / jnp.sqrt(scale_terms)
+        statistic = factor * cross_share / scale
         return jnp.where(inside, statistic, jnp.zeros_like(statistic))
 
-    head = [statistic_of(x[:share_rows], *group) for x, group in zip(shares[:-1], groups)]
+    head = [statistic_of(x[:share_rows], scale_of(*group), *group) for x, group in zip(shares[:-1], groups)]
     head = jnp.pad(jnp.concatenate(head, axis=1), ((0, 0), (0, peak_width - ends[-1])))
-    head = lax.optimization_barrier(head)
-    return lax.dynamic_update_slice(head, statistic_of(shares[-1][:share_rows], *groups[-1]), (0, ends[-1]))[None]
+    head, scale = lax.optimization_barrier((head, scale_of(*groups[-1])))
+    return lax.dynamic_update_slice(head, statistic_of(shares[-1][:share_rows], scale, *groups[-1]), (0, ends[-1]))[None]
 
 
 def solution(mesh):

time: 126 us -> 126 us (level)
  no operation moved by 1% of the time
where the time goes in v4:
time: 126 us; the launch traced here: 125 us
  waiting for transfers between devices  50.5 us (40%)
  starting transfers between devices  50 us (40%)
  matrix products  9.06 us (7%)
  Pallas kernels  6.62 us (5%)
  local copies, waits for them, and re-layouts  5.92 us (5%)
  other arithmetic  2.64 us (2%)
    ppermute x7, waiting for transfers between devices, statistics_share(): held.append(lax.ppermute(piece, 'pos', swap))  23 us
    ppermute x5, starting transfers between devices, hop(): return lax.ppermute(array, ('samp', 'pos'), flat)  18.7 us
    ppermute x4, waiting for transfers between devices, statistics_share(): passed = [lax.ppermute(x, 'pos', onward) for x in first]  14.5 us
    ppermute x4, starting transfers between devices, statistics_share(): passed = [lax.ppermute(x, 'pos', onward) for x in first]  12.9 us
    ppermute x5, waiting for transfers between devices, hop(): return lax.ppermute(array, ('samp', 'pos'), flat)  12.7 us
    ppermute x7, starting transfers between devices, statistics_share(): held.append(lax.ppermute(piece, 'pos', swap))  12.1 us
    dot_general x9, matrix products, cross_rows(): lax.dot_general(variant_panel, phenotypes, (((0,), (0,)), ((), ())), pref...  9.06 us
    pallas_call x2, Pallas kernels, own_block(): pl.pallas_call(functools.partial(own_kernel, share_rows), grid=(steps,),...  6.3 us
  transfers between devices with their start and end apart: 23, of which 10 were waited for; matrix products, arithmetic and copies ran while one was open for 10% of the time, Pallas kernels for 5%

profile of v4, /device:TPU:0, one launch (start us, length us, event | category | flops | bytes accessed | tf_op | source)
XLA Modules:
  0.0 125.2 jit_solution(15164621951856363879)
XLA Ops:
  0.0 1.3 %fusion.50 = (bf16[512,384]{1,0:T(8,128)(2,1)S(1)}, bf16[512,384]{1,0:T(8,128)(2,1)S(1)}) fusion(bf16[4096,384]{1,0:T(8,128)(2,1)} %source), kind=kLoop, calls=%fused_computation.82 | loop fusion | bytes 1572864 | tf_op jit(solution)/shard_map/slice | solution.py:169
  1.3 3.1 %collective-permute-start.2 = (bf16[512,384]{1,0:T(8,128)(2,1)S(1)}, bf16[512,384]{1,0:T(8,128)(2,1)S(1)}, u32[]{:S(2)}, u32[]{:S(2)}) collective-permute-start(bf16[512,384]{1,0:T(8,128)(2,1)S(1)} %get-tuple-element.42), channel_id=1, source_target_pairs={{0,1},{1,0},{2,3},{3,2},{4,5},{5,4},{6,7},{7,6},{8,9},{9,8},{10,11... | collective-permute-start | bytes 1179656 | tf_op jit(solution)/shard_map/ppermute | solution.py:170
  4.5 1.9 %copy-done.1 = bf16[4096,384]{1,0:T(8,128)(2,1)S(1)} copy-done((bf16[4096,384]{1,0:T(8,128)(2,1)S(1)}, bf16[4096,384]{1,0:T(8,128)(2,1)}, u32[]{:S(2)}) %copy-start.1) | copy-done | bytes 3145752
  6.7 2.0 %collective-permute-start.19 = (bf16[512,128]{1,0:T(8,128)(2,1)S(1)}, bf16[512,128]{1,0:T(8,128)(2,1)S(1)}, u32[]{:S(2)}, u32[]{:S(2)}) collective-permute-start(bf16[512,128]{1,0:T(8,128)(2,1)S(1)} %slice.123), channel_id=1, source_target_pairs={{0,1},{1,0},{2,3},{3,2},{4,5},{5,4},{6,7},{7,6},{8,9},{9,8},{10,11... | collective-permute-start | bytes 393224 | tf_op jit(solution)/shard_map/ppermute | solution.py:170
  9.0 1.9 %collective-permute-start.4 = (bf16[512,384]{1,0:T(8,128)(2,1)S(1)}, bf16[512,384]{1,0:T(8,128)(2,1)S(1)}, u32[]{:S(2)}, u32[]{:S(2)}) collective-permute-start(bf16[512,384]{1,0:T(8,128)(2,1)S(1)} %get-tuple-element.41), channel_id=1, source_target_pairs={{0,1},{1,0},{2,3},{3,2},{4,5},{5,4},{6,7},{7,6},{8,9},{9,8},{10,11... | collective-permute-start | bytes 1179656 | tf_op jit(solution)/shard_map/ppermute | solution.py:170
  10.9 3.1 %own_block.3 = (f32[520,384]{1,0:T(8,128)S(1)}, f32[520,384]{1,0:T(8,128)S(1)}, f32[16,256]{1,0:T(8,128)S(1)}) custom-call(bf16[4096,1024]{1,0:T(8,128)(2,1)S(1)} %copy-done, bf16[4096,384]{1,0:T(8,128)(2,1)S(1)} %shard_map.46.phenotypes), custom_call_target="tpu_custom_call" | custom-call | tf_op jit(solution)/shard_map/own_block/pallas_call | solution.py:99
  14.1 3.2 %own_block.2 = (f32[520,384]{1,0:T(8,128)S(1)}, f32[520,384]{1,0:T(8,128)S(1)}, f32[16,256]{1,0:T(8,128)S(1)}) custom-call(bf16[4096,1024]{1,0:T(8,128)(2,1)S(1)} %copy-done, bf16[4096,384]{1,0:T(8,128)(2,1)S(1)} %shard_map.46.phenotypes), custom_call_target="tpu_custom_call" | custom-call | tf_op jit(solution)/shard_map/own_block/pallas_call | solution.py:99
  19.2 6.4 %collective-permute-done.19 = bf16[512,128]{1,0:T(8,128)(2,1)S(1)} collective-permute-done((bf16[512,128]{1,0:T(8,128)(2,1)S(1)}, bf16[512,128]{1,0:T(8,128)(2,1)S(1)}, u32[]{:S(2)}, u32[]{:S(2)}) %collective-permute-start.19) | collective-permute-done | bytes 131104 | tf_op jit(solution)/shard_map/ppermute | solution.py:170
  25.6 1.3 %collective-permute-start = (bf16[2048,512]{1,0:T(8,128)(2,1)S(1)}, bf16[2048,512]{1,0:T(8,128)(2,1)S(1)}, u32[]{:S(2)}, u32[]{:S(2)}) collective-permute-start(bf16[2048,512]{1,0:T(8,128)(2,1)S(1)} %constant_dynamic-slice_fusion), channel_id=1, source_target_pairs={{2,0},{4,2},{6,4},{1,3},{3,5},{5,7},{10,8},{12,10},{14,12},{9,11},... | collective-permute-start | bytes 6291464 | tf_op jit(solution)/shard_map/ppermute | solution.py:177
  26.9 7.1 %collective-permute-done.5 = bf16[512,384]{1,0:T(8,128)(2,1)S(1)} collective-permute-done((bf16[512,384]{1,0:T(8,128)(2,1)S(1)}, bf16[512,384]{1,0:T(8,128)(2,1)S(1)}, u32[]{:S(2)}, u32[]{:S(2)}) %collective-permute-start.5) | collective-permute-done | bytes 393248 | tf_op jit(solution)/shard_map/ppermute | solution.py:170
  34.0 4.0 %collective-permute-start.10 = (bf16[512,384]{1,0:T(8,128)(2,1)S(1)}, bf16[512,384]{1,0:T(8,128)(2,1)S(1)}, u32[]{:S(2)}, u32[]{:S(2)}) collective-permute-start(bf16[512,384]{1,0:T(8,128)(2,1)S(1)} %collective-permute-done.5), channel_id=1, source_target_pairs={{0,2},{2,4},{4,6},{3,1},{5,3},{7,5},{8,10},{10,12},{12,14},{11,9},... | collective-permute-start | bytes 1179656 | tf_op jit(solution)/shard_map/ppermute | solution.py:174
  38.7 3.5 %collective-permute-start.7 = (bf16[512,384]{1,0:T(8,128)(2,1)S(1)}, bf16[512,384]{1,0:T(8,128)(2,1)S(1)}, u32[]{:S(2)}, u32[]{:S(2)}) collective-permute-start(bf16[512,384]{1,0:T(8,128)(2,1)S(1)} %collective-permute-done.2), channel_id=1, source_target_pairs={{0,2},{2,4},{4,6},{3,1},{5,3},{7,5},{8,10},{10,12},{12,14},{11,9},... | collective-permute-start | bytes 1179656 | tf_op jit(solution)/shard_map/ppermute | solution.py:174
  42.2 3.5 %collective-permute-start.8 = (bf16[512,384]{1,0:T(8,128)(2,1)S(1)}, bf16[512,384]{1,0:T(8,128)(2,1)S(1)}, u32[]{:S(2)}, u32[]{:S(2)}) collective-permute-start(bf16[512,384]{1,0:T(8,128)(2,1)S(1)} %collective-permute-done.3), channel_id=1, source_target_pairs={{0,2},{2,4},{4,6},{3,1},{5,3},{7,5},{8,10},{10,12},{12,14},{11,9},... | collective-permute-start | bytes 1179656 | tf_op jit(solution)/shard_map/ppermute | solution.py:174
  45.7 1.9 %collective-permute-start.9 = (bf16[512,384]{1,0:T(8,128)(2,1)S(1)}, bf16[512,384]{1,0:T(8,128)(2,1)S(1)}, u32[]{:S(2)}, u32[]{:S(2)}) collective-permute-start(bf16[512,384]{1,0:T(8,128)(2,1)S(1)} %collective-permute-done.4), channel_id=1, source_target_pairs={{0,2},{2,4},{4,6},{3,1},{5,3},{7,5},{8,10},{10,12},{12,14},{11,9},... | collective-permute-start | bytes 1179656 | tf_op jit(solution)/shard_map/ppermute | solution.py:174
  47.6 1.9 %fusion.2 = f32[512,384]{1,0:T(8,128)S(1)} fusion(bf16[4096,1024]{1,0:T(8,128)(2,1)S(1)} %copy-done, s32[]{:T(128)S(6)} %select_n.145, bf16[512,384]{1,0:T(8,128)(2,1)S(1)} %collective-permute-done.5, bf16[512,384]{1,0:T(8,128)(2,1)S(1)} %collective-permute-done.4, bf16[512,384]{1,0:T(8,128)(2,1)S(1)} %collective-permute-done.3, ...), kind=kOutput, calls=%fused_computation.2 | convolution fusion | flops 811597824 | bytes 4456452 | tf_op jit(solution)/shard_map/dot_general | solution.py:29
  50.4 5.6 %collective-permute-done.7 = bf16[512,384]{1,0:T(8,128)(2,1)S(1)} collective-permute-done((bf16[512,384]{1,0:T(8,128)(2,1)S(1)}, bf16[512,384]{1,0:T(8,128)(2,1)S(1)}, u32[]{:S(2)}, u32[]{:S(2)}) %collective-permute-start.7) | collective-permute-done | bytes 393248 | tf_op jit(solution)/shard_map/ppermute | solution.py:174
  55.9 2.4 %collective-permute-start.18 = (bf16[1536,128]{1,0:T(8,128)(2,1)S(1)}, bf16[1536,128]{1,0:T(8,128)(2,1)S(1)}, u32[]{:S(2)}, u32[]{:S(2)}) collective-permute-start(bf16[1536,128]{1,0:T(8,128)(2,1)S(1)} %slice.121), channel_id=1, source_target_pairs={{0,1},{1,0},{2,3},{3,2},{4,5},{5,4},{6,7},{7,6},{8,9},{9,8},{10,11... | collective-permute-start | bytes 1179656 | tf_op jit(solution)/shard_map/ppermute | solution.py:170
  58.4 6.0 %collective-permute-done.8 = bf16[512,384]{1,0:T(8,128)(2,1)S(1)} collective-permute-done((bf16[512,384]{1,0:T(8,128)(2,1)S(1)}, bf16[512,384]{1,0:T(8,128)(2,1)S(1)}, u32[]{:S(2)}, u32[]{:S(2)}) %collective-permute-start.8) | collective-permute-done | bytes 393248 | tf_op jit(solution)/shard_map/ppermute | solution.py:174
  64.4 2.4 %collective-permute-start.1 = (bf16[2048,256]{1,0:T(8,128)(2,1)S(1)}, bf16[2048,256]{1,0:T(8,128)(2,1)S(1)}, u32[]{:S(2)}, u32[]{:S(2)}) collective-permute-start(bf16[2048,256]{1,0:T(8,128)(2,1)S(1)} %slice.109), channel_id=1, source_target_pairs={{0,1},{1,0},{2,3},{3,2},{4,5},{5,4},{6,7},{7,6},{8,9},{9,8},{10,11... | collective-permute-start | bytes 3145736 | tf_op jit(solution)/shard_map/ppermute | solution.py:170
  66.8 2.9 %collective-permute-done.9 = bf16[512,384]{1,0:T(8,128)(2,1)S(1)} collective-permute-done((bf16[512,384]{1,0:T(8,128)(2,1)S(1)}, bf16[512,384]{1,0:T(8,128)(2,1)S(1)}, u32[]{:S(2)}, u32[]{:S(2)}) %collective-permute-start.9) | collective-permute-done | bytes 393248 | tf_op jit(solution)/shard_map/ppermute | solution.py:174
  69.7 1.5 %fusion.15 = f32[512,384]{1,0:T(8,128)S(1)} fusion(bf16[4096,1024]{1,0:T(8,128)(2,1)S(1)} %copy-done, s32[]{:T(128)S(6)} %select_n.146, bf16[512,384]{1,0:T(8,128)(2,1)S(1)} %collective-permute-done.9, bf16[512,384]{1,0:T(8,128)(2,1)S(1)} %collective-permute-done.8, bf16[512,384]{1,0:T(8,128)(2,1)S(1)} %collective-permute-done.7), kind=kOutput, calls=%fused_computation.15 | convolution fusion | flops 607518720 | bytes 3538948 | tf_op jit(solution)/shard_map/dot_general | solution.py:29
  71.8 1.6 %collective-permute-start.17 = (f32[8,128]{1,0:T(8,128)S(1)}, f32[8,128]{1,0:T(8,128)S(1)}, u32[]{:S(2)}, u32[]{:S(2)}) collective-permute-start(f32[8,128]{1,0:T(8,128)S(1)} %slice_maximum_fusion), channel_id=1, source_target_pairs={{0,16},{8,24},{16,0},{24,8},{1,17},{9,25},{17,1},{25,9},{2,18},{10... | collective-permute-start | bytes 12296 | tf_op jit(solution)/shard_map/ppermute | solution.py:216
  74.5 2.7 %collective-permute-start.16 = (f32[520,384]{1,0:T(8,128)S(1)}, f32[520,384]{1,0:T(8,128)S(1)}, u32[]{:S(2)}, u32[]{:S(2)}) collective-permute-start(f32[520,384]{1,0:T(8,128)S(1)} %select_add_fusion), channel_id=1, source_target_pairs={{24,8},{0,16},{25,9},{1,17},{26,10},{2,18},{27,11},{3,19},{28,12},... | collective-permute-start | bytes 2396168 | tf_op jit(solution)/shard_map/ppermute | solution.py:214
  77.2 9.4 %collective-permute-done.1 = bf16[2048,256]{1,0:T(8,128)(2,1)S(1)} collective-permute-done((bf16[2048,256]{1,0:T(8,128)(2,1)S(1)}, bf16[2048,256]{1,0:T(8,128)(2,1)S(1)}, u32[]{:S(2)}, u32[]{:S(2)}) %collective-permute-start.1) | collective-permute-done | bytes 1048608 | tf_op jit(solution)/shard_map/ppermute | solution.py:170
  86.6 1.4 %fusion = f32[512,256]{1,0:T(8,128)S(1)} fusion(bf16[2048,256]{1,0:T(8,128)(2,1)S(1)} %collective-permute-done.1, bf16[4096,1024]{1,0:T(8,128)(2,1)S(1)} %copy-done, s32[]{:T(128)S(6)} %select_n.145), kind=kOutput, calls=%fused_computation | convolution fusion | flops 536870912 | bytes 3670020 | tf_op jit(solution)/shard_map/dot_general | solution.py:29
  91.8 1.3 %collective-permute-start.14 = (f32[520,256]{1,0:T(8,128)S(1)}, f32[520,256]{1,0:T(8,128)S(1)}, u32[]{:S(2)}, u32[]{:S(2)}) collective-permute-start(f32[520,256]{1,0:T(8,128)S(1)} %slice_add_fusion), channel_id=1, source_target_pairs={{16,1},{17,0},{18,3},{19,2},{20,5},{21,4},{22,7},{23,6},{8,25},{9,... | collective-permute-start | bytes 1597448 | tf_op jit(solution)/shard_map/ppermute | solution.py:151
  93.1 13.5 %collective-permute-start.13 = (f32[520,256]{1,0:T(8,128)S(1)}, f32[520,256]{1,0:T(8,128)S(1)}, u32[]{:S(2)}, u32[]{:S(2)}) collective-permute-start(f32[520,256]{1,0:T(8,128)S(1)} %slice_add_fusion), channel_id=1, source_target_pairs={{0,1},{1,0},{2,3},{3,2},{4,5},{5,4},{6,7},{7,6},{24,25},{25,24},{2... | collective-permute-start | bytes 1597448 | tf_op jit(solution)/shard_map/ppermute | solution.py:151
  106.9 1.3 %collective-permute-start.22 = (f32[512,128]{1,0:T(8,128)S(1)}, f32[512,128]{1,0:T(8,128)S(1)}, u32[]{:S(2)}, u32[]{:S(2)}) collective-permute-start(f32[512,128]{1,0:T(8,128)S(1)} %slice_add_fusion.2), channel_id=1, source_target_pairs={{16,1},{17,0},{18,3},{19,2},{20,5},{21,4},{22,7},{23,6},{8,25},{9,... | collective-permute-start | bytes 786440 | tf_op jit(solution)/shard_map/ppermute | solution.py:151
  108.2 1.9 %collective-permute-start.21 = (f32[512,128]{1,0:T(8,128)S(1)}, f32[512,128]{1,0:T(8,128)S(1)}, u32[]{:S(2)}, u32[]{:S(2)}) collective-permute-start(f32[512,128]{1,0:T(8,128)S(1)} %slice_add_fusion.2), channel_id=1, source_target_pairs={{0,1},{1,0},{2,3},{3,2},{4,5},{5,4},{6,7},{7,6},{24,25},{25,24},{2... | collective-permute-start | bytes 786440 | tf_op jit(solution)/shard_map/ppermute | solution.py:151
  110.1 2.9 %collective-permute-done.14 = f32[520,256]{1,0:T(8,128)S(1)} collective-permute-done((f32[520,256]{1,0:T(8,128)S(1)}, f32[520,256]{1,0:T(8,128)S(1)}, u32[]{:S(2)}, u32[]{:S(2)}) %collective-permute-start.14) | collective-permute-done | bytes 532512 | tf_op jit(solution)/shard_map/ppermute | solution.py:151
  113.0 8.5 %collective-permute-done.13 = f32[520,256]{1,0:T(8,128)S(1)} collective-permute-done((f32[520,256]{1,0:T(8,128)S(1)}, f32[520,256]{1,0:T(8,128)S(1)}, u32[]{:S(2)}, u32[]{:S(2)}) %collective-permute-start.13) | collective-permute-done | bytes 532512 | tf_op jit(solution)/shard_map/ppermute | solution.py:151
  123.0 1.3 %collective-permute-done.21 = f32[512,128]{1,0:T(8,128)S(1)} collective-permute-done((f32[512,128]{1,0:T(8,128)S(1)}, f32[512,128]{1,0:T(8,128)S(1)}, u32[]{:S(2)}, u32[]{:S(2)}) %collective-permute-start.21) | collective-permute-done | bytes 262176 | tf_op jit(solution)/shard_map/ppermute | solution.py:151
  (71 shorter events, 11.8 us)
Async XLA Ops:
  0.0 10.9 %copy-start = (bf16[4096,1024]{1,0:T(8,128)(2,1)S(1)}, bf16[4096,1024]{1,0:T(8,128)(2,1)}, u32[]{:S(2)}) copy-start(bf16[4096,1024]{1,0:T(8,128)(2,1)} %dosages.1) | copy-start | bytes 25165828
  1.3 37.3 %collective-permute-start.2 = (bf16[512,384]{1,0:T(8,128)(2,1)S(1)}, bf16[512,384]{1,0:T(8,128)(2,1)S(1)}, u32[]{:S(2)}, u32[]{:S(2)}) collective-permute-start(bf16[512,384]{1,0:T(8,128)(2,1)S(1)} %get-tuple-element.42), channel_id=1, source_target_pairs={{0,1},{1,0},{2,3},{3,2},{4,5},{5,4},{6,7},{7,6},{8,9},{9,8},{10,11... | collective-permute-start | bytes 1179656 | tf_op jit(solution)/shard_map/ppermute | solution.py:170
  4.4 37.8 %collective-permute-start.3 = (bf16[512,384]{1,0:T(8,128)(2,1)S(1)}, bf16[512,384]{1,0:T(8,128)(2,1)S(1)}, u32[]{:S(2)}, u32[]{:S(2)}) collective-permute-start(bf16[512,384]{1,0:T(8,128)(2,1)S(1)} %get-tuple-element.43), channel_id=1, source_target_pairs={{0,1},{1,0},{2,3},{3,2},{4,5},{5,4},{6,7},{7,6},{8,9},{9,8},{10,11... | collective-permute-start | bytes 1179656 | tf_op jit(solution)/shard_map/ppermute | solution.py:170
  4.5 1.9 %copy-start.1 = (bf16[4096,384]{1,0:T(8,128)(2,1)S(1)}, bf16[4096,384]{1,0:T(8,128)(2,1)}, u32[]{:S(2)}) copy-start(bf16[4096,384]{1,0:T(8,128)(2,1)} %source) | copy-start | bytes 9437188
  6.7 18.9 %collective-permute-start.19 = (bf16[512,128]{1,0:T(8,128)(2,1)S(1)}, bf16[512,128]{1,0:T(8,128)(2,1)S(1)}, u32[]{:S(2)}, u32[]{:S(2)}) collective-permute-start(bf16[512,128]{1,0:T(8,128)(2,1)S(1)} %slice.123), channel_id=1, source_target_pairs={{0,1},{1,0},{2,3},{3,2},{4,5},{5,4},{6,7},{7,6},{8,9},{9,8},{10,11... | collective-permute-start | bytes 393224 | tf_op jit(solution)/shard_map/ppermute | solution.py:170
  8.8 25.2 %collective-permute-start.5 = (bf16[512,384]{1,0:T(8,128)(2,1)S(1)}, bf16[512,384]{1,0:T(8,128)(2,1)S(1)}, u32[]{:S(2)}, u32[]{:S(2)}) collective-permute-start(bf16[512,384]{1,0:T(8,128)(2,1)S(1)} %get-tuple-element.40), channel_id=1, source_target_pairs={{0,1},{1,0},{2,3},{3,2},{4,5},{5,4},{6,7},{7,6},{8,9},{9,8},{10,11... | collective-permute-start | bytes 1179656 | tf_op jit(solution)/shard_map/ppermute | solution.py:170
  9.0 36.7 %collective-permute-start.4 = (bf16[512,384]{1,0:T(8,128)(2,1)S(1)}, bf16[512,384]{1,0:T(8,128)(2,1)S(1)}, u32[]{:S(2)}, u32[]{:S(2)}) collective-permute-start(bf16[512,384]{1,0:T(8,128)(2,1)S(1)} %get-tuple-element.41), channel_id=1, source_target_pairs={{0,1},{1,0},{2,3},{3,2},{4,5},{5,4},{6,7},{7,6},{8,9},{9,8},{10,11... | collective-permute-start | bytes 1179656 | tf_op jit(solution)/shard_map/ppermute | solution.py:170
  18.3 0.7 copy-start.2
  18.4 0.7 copy-start.3
  25.6 63.3 %collective-permute-start = (bf16[2048,512]{1,0:T(8,128)(2,1)S(1)}, bf16[2048,512]{1,0:T(8,128)(2,1)S(1)}, u32[]{:S(2)}, u32[]{:S(2)}) collective-permute-start(bf16[2048,512]{1,0:T(8,128)(2,1)S(1)} %constant_dynamic-slice_fusion), channel_id=1, source_target_pairs={{2,0},{4,2},{6,4},{1,3},{3,5},{5,7},{10,8},{12,10},{14,12},{9,11},... | collective-permute-start | bytes 6291464 | tf_op jit(solution)/shard_map/ppermute | solution.py:177
  34.0 15.5 %collective-permute-start.10 = (bf16[512,384]{1,0:T(8,128)(2,1)S(1)}, bf16[512,384]{1,0:T(8,128)(2,1)S(1)}, u32[]{:S(2)}, u32[]{:S(2)}) collective-permute-start(bf16[512,384]{1,0:T(8,128)(2,1)S(1)} %collective-permute-done.5), channel_id=1, source_target_pairs={{0,2},{2,4},{4,6},{3,1},{5,3},{7,5},{8,10},{10,12},{12,14},{11,9},... | collective-permute-start | bytes 1179656 | tf_op jit(solution)/shard_map/ppermute | solution.py:174
  38.7 17.3 %collective-permute-start.7 = (bf16[512,384]{1,0:T(8,128)(2,1)S(1)}, bf16[512,384]{1,0:T(8,128)(2,1)S(1)}, u32[]{:S(2)}, u32[]{:S(2)}) collective-permute-start(bf16[512,384]{1,0:T(8,128)(2,1)S(1)} %collective-permute-done.2), channel_id=1, source_target_pairs={{0,2},{2,4},{4,6},{3,1},{5,3},{7,5},{8,10},{10,12},{12,14},{11,9},... | collective-permute-start | bytes 1179656 | tf_op jit(solution)/shard_map/ppermute | solution.py:174
  42.2 22.2 %collective-permute-start.8 = (bf16[512,384]{1,0:T(8,128)(2,1)S(1)}, bf16[512,384]{1,0:T(8,128)(2,1)S(1)}, u32[]{:S(2)}, u32[]{:S(2)}) collective-permute-start(bf16[512,384]{1,0:T(8,128)(2,1)S(1)} %collective-permute-done.3), channel_id=1, source_target_pairs={{0,2},{2,4},{4,6},{3,1},{5,3},{7,5},{8,10},{10,12},{12,14},{11,9},... | collective-permute-start | bytes 1179656 | tf_op jit(solution)/shard_map/ppermute | solution.py:174
  45.7 24.0 %collective-permute-start.9 = (bf16[512,384]{1,0:T(8,128)(2,1)S(1)}, bf16[512,384]{1,0:T(8,128)(2,1)S(1)}, u32[]{:S(2)}, u32[]{:S(2)}) collective-permute-start(bf16[512,384]{1,0:T(8,128)(2,1)S(1)} %collective-permute-done.4), channel_id=1, source_target_pairs={{0,2},{2,4},{4,6},{3,1},{5,3},{7,5},{8,10},{10,12},{12,14},{11,9},... | collective-permute-start | bytes 1179656 | tf_op jit(solution)/shard_map/ppermute | solution.py:174
  49.5 21.9 %collective-permute-start.15 = (f32[520,384]{1,0:T(8,128)S(1)}, f32[520,384]{1,0:T(8,128)S(1)}, u32[]{:S(2)}, u32[]{:S(2)}) collective-permute-start(f32[520,384]{1,0:T(8,128)S(1)} %broadcast_select_fusion), channel_id=1, source_target_pairs={{0,8},{8,0},{16,24},{24,16},{1,9},{9,1},{17,25},{25,17},{2,10},{10... | collective-permute-start | bytes 2396168 | tf_op jit(solution)/shard_map/ppermute | solution.py:199
  55.9 17.4 %collective-permute-start.18 = (bf16[1536,128]{1,0:T(8,128)(2,1)S(1)}, bf16[1536,128]{1,0:T(8,128)(2,1)S(1)}, u32[]{:S(2)}, u32[]{:S(2)}) collective-permute-start(bf16[1536,128]{1,0:T(8,128)(2,1)S(1)} %slice.121), channel_id=1, source_target_pairs={{0,1},{1,0},{2,3},{3,2},{4,5},{5,4},{6,7},{7,6},{8,9},{9,8},{10,11... | collective-permute-start | bytes 1179656 | tf_op jit(solution)/shard_map/ppermute | solution.py:170
  64.4 22.2 %collective-permute-start.1 = (bf16[2048,256]{1,0:T(8,128)(2,1)S(1)}, bf16[2048,256]{1,0:T(8,128)(2,1)S(1)}, u32[]{:S(2)}, u32[]{:S(2)}) collective-permute-start(bf16[2048,256]{1,0:T(8,128)(2,1)S(1)} %slice.109), channel_id=1, source_target_pairs={{0,1},{1,0},{2,3},{3,2},{4,5},{5,4},{6,7},{7,6},{8,9},{9,8},{10,11... | collective-permute-start | bytes 3145736 | tf_op jit(solution)/shard_map/ppermute | solution.py:170
  71.4 16.6 %collective-permute-start.11 = (f32[520,384]{1,0:T(8,128)S(1)}, f32[520,384]{1,0:T(8,128)S(1)}, u32[]{:S(2)}, u32[]{:S(2)}) collective-permute-start(f32[520,384]{1,0:T(8,128)S(1)} %fusion.22), channel_id=1, source_target_pairs={{0,8},{8,0},{16,24},{24,16},{1,9},{9,1},{17,25},{25,17},{2,10},{10... | collective-permute-start | bytes 2396168 | tf_op jit(solution)/shard_map/ppermute | solution.py:199
  71.8 5.4 %collective-permute-start.17 = (f32[8,128]{1,0:T(8,128)S(1)}, f32[8,128]{1,0:T(8,128)S(1)}, u32[]{:S(2)}, u32[]{:S(2)}) collective-permute-start(f32[8,128]{1,0:T(8,128)S(1)} %slice_maximum_fusion), channel_id=1, source_target_pairs={{0,16},{8,24},{16,0},{24,8},{1,17},{9,25},{17,1},{25,9},{2,18},{10... | collective-permute-start | bytes 12296 | tf_op jit(solution)/shard_map/ppermute | solution.py:216
  74.5 32.2 %collective-permute-start.16 = (f32[520,384]{1,0:T(8,128)S(1)}, f32[520,384]{1,0:T(8,128)S(1)}, u32[]{:S(2)}, u32[]{:S(2)}) collective-permute-start(f32[520,384]{1,0:T(8,128)S(1)} %select_add_fusion), channel_id=1, source_target_pairs={{24,8},{0,16},{25,9},{1,17},{26,10},{2,18},{27,11},{3,19},{28,12},... | collective-permute-start | bytes 2396168 | tf_op jit(solution)/shard_map/ppermute | solution.py:214
  88.1 3.3 %collective-permute-start.12 = (f32[520,384]{1,0:T(8,128)S(1)}, f32[520,384]{1,0:T(8,128)S(1)}, u32[]{:S(2)}, u32[]{:S(2)}) collective-permute-start(f32[520,384]{1,0:T(8,128)S(1)} %select_add_fusion.1), channel_id=1, source_target_pairs={{1,3},{3,5},{5,7},{10,8},{12,10},{14,12},{17,19},{19,21},{21,23},{... | collective-permute-start | bytes 2396168 | tf_op jit(solution)/shard_map/ppermute | solution.py:151
  89.7 2.0 %collective-permute-start.6 = (f32[520,256]{1,0:T(8,128)S(1)}, f32[520,256]{1,0:T(8,128)S(1)}, u32[]{:S(2)}, u32[]{:S(2)}) collective-permute-start(f32[520,256]{1,0:T(8,128)S(1)} %fusion.31), channel_id=1, source_target_pairs={{0,8},{8,0},{16,24},{24,16},{1,9},{9,1},{17,25},{25,17},{2,10},{10... | collective-permute-start | bytes 1597448 | tf_op jit(solution)/shard_map/ppermute | solution.py:199
  90.8 16.0 %collective-permute-start.20 = (f32[512,128]{1,0:T(8,128)S(1)}, f32[512,128]{1,0:T(8,128)S(1)}, u32[]{:S(2)}, u32[]{:S(2)}) collective-permute-start(f32[512,128]{1,0:T(8,128)S(1)} %get-tuple-element.37), channel_id=1, source_target_pairs={{0,8},{8,0},{16,24},{24,16},{1,9},{9,1},{17,25},{25,17},{2,10},{10... | collective-permute-start | bytes 786440 | tf_op jit(solution)/shard_map/ppermute | solution.py:199
  91.8 21.1 %collective-permute-start.14 = (f32[520,256]{1,0:T(8,128)S(1)}, f32[520,256]{1,0:T(8,128)S(1)}, u32[]{:S(2)}, u32[]{:S(2)}) collective-permute-start(f32[520,256]{1,0:T(8,128)S(1)} %slice_add_fusion), channel_id=1, source_target_pairs={{16,1},{17,0},{18,3},{19,2},{20,5},{21,4},{22,7},{23,6},{8,25},{9,... | collective-permute-start | bytes 1597448 | tf_op jit(solution)/shard_map/ppermute | solution.py:151
  93.1 28.4 %collective-permute-start.13 = (f32[520,256]{1,0:T(8,128)S(1)}, f32[520,256]{1,0:T(8,128)S(1)}, u32[]{:S(2)}, u32[]{:S(2)}) collective-permute-start(f32[520,256]{1,0:T(8,128)S(1)} %slice_add_fusion), channel_id=1, source_target_pairs={{0,1},{1,0},{2,3},{3,2},{4,5},{5,4},{6,7},{7,6},{24,25},{25,24},{2... | collective-permute-start | bytes 1597448 | tf_op jit(solution)/shard_map/ppermute | solution.py:151
  106.8 14.9 %slice-start = ((s32[384]{0:T(512)}), s32[256]{0:T(256)S(1)}, s32[]{:S(2)}) async-start(s32[384]{0:T(512)} %param.6), calls=%async_computation | async-start | bytes 2048 | tf_op jit(solution)/shard_map/slice | solution.py:275
  106.8 14.9 %slice-start.1 = ((s32[384]{0:T(512)}), s32[256]{0:T(256)S(1)}, s32[]{:S(2)}) async-start(s32[384]{0:T(512)} %param.7), calls=%async_computation.1 | async-start | bytes 2048 | tf_op jit(solution)/shard_map/slice | solution.py:275
  106.9 16.1 %collective-permute-start.22 = (f32[512,128]{1,0:T(8,128)S(1)}, f32[512,128]{1,0:T(8,128)S(1)}, u32[]{:S(2)}, u32[]{:S(2)}) collective-permute-start(f32[512,128]{1,0:T(8,128)S(1)} %slice_add_fusion.2), channel_id=1, source_target_pairs={{16,1},{17,0},{18,3},{19,2},{20,5},{21,4},{22,7},{23,6},{8,25},{9,... | collective-permute-start | bytes 786440 | tf_op jit(solution)/shard_map/ppermute | solution.py:151
  108.2 16.1 %collective-permute-start.21 = (f32[512,128]{1,0:T(8,128)S(1)}, f32[512,128]{1,0:T(8,128)S(1)}, u32[]{:S(2)}, u32[]{:S(2)}) collective-permute-start(f32[512,128]{1,0:T(8,128)S(1)} %slice_add_fusion.2), channel_id=1, source_target_pairs={{0,1},{1,0},{2,3},{3,2},{4,5},{5,4},{6,7},{7,6},{24,25},{25,24},{2... | collective-permute-start | bytes 786440 | tf_op jit(solution)/shard_map/ppermute | solution.py:151

commit v5 on v3

--- a/solution.py
+++ b/solution.py
@@ -17,7 +17,6 @@
 EARLY_PARTS = 4
 END_SHARE = 2
 GROUP_TILES = (2,)
-X_STAGE = False
 OWN_CALLS = 2
 DIRECT_CUTS = 2
 COPY_STEPS = 4
@@ -250,11 +249,7 @@
         up_tails = [parity(x, 0.0) for x in near_tails] if g == 0 else None
         down_tails = [parity(0.0, x) for x in near_tails] if g == 0 else None
         edge = reduced(pieces_of((up, up_tails), (down, down_tails), outer_shares), low, high)
-        if X_STAGE:
-            edge = edge + lax.ppermute(edge, "samp", [(t ^ half, t) for t in outer_shares])
-            totals.append(hop(edge, straight))
-        else:
-            totals.append(hop(edge, straight) + hop(edge, across))
+        totals.append(hop(edge, straight) + hop(edge, across))
 
     low, high = groups[-1]
     near_edge = near_early[:, low:high] + cross_rows(half_rows(near_start, early, end), right)

time: 126 us -> 126 us (level)
  no operation moved by 1% of the time
where the time goes in v5:
time: 126 us; the launch traced here: 125 us
  waiting for transfers between devices  50.7 us (40%)
  starting transfers between devices  50 us (40%)
  matrix products  9.06 us (7%)
  Pallas kernels  6.62 us (5%)
  local copies, waits for them, and re-layouts  5.92 us (5%)
  other arithmetic  2.55 us (2%)
    ppermute x7, waiting for transfers between devices, statistics_share(): held.append(lax.ppermute(piece, 'pos', swap))  23 us
    ppermute x5, starting transfers between devices, hop(): return lax.ppermute(array, ('samp', 'pos'), flat)  18.7 us
    ppermute x4, waiting for transfers between devices, statistics_share(): passed = [lax.ppermute(x, 'pos', onward) for x in first]  14.5 us
    ppermute x5, waiting for transfers between devices, hop(): return lax.ppermute(array, ('samp', 'pos'), flat)  12.9 us
    ppermute x4, starting transfers between devices, statistics_share(): passed = [lax.ppermute(x, 'pos', onward) for x in first]  12.9 us
    ppermute x7, starting transfers between devices, statistics_share(): held.append(lax.ppermute(piece, 'pos', swap))  12.1 us
    dot_general x9, matrix products, cross_rows(): lax.dot_general(variant_panel, phenotypes, (((0,), (0,)), ((), ())), pref...  9.06 us
    pallas_call x2, Pallas kernels, own_block(): pl.pallas_call(functools.partial(own_kernel, share_rows), grid=(steps,),...  6.3 us
  transfers between devices with their start and end apart: 23, of which 10 were waited for; matrix products, arithmetic and copies ran while one was open for 10% of the time, Pallas kernels for 5%

profile of v5, /device:TPU:0, one launch (start us, length us, event | category | flops | bytes accessed | tf_op | source)
XLA Modules:
  0.0 125.2 jit_solution(2374297571739812785)
XLA Ops:
  0.0 1.3 %fusion.50 = (bf16[512,384]{1,0:T(8,128)(2,1)S(1)}, bf16[512,384]{1,0:T(8,128)(2,1)S(1)}) fusion(bf16[4096,384]{1,0:T(8,128)(2,1)} %source), kind=kLoop, calls=%fused_computation.81 | loop fusion | bytes 1572864 | tf_op jit(solution)/shard_map/slice | solution.py:169
  1.3 3.1 %collective-permute-start.2 = (bf16[512,384]{1,0:T(8,128)(2,1)S(1)}, bf16[512,384]{1,0:T(8,128)(2,1)S(1)}, u32[]{:S(2)}, u32[]{:S(2)}) collective-permute-start(bf16[512,384]{1,0:T(8,128)(2,1)S(1)} %get-tuple-element.38), channel_id=1, source_target_pairs={{0,1},{1,0},{2,3},{3,2},{4,5},{5,4},{6,7},{7,6},{8,9},{9,8},{10,11... | collective-permute-start | bytes 1179656 | tf_op jit(solution)/shard_map/ppermute | solution.py:170
  4.5 1.9 %copy-done.1 = bf16[4096,384]{1,0:T(8,128)(2,1)S(1)} copy-done((bf16[4096,384]{1,0:T(8,128)(2,1)S(1)}, bf16[4096,384]{1,0:T(8,128)(2,1)}, u32[]{:S(2)}) %copy-start.1) | copy-done | bytes 3145752
  6.7 2.0 %collective-permute-start.19 = (bf16[512,128]{1,0:T(8,128)(2,1)S(1)}, bf16[512,128]{1,0:T(8,128)(2,1)S(1)}, u32[]{:S(2)}, u32[]{:S(2)}) collective-permute-start(bf16[512,128]{1,0:T(8,128)(2,1)S(1)} %slice.123), channel_id=1, source_target_pairs={{0,1},{1,0},{2,3},{3,2},{4,5},{5,4},{6,7},{7,6},{8,9},{9,8},{10,11... | collective-permute-start | bytes 393224 | tf_op jit(solution)/shard_map/ppermute | solution.py:170
  9.0 1.9 %collective-permute-start.4 = (bf16[512,384]{1,0:T(8,128)(2,1)S(1)}, bf16[512,384]{1,0:T(8,128)(2,1)S(1)}, u32[]{:S(2)}, u32[]{:S(2)}) collective-permute-start(bf16[512,384]{1,0:T(8,128)(2,1)S(1)} %get-tuple-element.37), channel_id=1, source_target_pairs={{0,1},{1,0},{2,3},{3,2},{4,5},{5,4},{6,7},{7,6},{8,9},{9,8},{10,11... | collective-permute-start | bytes 1179656 | tf_op jit(solution)/shard_map/ppermute | solution.py:170
  10.9 3.1 %own_block.3 = (f32[520,384]{1,0:T(8,128)S(1)}, f32[520,384]{1,0:T(8,128)S(1)}, f32[16,256]{1,0:T(8,128)S(1)}) custom-call(bf16[4096,1024]{1,0:T(8,128)(2,1)S(1)} %copy-done, bf16[4096,384]{1,0:T(8,128)(2,1)S(1)} %shard_map.46.phenotypes), custom_call_target="tpu_custom_call" | custom-call | tf_op jit(solution)/shard_map/own_block/pallas_call | solution.py:99
  14.1 3.2 %own_block.2 = (f32[520,384]{1,0:T(8,128)S(1)}, f32[520,384]{1,0:T(8,128)S(1)}, f32[16,256]{1,0:T(8,128)S(1)}) custom-call(bf16[4096,1024]{1,0:T(8,128)(2,1)S(1)} %copy-done, bf16[4096,384]{1,0:T(8,128)(2,1)S(1)} %shard_map.46.phenotypes), custom_call_target="tpu_custom_call" | custom-call | tf_op jit(solution)/shard_map/own_block/pallas_call | solution.py:99
  19.2 6.4 %collective-permute-done.19 = bf16[512,128]{1,0:T(8,128)(2,1)S(1)} collective-permute-done((bf16[512,128]{1,0:T(8,128)(2,1)S(1)}, bf16[512,128]{1,0:T(8,128)(2,1)S(1)}, u32[]{:S(2)}, u32[]{:S(2)}) %collective-permute-start.19) | collective-permute-done | bytes 131104 | tf_op jit(solution)/shard_map/ppermute | solution.py:170
  25.6 1.3 %collective-permute-start = (bf16[2048,512]{1,0:T(8,128)(2,1)S(1)}, bf16[2048,512]{1,0:T(8,128)(2,1)S(1)}, u32[]{:S(2)}, u32[]{:S(2)}) collective-permute-start(bf16[2048,512]{1,0:T(8,128)(2,1)S(1)} %constant_dynamic-slice_fusion), channel_id=1, source_target_pairs={{2,0},{4,2},{6,4},{1,3},{3,5},{5,7},{10,8},{12,10},{14,12},{9,11},... | collective-permute-start | bytes 6291464 | tf_op jit(solution)/shard_map/ppermute | solution.py:177
  26.9 7.1 %collective-permute-done.5 = bf16[512,384]{1,0:T(8,128)(2,1)S(1)} collective-permute-done((bf16[512,384]{1,0:T(8,128)(2,1)S(1)}, bf16[512,384]{1,0:T(8,128)(2,1)S(1)}, u32[]{:S(2)}, u32[]{:S(2)}) %collective-permute-start.5) | collective-permute-done | bytes 393248 | tf_op jit(solution)/shard_map/ppermute | solution.py:170
  34.0 4.0 %collective-permute-start.10 = (bf16[512,384]{1,0:T(8,128)(2,1)S(1)}, bf16[512,384]{1,0:T(8,128)(2,1)S(1)}, u32[]{:S(2)}, u32[]{:S(2)}) collective-permute-start(bf16[512,384]{1,0:T(8,128)(2,1)S(1)} %collective-permute-done.5), channel_id=1, source_target_pairs={{0,2},{2,4},{4,6},{3,1},{5,3},{7,5},{8,10},{10,12},{12,14},{11,9},... | collective-permute-start | bytes 1179656 | tf_op jit(solution)/shard_map/ppermute | solution.py:174
  38.7 3.5 %collective-permute-start.7 = (bf16[512,384]{1,0:T(8,128)(2,1)S(1)}, bf16[512,384]{1,0:T(8,128)(2,1)S(1)}, u32[]{:S(2)}, u32[]{:S(2)}) collective-permute-start(bf16[512,384]{1,0:T(8,128)(2,1)S(1)} %collective-permute-done.2), channel_id=1, source_target_pairs={{0,2},{2,4},{4,6},{3,1},{5,3},{7,5},{8,10},{10,12},{12,14},{11,9},... | collective-permute-start | bytes 1179656 | tf_op jit(solution)/shard_map/ppermute | solution.py:174
  42.2 3.5 %collective-permute-start.8 = (bf16[512,384]{1,0:T(8,128)(2,1)S(1)}, bf16[512,384]{1,0:T(8,128)(2,1)S(1)}, u32[]{:S(2)}, u32[]{:S(2)}) collective-permute-start(bf16[512,384]{1,0:T(8,128)(2,1)S(1)} %collective-permute-done.3), channel_id=1, source_target_pairs={{0,2},{2,4},{4,6},{3,1},{5,3},{7,5},{8,10},{10,12},{12,14},{11,9},... | collective-permute-start | bytes 1179656 | tf_op jit(solution)/shard_map/ppermute | solution.py:174
  45.7 1.9 %collective-permute-start.9 = (bf16[512,384]{1,0:T(8,128)(2,1)S(1)}, bf16[512,384]{1,0:T(8,128)(2,1)S(1)}, u32[]{:S(2)}, u32[]{:S(2)}) collective-permute-start(bf16[512,384]{1,0:T(8,128)(2,1)S(1)} %collective-permute-done.4), channel_id=1, source_target_pairs={{0,2},{2,4},{4,6},{3,1},{5,3},{7,5},{8,10},{10,12},{12,14},{11,9},... | collective-permute-start | bytes 1179656 | tf_op jit(solution)/shard_map/ppermute | solution.py:174
  47.6 1.9 %fusion.2 = f32[512,384]{1,0:T(8,128)S(1)} fusion(bf16[4096,1024]{1,0:T(8,128)(2,1)S(1)} %copy-done, s32[]{:T(128)S(6)} %select_n.145, bf16[512,384]{1,0:T(8,128)(2,1)S(1)} %collective-permute-done.5, bf16[512,384]{1,0:T(8,128)(2,1)S(1)} %collective-permute-done.4, bf16[512,384]{1,0:T(8,128)(2,1)S(1)} %collective-permute-done.3, ...), kind=kOutput, calls=%fused_computation.2 | convolution fusion | flops 811597824 | bytes 4456452 | tf_op jit(solution)/shard_map/dot_general | solution.py:29
  50.4 5.6 %collective-permute-done.7 = bf16[512,384]{1,0:T(8,128)(2,1)S(1)} collective-permute-done((bf16[512,384]{1,0:T(8,128)(2,1)S(1)}, bf16[512,384]{1,0:T(8,128)(2,1)S(1)}, u32[]{:S(2)}, u32[]{:S(2)}) %collective-permute-start.7) | collective-permute-done | bytes 393248 | tf_op jit(solution)/shard_map/ppermute | solution.py:174
  55.9 2.4 %collective-permute-start.18 = (bf16[1536,128]{1,0:T(8,128)(2,1)S(1)}, bf16[1536,128]{1,0:T(8,128)(2,1)S(1)}, u32[]{:S(2)}, u32[]{:S(2)}) collective-permute-start(bf16[1536,128]{1,0:T(8,128)(2,1)S(1)} %slice.121), channel_id=1, source_target_pairs={{0,1},{1,0},{2,3},{3,2},{4,5},{5,4},{6,7},{7,6},{8,9},{9,8},{10,11... | collective-permute-start | bytes 1179656 | tf_op jit(solution)/shard_map/ppermute | solution.py:170
  58.4 6.0 %collective-permute-done.8 = bf16[512,384]{1,0:T(8,128)(2,1)S(1)} collective-permute-done((bf16[512,384]{1,0:T(8,128)(2,1)S(1)}, bf16[512,384]{1,0:T(8,128)(2,1)S(1)}, u32[]{:S(2)}, u32[]{:S(2)}) %collective-permute-start.8) | collective-permute-done | bytes 393248 | tf_op jit(solution)/shard_map/ppermute | solution.py:174
  64.4 2.4 %collective-permute-start.1 = (bf16[2048,256]{1,0:T(8,128)(2,1)S(1)}, bf16[2048,256]{1,0:T(8,128)(2,1)S(1)}, u32[]{:S(2)}, u32[]{:S(2)}) collective-permute-start(bf16[2048,256]{1,0:T(8,128)(2,1)S(1)} %slice.109), channel_id=1, source_target_pairs={{0,1},{1,0},{2,3},{3,2},{4,5},{5,4},{6,7},{7,6},{8,9},{9,8},{10,11... | collective-permute-start | bytes 3145736 | tf_op jit(solution)/shard_map/ppermute | solution.py:170
  66.8 2.9 %collective-permute-done.9 = bf16[512,384]{1,0:T(8,128)(2,1)S(1)} collective-permute-done((bf16[512,384]{1,0:T(8,128)(2,1)S(1)}, bf16[512,384]{1,0:T(8,128)(2,1)S(1)}, u32[]{:S(2)}, u32[]{:S(2)}) %collective-permute-start.9) | collective-permute-done | bytes 393248 | tf_op jit(solution)/shard_map/ppermute | solution.py:174
  69.7 1.5 %fusion.15 = f32[512,384]{1,0:T(8,128)S(1)} fusion(bf16[4096,1024]{1,0:T(8,128)(2,1)S(1)} %copy-done, s32[]{:T(128)S(6)} %select_n.146, bf16[512,384]{1,0:T(8,128)(2,1)S(1)} %collective-permute-done.9, bf16[512,384]{1,0:T(8,128)(2,1)S(1)} %collective-permute-done.8, bf16[512,384]{1,0:T(8,128)(2,1)S(1)} %collective-permute-done.7), kind=kOutput, calls=%fused_computation.15 | convolution fusion | flops 607518720 | bytes 3538948 | tf_op jit(solution)/shard_map/dot_general | solution.py:29
  71.8 1.6 %collective-permute-start.17 = (f32[8,128]{1,0:T(8,128)S(1)}, f32[8,128]{1,0:T(8,128)S(1)}, u32[]{:S(2)}, u32[]{:S(2)}) collective-permute-start(f32[8,128]{1,0:T(8,128)S(1)} %slice_maximum_fusion), channel_id=1, source_target_pairs={{0,16},{8,24},{16,0},{24,8},{1,17},{9,25},{17,1},{25,9},{2,18},{10... | collective-permute-start | bytes 12296 | tf_op jit(solution)/shard_map/ppermute | solution.py:216
  74.5 2.7 %collective-permute-start.16 = (f32[520,384]{1,0:T(8,128)S(1)}, f32[520,384]{1,0:T(8,128)S(1)}, u32[]{:S(2)}, u32[]{:S(2)}) collective-permute-start(f32[520,384]{1,0:T(8,128)S(1)} %select_add_fusion), channel_id=1, source_target_pairs={{24,8},{0,16},{25,9},{1,17},{26,10},{2,18},{27,11},{3,19},{28,12},... | collective-permute-start | bytes 2396168 | tf_op jit(solution)/shard_map/ppermute | solution.py:214
  77.2 9.4 %collective-permute-done.1 = bf16[2048,256]{1,0:T(8,128)(2,1)S(1)} collective-permute-done((bf16[2048,256]{1,0:T(8,128)(2,1)S(1)}, bf16[2048,256]{1,0:T(8,128)(2,1)S(1)}, u32[]{:S(2)}, u32[]{:S(2)}) %collective-permute-start.1) | collective-permute-done | bytes 1048608 | tf_op jit(solution)/shard_map/ppermute | solution.py:170
  86.6 1.4 %fusion = f32[512,256]{1,0:T(8,128)S(1)} fusion(bf16[2048,256]{1,0:T(8,128)(2,1)S(1)} %collective-permute-done.1, bf16[4096,1024]{1,0:T(8,128)(2,1)S(1)} %copy-done, s32[]{:T(128)S(6)} %select_n.145), kind=kOutput, calls=%fused_computation | convolution fusion | flops 536870912 | bytes 3670020 | tf_op jit(solution)/shard_map/dot_general | solution.py:29
  91.8 1.3 %collective-permute-start.14 = (f32[520,256]{1,0:T(8,128)S(1)}, f32[520,256]{1,0:T(8,128)S(1)}, u32[]{:S(2)}, u32[]{:S(2)}) collective-permute-start(f32[520,256]{1,0:T(8,128)S(1)} %slice_add_fusion), channel_id=1, source_target_pairs={{16,1},{17,0},{18,3},{19,2},{20,5},{21,4},{22,7},{23,6},{8,25},{9,... | collective-permute-start | bytes 1597448 | tf_op jit(solution)/shard_map/ppermute | solution.py:151
  93.1 13.5 %collective-permute-start.13 = (f32[520,256]{1,0:T(8,128)S(1)}, f32[520,256]{1,0:T(8,128)S(1)}, u32[]{:S(2)}, u32[]{:S(2)}) collective-permute-start(f32[520,256]{1,0:T(8,128)S(1)} %slice_add_fusion), channel_id=1, source_target_pairs={{0,1},{1,0},{2,3},{3,2},{4,5},{5,4},{6,7},{7,6},{24,25},{25,24},{2... | collective-permute-start | bytes 1597448 | tf_op jit(solution)/shard_map/ppermute | solution.py:151
  106.9 1.3 %collective-permute-start.22 = (f32[512,128]{1,0:T(8,128)S(1)}, f32[512,128]{1,0:T(8,128)S(1)}, u32[]{:S(2)}, u32[]{:S(2)}) collective-permute-start(f32[512,128]{1,0:T(8,128)S(1)} %slice_add_fusion.2), channel_id=1, source_target_pairs={{16,1},{17,0},{18,3},{19,2},{20,5},{21,4},{22,7},{23,6},{8,25},{9,... | collective-permute-start | bytes 786440 | tf_op jit(solution)/shard_map/ppermute | solution.py:151
  108.2 1.9 %collective-permute-start.21 = (f32[512,128]{1,0:T(8,128)S(1)}, f32[512,128]{1,0:T(8,128)S(1)}, u32[]{:S(2)}, u32[]{:S(2)}) collective-permute-start(f32[512,128]{1,0:T(8,128)S(1)} %slice_add_fusion.2), channel_id=1, source_target_pairs={{0,1},{1,0},{2,3},{3,2},{4,5},{5,4},{6,7},{7,6},{24,25},{25,24},{2... | collective-permute-start | bytes 786440 | tf_op jit(solution)/shard_map/ppermute | solution.py:151
  110.1 2.9 %collective-permute-done.14 = f32[520,256]{1,0:T(8,128)S(1)} collective-permute-done((f32[520,256]{1,0:T(8,128)S(1)}, f32[520,256]{1,0:T(8,128)S(1)}, u32[]{:S(2)}, u32[]{:S(2)}) %collective-permute-start.14) | collective-permute-done | bytes 532512 | tf_op jit(solution)/shard_map/ppermute | solution.py:151
  113.0 8.5 %collective-permute-done.13 = f32[520,256]{1,0:T(8,128)S(1)} collective-permute-done((f32[520,256]{1,0:T(8,128)S(1)}, f32[520,256]{1,0:T(8,128)S(1)}, u32[]{:S(2)}, u32[]{:S(2)}) %collective-permute-start.13) | collective-permute-done | bytes 532512 | tf_op jit(solution)/shard_map/ppermute | solution.py:151
  122.8 1.5 %collective-permute-done.21 = f32[512,128]{1,0:T(8,128)S(1)} collective-permute-done((f32[512,128]{1,0:T(8,128)S(1)}, f32[512,128]{1,0:T(8,128)S(1)}, u32[]{:S(2)}, u32[]{:S(2)}) %collective-permute-start.21) | collective-permute-done | bytes 262176 | tf_op jit(solution)/shard_map/ppermute | solution.py:151
  (70 shorter events, 11.8 us)
Async XLA Ops:
  0.0 10.9 %copy-start = (bf16[4096,1024]{1,0:T(8,128)(2,1)S(1)}, bf16[4096,1024]{1,0:T(8,128)(2,1)}, u32[]{:S(2)}) copy-start(bf16[4096,1024]{1,0:T(8,128)(2,1)} %dosages.1) | copy-start | bytes 25165828
  1.3 37.3 %collective-permute-start.2 = (bf16[512,384]{1,0:T(8,128)(2,1)S(1)}, bf16[512,384]{1,0:T(8,128)(2,1)S(1)}, u32[]{:S(2)}, u32[]{:S(2)}) collective-permute-start(bf16[512,384]{1,0:T(8,128)(2,1)S(1)} %get-tuple-element.38), channel_id=1, source_target_pairs={{0,1},{1,0},{2,3},{3,2},{4,5},{5,4},{6,7},{7,6},{8,9},{9,8},{10,11... | collective-permute-start | bytes 1179656 | tf_op jit(solution)/shard_map/ppermute | solution.py:170
  4.4 37.8 %collective-permute-start.3 = (bf16[512,384]{1,0:T(8,128)(2,1)S(1)}, bf16[512,384]{1,0:T(8,128)(2,1)S(1)}, u32[]{:S(2)}, u32[]{:S(2)}) collective-permute-start(bf16[512,384]{1,0:T(8,128)(2,1)S(1)} %get-tuple-element.39), channel_id=1, source_target_pairs={{0,1},{1,0},{2,3},{3,2},{4,5},{5,4},{6,7},{7,6},{8,9},{9,8},{10,11... | collective-permute-start | bytes 1179656 | tf_op jit(solution)/shard_map/ppermute | solution.py:170
  4.5 1.9 %copy-start.1 = (bf16[4096,384]{1,0:T(8,128)(2,1)S(1)}, bf16[4096,384]{1,0:T(8,128)(2,1)}, u32[]{:S(2)}) copy-start(bf16[4096,384]{1,0:T(8,128)(2,1)} %source) | copy-start | bytes 9437188
  6.7 18.9 %collective-permute-start.19 = (bf16[512,128]{1,0:T(8,128)(2,1)S(1)}, bf16[512,128]{1,0:T(8,128)(2,1)S(1)}, u32[]{:S(2)}, u32[]{:S(2)}) collective-permute-start(bf16[512,128]{1,0:T(8,128)(2,1)S(1)} %slice.123), channel_id=1, source_target_pairs={{0,1},{1,0},{2,3},{3,2},{4,5},{5,4},{6,7},{7,6},{8,9},{9,8},{10,11... | collective-permute-start | bytes 393224 | tf_op jit(solution)/shard_map/ppermute | solution.py:170
  8.8 25.2 %collective-permute-start.5 = (bf16[512,384]{1,0:T(8,128)(2,1)S(1)}, bf16[512,384]{1,0:T(8,128)(2,1)S(1)}, u32[]{:S(2)}, u32[]{:S(2)}) collective-permute-start(bf16[512,384]{1,0:T(8,128)(2,1)S(1)} %get-tuple-element.36), channel_id=1, source_target_pairs={{0,1},{1,0},{2,3},{3,2},{4,5},{5,4},{6,7},{7,6},{8,9},{9,8},{10,11... | collective-permute-start | bytes 1179656 | tf_op jit(solution)/shard_map/ppermute | solution.py:170
  9.0 36.7 %collective-permute-start.4 = (bf16[512,384]{1,0:T(8,128)(2,1)S(1)}, bf16[512,384]{1,0:T(8,128)(2,1)S(1)}, u32[]{:S(2)}, u32[]{:S(2)}) collective-permute-start(bf16[512,384]{1,0:T(8,128)(2,1)S(1)} %get-tuple-element.37), channel_id=1, source_target_pairs={{0,1},{1,0},{2,3},{3,2},{4,5},{5,4},{6,7},{7,6},{8,9},{9,8},{10,11... | collective-permute-start | bytes 1179656 | tf_op jit(solution)/shard_map/ppermute | solution.py:170
  18.3 0.7 copy-start.2
  18.4 0.7 copy-start.3
  25.6 63.3 %collective-permute-start = (bf16[2048,512]{1,0:T(8,128)(2,1)S(1)}, bf16[2048,512]{1,0:T(8,128)(2,1)S(1)}, u32[]{:S(2)}, u32[]{:S(2)}) collective-permute-start(bf16[2048,512]{1,0:T(8,128)(2,1)S(1)} %constant_dynamic-slice_fusion), channel_id=1, source_target_pairs={{2,0},{4,2},{6,4},{1,3},{3,5},{5,7},{10,8},{12,10},{14,12},{9,11},... | collective-permute-start | bytes 6291464 | tf_op jit(solution)/shard_map/ppermute | solution.py:177
  34.0 15.5 %collective-permute-start.10 = (bf16[512,384]{1,0:T(8,128)(2,1)S(1)}, bf16[512,384]{1,0:T(8,128)(2,1)S(1)}, u32[]{:S(2)}, u32[]{:S(2)}) collective-permute-start(bf16[512,384]{1,0:T(8,128)(2,1)S(1)} %collective-permute-done.5), channel_id=1, source_target_pairs={{0,2},{2,4},{4,6},{3,1},{5,3},{7,5},{8,10},{10,12},{12,14},{11,9},... | collective-permute-start | bytes 1179656 | tf_op jit(solution)/shard_map/ppermute | solution.py:174
  38.7 17.3 %collective-permute-start.7 = (bf16[512,384]{1,0:T(8,128)(2,1)S(1)}, bf16[512,384]{1,0:T(8,128)(2,1)S(1)}, u32[]{:S(2)}, u32[]{:S(2)}) collective-permute-start(bf16[512,384]{1,0:T(8,128)(2,1)S(1)} %collective-permute-done.2), channel_id=1, source_target_pairs={{0,2},{2,4},{4,6},{3,1},{5,3},{7,5},{8,10},{10,12},{12,14},{11,9},... | collective-permute-start | bytes 1179656 | tf_op jit(solution)/shard_map/ppermute | solution.py:174
  42.2 22.2 %collective-permute-start.8 = (bf16[512,384]{1,0:T(8,128)(2,1)S(1)}, bf16[512,384]{1,0:T(8,128)(2,1)S(1)}, u32[]{:S(2)}, u32[]{:S(2)}) collective-permute-start(bf16[512,384]{1,0:T(8,128)(2,1)S(1)} %collective-permute-done.3), channel_id=1, source_target_pairs={{0,2},{2,4},{4,6},{3,1},{5,3},{7,5},{8,10},{10,12},{12,14},{11,9},... | collective-permute-start | bytes 1179656 | tf_op jit(solution)/shard_map/ppermute | solution.py:174
  45.7 24.0 %collective-permute-start.9 = (bf16[512,384]{1,0:T(8,128)(2,1)S(1)}, bf16[512,384]{1,0:T(8,128)(2,1)S(1)}, u32[]{:S(2)}, u32[]{:S(2)}) collective-permute-start(bf16[512,384]{1,0:T(8,128)(2,1)S(1)} %collective-permute-done.4), channel_id=1, source_target_pairs={{0,2},{2,4},{4,6},{3,1},{5,3},{7,5},{8,10},{10,12},{12,14},{11,9},... | collective-permute-start | bytes 1179656 | tf_op jit(solution)/shard_map/ppermute | solution.py:174
  49.5 21.9 %collective-permute-start.15 = (f32[520,384]{1,0:T(8,128)S(1)}, f32[520,384]{1,0:T(8,128)S(1)}, u32[]{:S(2)}, u32[]{:S(2)}) collective-permute-start(f32[520,384]{1,0:T(8,128)S(1)} %broadcast_select_fusion), channel_id=1, source_target_pairs={{0,8},{8,0},{16,24},{24,16},{1,9},{9,1},{17,25},{25,17},{2,10},{10... | collective-permute-start | bytes 2396168 | tf_op jit(solution)/shard_map/ppermute | solution.py:199
  55.9 17.4 %collective-permute-start.18 = (bf16[1536,128]{1,0:T(8,128)(2,1)S(1)}, bf16[1536,128]{1,0:T(8,128)(2,1)S(1)}, u32[]{:S(2)}, u32[]{:S(2)}) collective-permute-start(bf16[1536,128]{1,0:T(8,128)(2,1)S(1)} %slice.121), channel_id=1, source_target_pairs={{0,1},{1,0},{2,3},{3,2},{4,5},{5,4},{6,7},{7,6},{8,9},{9,8},{10,11... | collective-permute-start | bytes 1179656 | tf_op jit(solution)/shard_map/ppermute | solution.py:170
  64.4 22.2 %collective-permute-start.1 = (bf16[2048,256]{1,0:T(8,128)(2,1)S(1)}, bf16[2048,256]{1,0:T(8,128)(2,1)S(1)}, u32[]{:S(2)}, u32[]{:S(2)}) collective-permute-start(bf16[2048,256]{1,0:T(8,128)(2,1)S(1)} %slice.109), channel_id=1, source_target_pairs={{0,1},{1,0},{2,3},{3,2},{4,5},{5,4},{6,7},{7,6},{8,9},{9,8},{10,11... | collective-permute-start | bytes 3145736 | tf_op jit(solution)/shard_map/ppermute | solution.py:170
  71.4 16.6 %collective-permute-start.11 = (f32[520,384]{1,0:T(8,128)S(1)}, f32[520,384]{1,0:T(8,128)S(1)}, u32[]{:S(2)}, u32[]{:S(2)}) collective-permute-start(f32[520,384]{1,0:T(8,128)S(1)} %fusion.22), channel_id=1, source_target_pairs={{0,8},{8,0},{16,24},{24,16},{1,9},{9,1},{17,25},{25,17},{2,10},{10... | collective-permute-start | bytes 2396168 | tf_op jit(solution)/shard_map/ppermute | solution.py:199
  71.8 5.4 %collective-permute-start.17 = (f32[8,128]{1,0:T(8,128)S(1)}, f32[8,128]{1,0:T(8,128)S(1)}, u32[]{:S(2)}, u32[]{:S(2)}) collective-permute-start(f32[8,128]{1,0:T(8,128)S(1)} %slice_maximum_fusion), channel_id=1, source_target_pairs={{0,16},{8,24},{16,0},{24,8},{1,17},{9,25},{17,1},{25,9},{2,18},{10... | collective-permute-start | bytes 12296 | tf_op jit(solution)/shard_map/ppermute | solution.py:216
  74.5 32.2 %collective-permute-start.16 = (f32[520,384]{1,0:T(8,128)S(1)}, f32[520,384]{1,0:T(8,128)S(1)}, u32[]{:S(2)}, u32[]{:S(2)}) collective-permute-start(f32[520,384]{1,0:T(8,128)S(1)} %select_add_fusion), channel_id=1, source_target_pairs={{24,8},{0,16},{25,9},{1,17},{26,10},{2,18},{27,11},{3,19},{28,12},... | collective-permute-start | bytes 2396168 | tf_op jit(solution)/shard_map/ppermute | solution.py:214
  88.1 3.3 %collective-permute-start.12 = (f32[520,384]{1,0:T(8,128)S(1)}, f32[520,384]{1,0:T(8,128)S(1)}, u32[]{:S(2)}, u32[]{:S(2)}) collective-permute-start(f32[520,384]{1,0:T(8,128)S(1)} %select_add_fusion.1), channel_id=1, source_target_pairs={{1,3},{3,5},{5,7},{10,8},{12,10},{14,12},{17,19},{19,21},{21,23},{... | collective-permute-start | bytes 2396168 | tf_op jit(solution)/shard_map/ppermute | solution.py:151
  89.7 2.0 %collective-permute-start.6 = (f32[520,256]{1,0:T(8,128)S(1)}, f32[520,256]{1,0:T(8,128)S(1)}, u32[]{:S(2)}, u32[]{:S(2)}) collective-permute-start(f32[520,256]{1,0:T(8,128)S(1)} %fusion.31), channel_id=1, source_target_pairs={{0,8},{8,0},{16,24},{24,16},{1,9},{9,1},{17,25},{25,17},{2,10},{10... | collective-permute-start | bytes 1597448 | tf_op jit(solution)/shard_map/ppermute | solution.py:199
  90.8 16.0 %collective-permute-start.20 = (f32[512,128]{1,0:T(8,128)S(1)}, f32[512,128]{1,0:T(8,128)S(1)}, u32[]{:S(2)}, u32[]{:S(2)}) collective-permute-start(f32[512,128]{1,0:T(8,128)S(1)} %get-tuple-element.33), channel_id=1, source_target_pairs={{0,8},{8,0},{16,24},{24,16},{1,9},{9,1},{17,25},{25,17},{2,10},{10... | collective-permute-start | bytes 786440 | tf_op jit(solution)/shard_map/ppermute | solution.py:199
  91.8 21.1 %collective-permute-start.14 = (f32[520,256]{1,0:T(8,128)S(1)}, f32[520,256]{1,0:T(8,128)S(1)}, u32[]{:S(2)}, u32[]{:S(2)}) collective-permute-start(f32[520,256]{1,0:T(8,128)S(1)} %slice_add_fusion), channel_id=1, source_target_pairs={{16,1},{17,0},{18,3},{19,2},{20,5},{21,4},{22,7},{23,6},{8,25},{9,... | collective-permute-start | bytes 1597448 | tf_op jit(solution)/shard_map/ppermute | solution.py:151
  93.1 28.4 %collective-permute-start.13 = (f32[520,256]{1,0:T(8,128)S(1)}, f32[520,256]{1,0:T(8,128)S(1)}, u32[]{:S(2)}, u32[]{:S(2)}) collective-permute-start(f32[520,256]{1,0:T(8,128)S(1)} %slice_add_fusion), channel_id=1, source_target_pairs={{0,1},{1,0},{2,3},{3,2},{4,5},{5,4},{6,7},{7,6},{24,25},{25,24},{2... | collective-permute-start | bytes 1597448 | tf_op jit(solution)/shard_map/ppermute | solution.py:151
  106.8 14.9 %slice-start = ((s32[384]{0:T(512)}), s32[256]{0:T(256)S(1)}, s32[]{:S(2)}) async-start(s32[384]{0:T(512)} %param.6), calls=%async_computation | async-start | bytes 2048 | tf_op jit(solution)/shard_map/slice | solution.py:272
  106.8 14.9 %slice-start.1 = ((s32[384]{0:T(512)}), s32[256]{0:T(256)S(1)}, s32[]{:S(2)}) async-start(s32[384]{0:T(512)} %param.7), calls=%async_computation.1 | async-start | bytes 2048 | tf_op jit(solution)/shard_map/slice | solution.py:272
  106.9 15.9 %collective-permute-start.22 = (f32[512,128]{1,0:T(8,128)S(1)}, f32[512,128]{1,0:T(8,128)S(1)}, u32[]{:S(2)}, u32[]{:S(2)}) collective-permute-start(f32[512,128]{1,0:T(8,128)S(1)} %slice_add_fusion.2), channel_id=1, source_target_pairs={{16,1},{17,0},{18,3},{19,2},{20,5},{21,4},{22,7},{23,6},{8,25},{9,... | collective-permute-start | bytes 786440 | tf_op jit(solution)/shard_map/ppermute | solution.py:151
  108.2 16.1 %collective-permute-start.21 = (f32[512,128]{1,0:T(8,128)S(1)}, f32[512,128]{1,0:T(8,128)S(1)}, u32[]{:S(2)}, u32[]{:S(2)}) collective-permute-start(f32[512,128]{1,0:T(8,128)S(1)} %slice_add_fusion.2), channel_id=1, source_target_pairs={{0,1},{1,0},{2,3},{3,2},{4,5},{5,4},{6,7},{7,6},{24,25},{25,24},{2... | collective-permute-start | bytes 786440 | tf_op jit(solution)/shard_map/ppermute | solution.py:151
